TPU v7x, 32 devices: a whole 2x2x4 slice. The times are simulated.
32 devices in a mesh: dp: 2 (over core), row: 4 (over y, x), col: 4 (over z).
Axes of the slice: x: 2, y: 2, z: 4, core: 2. Of those that a mesh axis runs over, the one named last changes fastest.
Arguments:
- hidden: bfloat16 [2048, 1024], P(('dp', 'row')), may hold values from -6 to 6
- segments: int32 [2, 1024], P('dp'), may hold values from 0 to 3, never falling along the last dimension, each value on 1 to 512 neighbouring positions
- cotangent: bfloat16 [2048, 1024], P(('dp', 'row')), may hold values from -6 to 6
- norm_gain: float32 [2, 1024], replicated, may hold values from 0.5 to 1.5
- zx_weight: bfloat16 [2, 1024, 4096], P(None, 'col', 'row'), may hold values from -0.1875 to 0.1875
- dt_weight: bfloat16 [2, 1024, 32], P(None, 'col', 'row'), may hold values from -0.1875 to 0.1875
- bc_weight: bfloat16 [2, 1024, 256], replicated, may hold values from -0.1875 to 0.1875
- conv_x: float32 [2, 4, 2048], P(None, None, ('row', 'col')), may hold values from -3 to 3
- conv_x_bias: float32 [2, 2048], P(None, ('row', 'col')), may hold values from -3 to 3
- conv_bc: float32 [2, 4, 256], replicated, may hold values from -3 to 3
- conv_bc_bias: float32 [2, 256], replicated, may hold values from -3 to 3
- dt_bias: float32 [2, 32], P(None, ('row', 'col')), may hold values from -6 to -2
- a_log: float32 [2, 32], P(None, ('row', 'col')), may hold values from -2 to 2.5
- skip_d: float32 [2, 32], P(None, ('row', 'col')), may hold values from 0.5 to 1.5
- gnorm_gain: float32 [2, 2048], P(None, ('row', 'col')), may hold values from 0.5 to 1.5
- out_weight: bfloat16 [2, 2048, 1024], P(None, ('row', 'col')), may hold values from -0.125 to 0.125
Outputs:
- hidden_out: bfloat16 [2048, 1024], P(('dp', 'row'))
- d_hidden: float32 [2048, 1024], P(('dp', 'row'))
- d_norm_gain: float32 [2, 1024], replicated
- d_zx_weight: float32 [2, 1024, 4096], P(None, 'col', 'row')
- d_dt_weight: float32 [2, 1024, 32], P(None, 'col', 'row')
- d_bc_weight: float32 [2, 1024, 256], replicated
- d_conv_x: float32 [2, 4, 2048], P(None, None, ('row', 'col'))
- d_conv_x_bias: float32 [2, 2048], P(None, ('row', 'col'))
- d_conv_bc: float32 [2, 4, 256], replicated
- d_conv_bc_bias: float32 [2, 256], replicated
- d_dt_bias: float32 [2, 32], P(None, ('row', 'col'))
- d_a_log: float32 [2, 32], P(None, ('row', 'col'))
- d_skip_d: float32 [2, 32], P(None, ('row', 'col'))
- d_gnorm_gain: float32 [2, 2048], P(None, ('row', 'col'))
- d_out_weight: float32 [2, 2048, 1024], P(None, ('row', 'col'))
Inputs may be any that keep to these rules, and one draw needn't show every extreme that they name: `segments`: within a sequence the document numbers never fall; each document is a run of 1 to 512 tokens, and in every sequence one document has exactly 512 tokens.
All inputs are finite; a program needn't handle non-finite values.
Results may differ from a plain program's by a relative error of at most 0.04.
Values may be sent and summed in bfloat16 or wider, within the bound.
No kernel may reach another device: no remote copies, remote signals or barrier semaphores. Data moves between devices by JAX's collectives and lax.ppermute only.
A program may use at most 128 MiB of HBM per device.

v0:
```python
from functools import partial

import jax
import jax.numpy as jnp
from jax import lax
from jax.sharding import PartitionSpec as P

HEADS = 32
HEAD_DIM = 64
BLOCK = 256


EPS = 1e-05
HIGHEST = lax.Precision.HIGHEST
CONTRACT_ROWS = (((0,), (0,)), ((), ()))
CONTRACT_COLS = (((1,), (1,)), ((), ()))


def shortened(array):

    def short(part):
        return part.astype(jnp.bfloat16) if part.dtype == jnp.float32 else part

    return jax.tree.map(short, array)


def conv_masks(seg_ids, taps):
    seg_masks = [jnp.ones(seg_ids.shape, jnp.float32)]
    for offset in range(1, taps):
        earlier = jnp.concatenate(
            [jnp.full((seg_ids.shape[0], offset), -1, jnp.int32), seg_ids[:, :-offset]], axis=1
        )
        seg_masks.append((earlier == seg_ids).astype(jnp.float32))
    return seg_masks


def causal_conv(values, kernel, conv_bias, seg_masks):
    running = conv_bias + kernel[0] * values
    for offset in range(1, kernel.shape[0]):
        padding = jnp.zeros((values.shape[0], offset, values.shape[2]), jnp.float32)
        shifted = jnp.concatenate([padding, values[:, :-offset]], axis=1)
        running = running + kernel[offset] * shifted * seg_masks[offset][:, :, None]
    return running


def mixer_piece(
    seg_ids,
    block,
    mixed_in,
    step_in,
    side_in,
    conv_x,
    conv_x_bias,
    conv_bc,
    conv_bc_bias,
    dt_bias,
    a_log,
    skip_d,
):
    seq_count, length = seg_ids.shape
    heads = step_in.shape[1]
    head_dim = mixed_in.shape[1] // (2 * heads)
    state = side_in.shape[1] // 2
    blocks = length // block
    seg_masks = conv_masks(seg_ids, conv_x.shape[0])
    halves = mixed_in.reshape(seq_count, length, heads, 2, head_dim)
    gate_in = halves[:, :, :, 0, :]
    values = halves[:, :, :, 1, :].reshape(seq_count, length, heads * head_dim)
    values = jax.nn.silu(causal_conv(values, conv_x, conv_x_bias, seg_masks))
    side = jax.nn.silu(
        causal_conv(side_in.reshape(seq_count, length, 2 * state), conv_bc, conv_bc_bias, seg_masks)
    )
    steps = jax.nn.softplus(step_in.reshape(seq_count, length, heads) + dt_bias)
    layout = (seq_count, blocks, block)
    inputs = side[:, :, :state].reshape(layout + (state,))
    readout = side[:, :, state:].reshape(layout + (state,))
    sources = values.reshape(layout + (heads, head_dim))
    steps_head = steps.reshape(layout + (heads,)).transpose(0, 1, 3, 2)
    decays = jnp.cumsum(steps_head * (-jnp.exp(a_log))[:, None], axis=3)
    seg_layout = seg_ids.reshape(layout)
    places = jnp.arange(block)
    causal = places[:, None] >= places[None, :]
    allowed = (seg_layout[:, :, :, None] == seg_layout[:, :, None, :]) & causal
    spans = decays[:, :, :, :, None] - decays[:, :, :, None, :]
    weights = jnp.exp(jnp.where(allowed[:, :, None], spans, -1e30))
    affinity = jnp.einsum("scqn,sckn->scqk", readout, inputs, precision=HIGHEST)
    scores = affinity[:, :, None] * weights * steps_head[:, :, :, None, :]
    result = jnp.einsum("schqk,sckhp->scqhp", scores, sources, precision=HIGHEST)
    last_seg = seg_layout[:, :, -1]
    same_last = (seg_layout == last_seg[:, :, None]).astype(jnp.float32)
    to_end = jnp.exp(decays[:, :, :, -1:] - decays) * same_last[:, :, None, :] * steps_head
    scaled = sources * to_end.transpose(0, 1, 3, 2)[..., None]
    states = jnp.einsum("sckn,sckhp->schnp", inputs, scaled, precision=HIGHEST)
    carried = states[:, 0]
    outputs = [jnp.zeros((seq_count, block, heads, head_dim), jnp.float32)]
    for index in range(1, blocks):
        keeper = (seg_layout[:, index] == last_seg[:, index - 1][:, None]).astype(jnp.float32)
        factor = jnp.exp(decays[:, index]) * keeper[:, None, :]
        earlier = jnp.einsum("sqn,shnp->sqhp", readout[:, index], carried, precision=HIGHEST)
        outputs.append(earlier * factor.transpose(0, 2, 1)[..., None])
        if index + 1 < blocks:
            linked = (last_seg[:, index] == last_seg[:, index - 1]).astype(jnp.float32)
            carry_decay = jnp.exp(decays[:, index, :, -1]) * linked[:, None]
            carried = states[:, index] + carry_decay[:, :, None, None] * carried
    result = result + jnp.stack(outputs, axis=1) + skip_d[:, None] * sources
    gated = result.reshape(seq_count, length, heads, head_dim) * jax.nn.silu(gate_in)
    return gated.reshape(seq_count * length, heads * head_dim)


def total_heads(terms):
    return jax.tree.map(lambda part: part.astype(jnp.float32), lax.psum(shortened(terms), "dp"))


def total_shared(terms):
    return lax.psum(terms, ("dp", "row", "col"))


def shards(
    hidden,
    segments,
    cotangent,
    norm_gain,
    zx_weight,
    dt_weight,
    bc_weight,
    conv_x,
    conv_x_bias,
    conv_bc,
    conv_bc_bias,
    dt_bias,
    a_log,
    skip_d,
    gnorm_gain,
    out_weight,
):
    col_count = lax.axis_size("col")
    row_count_axis = lax.axis_size("row")
    col_index = lax.axis_index("col")
    width = hidden.shape[1]
    col_width = width // col_count
    layers = zx_weight.shape[0]
    state_width = bc_weight.shape[2]
    inner_total = HEADS * HEAD_DIM
    rows_here = hidden.shape[0]
    resid = hidden.astype(jnp.float32)
    stored = []
    for layer_index in range(layers):
        scale = lax.rsqrt(jnp.mean(resid * resid, axis=1, keepdims=True) + EPS)
        normed = (resid * scale * norm_gain[layer_index]).astype(jnp.bfloat16)
        side = jnp.dot(normed, bc_weight[layer_index], preferred_element_type=jnp.float32).astype(
            jnp.bfloat16
        )
        normed_cols = lax.dynamic_slice_in_dim(normed, col_index * col_width, col_width, 1)
        gathered_cols, side_all = (
            lax.all_gather(normed_cols, "row", axis=0, tiled=True),
            lax.all_gather(side, "row", axis=0, tiled=True),
        )
        part_mixed = jnp.dot(
            gathered_cols, zx_weight[layer_index], preferred_element_type=jnp.float32
        )
        part_steps = jnp.dot(
            gathered_cols, dt_weight[layer_index], preferred_element_type=jnp.float32
        )
        mixed_sum, step_sum = (
            lax.psum_scatter(part_mixed, "col", scatter_dimension=1, tiled=True),
            lax.psum_scatter(part_steps, "col", scatter_dimension=1, tiled=True),
        )
        mixed_in = mixed_sum.astype(jnp.bfloat16)
        step_in = step_sum.astype(jnp.bfloat16)
        piece = partial(mixer_piece, segments, BLOCK)
        gated, pullback = jax.vjp(
            piece,
            mixed_in.astype(jnp.float32),
            step_in.astype(jnp.float32),
            side_all.astype(jnp.float32),
            conv_x[layer_index],
            conv_x_bias[layer_index],
            conv_bc[layer_index],
            conv_bc_bias[layer_index],
            dt_bias[layer_index],
            a_log[layer_index],
            skip_d[layer_index],
        )
        squares = lax.psum(jnp.sum(gated * gated, axis=1), ("row", "col"))
        inverse = lax.rsqrt(squares / inner_total + EPS)[:, None]
        normed_out = (gated * inverse * gnorm_gain[layer_index]).astype(jnp.bfloat16)

        def project(first_row, row_count, source=normed_out, weight=out_weight[layer_index]):
            return jnp.dot(source, weight, preferred_element_type=jnp.float32)

        kept_rows = normed_out.shape[0] // (row_count_axis * col_count)
        shared_rows = lax.psum_scatter(
            project(jnp.int32(0), lax.axis_size(("row", "col")) * kept_rows),
            ("row", "col"),
            scatter_dimension=0,
            tiled=True,
        )
        branch = lax.all_gather(shared_rows, "col", axis=0, tiled=True)
        stored.append((resid, scale, normed, gathered_cols, gated, inverse, normed_out, pullback))
        resid = resid + branch
    result_out = resid.astype(jnp.bfloat16)
    grad = cotangent.astype(jnp.float32)
    heads_terms = [None] * layers
    shared_terms = [None] * layers
    for layer_index in reversed(range(layers)):
        resid_in, scale, normed, gathered_cols, gated, inverse, normed_out, pullback = stored[
            layer_index
        ]
        grad_low = grad.astype(jnp.bfloat16)
        grad_full = lax.all_gather(grad_low, "row", axis=0, tiled=True)
        grad_out_w = lax.dot_general(
            normed_out, grad_full, CONTRACT_ROWS, preferred_element_type=jnp.float32
        )
        grad_normed_out = lax.dot_general(
            grad_full, out_weight[layer_index], CONTRACT_COLS, preferred_element_type=jnp.float32
        )
        grad_gnorm = jnp.sum(grad_normed_out * gated * inverse, axis=0)
        weighted = gnorm_gain[layer_index] * grad_normed_out
        inner_dot = lax.psum(jnp.sum(gated * weighted, axis=1), ("row", "col"))
        grad_gated = inverse * weighted - gated * inverse**3 * (inner_dot / inner_total)[:, None]
        (
            g_mixed,
            g_steps,
            g_side,
            g_conv_x,
            g_conv_x_bias,
            g_conv_bc,
            g_conv_bc_bias,
            g_dt_bias,
            g_a_log,
            g_skip,
        ) = pullback(grad_gated)
        mixed_rows, steps_rows = (
            lax.all_gather(g_mixed.astype(jnp.bfloat16), "col", axis=1, tiled=True),
            lax.all_gather(g_steps.astype(jnp.bfloat16), "col", axis=1, tiled=True),
        )
        grad_zx_w = lax.dot_general(
            gathered_cols, mixed_rows, CONTRACT_ROWS, preferred_element_type=jnp.float32
        )
        grad_dt_w = lax.dot_general(
            gathered_cols, steps_rows, CONTRACT_ROWS, preferred_element_type=jnp.float32
        )

        def back_rows(
            first_row,
            row_count,
            mixed_src=mixed_rows,
            steps_src=steps_rows,
            side_src=g_side,
            w_mixed=zx_weight[layer_index],
            w_steps=dt_weight[layer_index],
        ):
            main_part = lax.dot_general(
                mixed_src, w_mixed, CONTRACT_COLS, preferred_element_type=jnp.float32
            )
            main_part = main_part + lax.dot_general(
                steps_src, w_steps, CONTRACT_COLS, preferred_element_type=jnp.float32
            )
            return jnp.concatenate([main_part, side_src], axis=1)

        summed = lax.psum_scatter(
            back_rows(
                jnp.int32(0), lax.axis_size("row") * (mixed_rows.shape[0] // row_count_axis)
            ).astype(jnp.bfloat16),
            "row",
            scatter_dimension=0,
            tiled=True,
        ).astype(jnp.float32)
        all_cols = lax.all_gather(summed.astype(jnp.bfloat16), "col", axis=1, tiled=True).astype(
            summed.dtype
        )
        all_cols = all_cols.reshape(rows_here, col_count, col_width + state_width)
        grad_normed = all_cols[:, :, :col_width].reshape(rows_here, width)
        grad_side = jnp.sum(all_cols[:, :, col_width:], axis=1).astype(jnp.bfloat16)
        grad_normed = grad_normed + lax.dot_general(
            grad_side, bc_weight[layer_index], CONTRACT_COLS, preferred_element_type=jnp.float32
        )
        normed_local = lax.dynamic_slice_in_dim(normed, col_index * col_width, col_width, 1)
        bc_piece = lax.dot_general(
            normed_local, grad_side, CONTRACT_ROWS, preferred_element_type=jnp.float32
        )
        grad_bc_w = lax.dynamic_update_slice_in_dim(
            jnp.zeros((width, state_width), jnp.float32), bc_piece, col_index * col_width, 0
        )
        gain_terms = lax.dynamic_slice_in_dim(
            grad_normed * resid_in * scale, col_index * col_width, col_width, 1
        )
        grad_gain = lax.dynamic_update_slice_in_dim(
            jnp.zeros((width,), jnp.float32), jnp.sum(gain_terms, axis=0), col_index * col_width, 0
        )
        gain_dot = jnp.sum(resid_in * norm_gain[layer_index] * grad_normed, axis=1, keepdims=True)
        grad = (
            grad
            + scale * norm_gain[layer_index] * grad_normed
            - resid_in * scale**3 * gain_dot / width
        )
        head_tuple = (
            grad_zx_w,
            grad_dt_w,
            g_conv_x,
            g_conv_x_bias,
            g_dt_bias,
            g_a_log,
            g_skip,
            grad_gnorm,
            grad_out_w,
        )
        shared_tuple = (grad_gain, grad_bc_w, g_conv_bc, g_conv_bc_bias)
        heads_terms[layer_index] = head_tuple
        shared_terms[layer_index] = shared_tuple
    heads_stack = tuple(
        (jnp.stack([heads_terms[index][member] for index in range(layers)]) for member in range(9))
    )
    shared_stack = tuple(
        (jnp.stack([shared_terms[index][member] for index in range(layers)]) for member in range(4))
    )
    heads_stack = total_heads(heads_stack)
    shared_stack = total_shared(shared_stack)
    return (
        result_out,
        grad,
        shared_stack[0],
        heads_stack[0],
        heads_stack[1],
        shared_stack[1],
        heads_stack[2],
        heads_stack[3],
        shared_stack[2],
        shared_stack[3],
        heads_stack[4],
        heads_stack[5],
        heads_stack[6],
        heads_stack[7],
        heads_stack[8],
    )


def solution(mesh):
    placed = (
        P(("dp", "row"), None),
        P("dp", None),
        P(("dp", "row"), None),
        P(),
        P(None, "col", "row"),
        P(None, "col", "row"),
        P(),
        P(None, None, ("row", "col")),
        P(None, ("row", "col")),
        P(),
        P(),
        P(None, ("row", "col")),
        P(None, ("row", "col")),
        P(None, ("row", "col")),
        P(None, ("row", "col")),
        P(None, ("row", "col"), None),
    )
    return jax.shard_map(
        shards,
        mesh=mesh,
        in_specs=placed,
        out_specs=(
            P(("dp", "row"), None),
            P(("dp", "row"), None),
            P(),
            P(None, "col", "row"),
            P(None, "col", "row"),
            P(),
            P(None, None, ("row", "col")),
            P(None, ("row", "col")),
            P(),
            P(),
            P(None, ("row", "col")),
            P(None, ("row", "col")),
            P(None, ("row", "col")),
            P(None, ("row", "col")),
            P(None, ("row", "col"), None),
        ),
        check_vma=False,
    )
```

profile of v0, /device:TPU:0, one launch (start us, length us, event | category | flops | bytes accessed | tf_op | source)
XLA Modules:
  0.0 1166.7 jit_solution(9310738073706395560)
XLA Ops:
  12.0 11.5 all_gather.42
  23.6 2.7 fusion.148
  28.4 20.9 %all-reduce.74 = bf16[1024,8]{0,1:T(8,128)(2,1)S(1)} all-reduce(f32[1024,8]{0,1:T(8,128)S(1)} %fusion.316), channel_id=5, replica_groups=mesh['dp'=2,'row'=4,'col'=4] {'col'}, use_global_device_ids=true, to_apply=%region_2.0.clone | all-reduce | flops 8192 | bytes 49152
  61.7 9.9 all_gather.43
  82.4 22.0 %reduce-scatter.7.cloned.1.call-done = f32[1024,256]{1,0:T(8,128)} async-done(((f32[1024,1024]{1,0:T(8,128)}), f32[1024,256]{1,0:T(8,128)}) %reduce-scatter.7.cloned.1.call-update) | async-done | bytes 1048592 | tf_op jit(solution)/shard_map/reduce_scatter | solution.py:165
  120.1 3.7 multiply_reduce_fusion.29
  123.8 41.3 %psum.119 = f32[1024]{0:T(1024)S(1)} all-reduce(f32[1024]{0:T(1024)S(1)} %bitcast.1228), channel_id=1, replica_groups=mesh['dp'=2,'row'=4,'col'=4] {'row','col'}, use_global_device_ids=true, to_apply=%region_6.8 | all-reduce | flops 1024 | bytes 8192 | tf_op jit(solution)/shard_map/psum | solution.py:184
  167.1 2.7 fusion.186
  169.9 93.8 %reduce-scatter.9.cloned.1.call-done = f32[64,1024]{1,0:T(8,128)} async-done(((f32[1024,1024]{1,0:T(8,128)}), f32[64,1024]{1,0:T(8,128)}) %reduce-scatter.9.cloned.1.call-update) | async-done | bytes 262160 | tf_op jit(solution)/shard_map/reduce_scatter | solution.py:192
  263.8 28.2 %all-gather.11.cloned.1.call-done = f32[256,1024]{1,0:T(8,128)} async-done(((f32[64,1024]{1,0:T(8,128)}), f32[256,1024]{1,0:T(8,128)}) %all-gather.11.cloned.1.call-update) | async-done | bytes 1048592 | tf_op jit(solution)/shard_map/all_gather | solution.py:198
  295.0 10.2 all_gather.45
  305.2 3.9 fusion.142
  311.8 19.0 %all-reduce.75 = bf16[1024,8]{0,1:T(8,128)(2,1)S(1)} all-reduce(f32[1024,8]{0,1:T(8,128)S(1)} %fusion.313), channel_id=8, replica_groups=mesh['dp'=2,'row'=4,'col'=4] {'col'}, use_global_device_ids=true, to_apply=%region_10.12.clone | all-reduce | flops 8192 | bytes 49152
  334.9 13.8 %all_gather.46 = bf16[1024,256]{1,0:T(8,128)(2,1)S(1)} all-gather(bf16[256,256]{1,0:T(8,128)(2,1)S(1)} %convolution_convert_fusion.4), channel_id=1, replica_groups=mesh['dp'=2,'row'=4,'col'=4] {'row'}, dimensions={0}, use_global_device_ids=true | all-gather | bytes 655360 | tf_op jit(solution)/shard_map/all_gather | solution.py:156
  352.8 3.1 fusion.386
  355.9 30.0 %reduce-scatter.11.cloned.1.call-done = f32[1024,256]{1,0:T(8,128)} async-done(((f32[1024,1024]{1,0:T(8,128)}), f32[1024,256]{1,0:T(8,128)}) %reduce-scatter.11.cloned.1.call-update) | async-done | bytes 1048592 | tf_op jit(solution)/shard_map/reduce_scatter | solution.py:165
  388.2 2.6 copy.270
  407.7 3.6 multiply_reduce_fusion.28
  413.9 42.0 %psum.120 = f32[1024]{0:T(1024)} all-reduce(f32[1024]{0:T(1024)} %bitcast.1227), channel_id=1, replica_groups=mesh['dp'=2,'row'=4,'col'=4] {'row','col'}, use_global_device_ids=true, to_apply=%region_14.16 | all-reduce | flops 1024 | bytes 8192 | tf_op jit(solution)/shard_map/psum | solution.py:184
  457.2 4.5 multiply_reduce_fusion.14
  461.7 37.6 %psum.121 = f32[1024]{0:T(1024)} all-reduce(f32[1024]{0:T(1024)} %get-tuple-element.34), channel_id=1, replica_groups=mesh['dp'=2,'row'=4,'col'=4] {'row','col'}, use_global_device_ids=true, to_apply=%region_17.19 | all-reduce | flops 1024 | bytes 8192 | tf_op jit(solution)/shard_map/psum | solution.py:219
  500.0 3.2 fusion.124
  506.7 5.9 fusion.31
  528.8 3.7 fusion.36
  555.6 11.3 reduce-window.34
  579.3 14.0 %all-gather = bf16[1,1024,8]{1,0,2:T(2,128)(2,1)} all-gather(bf16[1,1024,2]{1,0,2:T(2,128)(2,1)S(1)} %copy.297), channel_id=2, replica_groups=mesh['dp'=2,'row'=4,'col'=4] {'col'}, dimensions={2}, use_global_device_ids=true | all-gather | bytes 20480 | tf_op jit(solution)/shard_map/all_gather | solution.py:235
  609.2 2.7 fusion.182
  612.0 22.5 %reduce-scatter.15.cloned.1.call-done = bf16[256,512]{1,0:T(8,128)(2,1)} async-done(((bf16[1024,512]{1,0:T(8,128)(2,1)}), bf16[256,512]{1,0:T(8,128)(2,1)}) %reduce-scatter.15.cloned.1.call-update) | async-done | bytes 262160 | tf_op jit(solution)/shard_map/reduce_scatter | solution.py:261
  634.5 115.4 %reduce-scatter.13.cloned.1.call-done = f32[64,1024]{1,0:T(8,128)} async-done(((f32[1024,1024]{1,0:T(8,128)}), f32[64,1024]{1,0:T(8,128)}) %reduce-scatter.13.cloned.1.call-update) | async-done | bytes 262160 | tf_op jit(solution)/shard_map/reduce_scatter | solution.py:192
  750.1 3.7 reshape.2426
  758.3 18.1 %all-gather.13.cloned.1.call-done = f32[256,1024]{1,0:T(8,128)} async-done(((f32[64,1024]{1,0:T(8,128)}), f32[256,1024]{1,0:T(8,128)}) %all-gather.13.cloned.1.call-update) | async-done | bytes 1048592 | tf_op jit(solution)/shard_map/all_gather | solution.py:198
  776.4 3.3 fusion.369
  783.3 31.0 %all-gather.21.cloned.1.call-done = bf16[1024,1024]{1,0:T(8,128)(2,1)} async-done(((bf16[256,1024]{1,0:T(8,128)(2,1)}), bf16[1024,1024]{1,0:T(8,128)(2,1)}) %all-gather.21.cloned.1.call-update) | async-done | bytes 2097168 | tf_op jit(solution)/shard_map/all_gather | solution.py:210
  814.3 4.4 multiply_reduce_fusion.15
  818.7 40.9 %psum.122 = f32[1024]{0:T(1024)S(1)} all-reduce(f32[1024]{0:T(1024)S(1)} %get-tuple-element.32), channel_id=1, replica_groups=mesh['dp'=2,'row'=4,'col'=4] {'row','col'}, use_global_device_ids=true, to_apply=%region_35.37 | all-reduce | flops 1024 | bytes 8192 | tf_op jit(solution)/shard_map/psum | solution.py:219
  859.6 3.2 fusion.125
  866.4 5.5 fusion.33
  880.9 3.7 fusion.45
  907.3 11.3 reduce-window.36
  930.9 14.0 %all-gather.1 = bf16[1,1024,8]{1,0,2:T(2,128)(2,1)} all-gather(bf16[1,1024,2]{1,0,2:T(2,128)(2,1)S(1)} %copy.319), channel_id=3, replica_groups=mesh['dp'=2,'row'=4,'col'=4] {'col'}, dimensions={2}, use_global_device_ids=true | all-gather | bytes 20480 | tf_op jit(solution)/shard_map/all_gather | solution.py:235
  966.7 18.4 %reduce-scatter.17.cloned.1.call-done = bf16[256,512]{1,0:T(8,128)(2,1)} async-done(((bf16[1024,512]{1,0:T(8,128)(2,1)}), bf16[256,512]{1,0:T(8,128)(2,1)}) %reduce-scatter.17.cloned.1.call-update) | async-done | bytes 262160 | tf_op jit(solution)/shard_map/reduce_scatter | solution.py:261
  995.0 3.6 all-reduce.77
  1002.7 10.6 all-gather.25.cloned.1.call-done
  1013.3 3.7 reshape.2428
  1022.6 2.8 convert_element_type.209
  1028.6 40.8 %all-reduce.76 = (f32[2,1024]{1,0:T(2,128)}, f32[2,4,256]{2,1,0:T(4,128)}, f32[2,256]{1,0:T(2,128)}) all-reduce(f32[2,1024]{1,0:T(2,128)S(1)} %pad_maximum_fusion.5, f32[2,4,256]{2,1,0:T(4,128)S(1)} %pad_maximum_fusion.7, f32[2,256]{1,0:T(2,128)S(1)} %pad_maximum_fusion.9), channel_id=1, replica_groups=mesh['dp'=2,'row'=4,'col'=4] {'dp','row','col'}, use_global_device_ids=true, to_apply=%region_54.56 | all-reduce | flops 4608 | bytes 36864 | tf_op jit(solution)/shard_map/psum | solution.py:115
  1070.7 85.4 %all-reduce.82.cloned.1.call-done = f32[2,1024,256]{2,1,0:T(8,128)} async-done(((f32[2,1024,256]{2,1,0:T(8,128)}), f32[2,1024,256]{2,1,0:T(8,128)}) %all-reduce.82.cloned.1.call-update) | async-done | bytes 2097168 | tf_op jit(solution)/shard_map/psum | solution.py:115
  1156.1 3.0 copy.438
  (803 shorter events, 251.5 us)
Async XLA Ops:
  8.0 96.3 %reduce-scatter.7.cloned.1.call-start = ((), (), s32[]{:S(2)}) async-start(), calls=%async_computation.6 | async-start | bytes 5242880 | tf_op jit(solution)/shard_map/reduce_scatter | solution.py:165
  8.9 285.1 %copy-start.111 = (f32[1,1024]{1,0:T(1,128)}, f32[1,1024]{1,0:T(1,128)S(1)}, u32[]{:S(2)}) copy-start(f32[1,1024]{1,0:T(1,128)S(1)} %get-tuple-element.187) | copy-start | bytes 12292
  12.0 49.4 %copy-start.54 = (bf16[256,1024]{1,0:T(8,128)(2,1)}, bf16[256,1024]{1,0:T(8,128)(2,1)S(1)}, u32[]{:S(2)}) copy-start(bf16[256,1024]{1,0:T(8,128)(2,1)S(1)} %fusion.68) | copy-start | bytes 1572868
  26.3 45.6 %copy-start.220 = (f32[2,128]{1,0:T(2,128)S(1)}, f32[2,128]{1,0:T(2,128)}, u32[]{:S(2)}) copy-start(f32[2,128]{1,0:T(2,128)} %param.25) | copy-start | bytes 3076
  26.3 46.1 %copy-start.221 = (f32[2,2]{1,0:T(2,128)S(1)}, f32[2,2]{1,0:T(2,128)}, u32[]{:S(2)}) copy-start(f32[2,2]{1,0:T(2,128)} %param.30) | copy-start | bytes 52
  26.4 46.7 %copy-start.214 = (f32[2,256]{1,0:T(2,128)S(1)}, f32[2,256]{1,0:T(2,128)}, u32[]{:S(2)}) copy-start(f32[2,256]{1,0:T(2,128)} %param.27) | copy-start | bytes 6148
  26.4 47.2 %copy-start.201 = (f32[2,4,128]{2,1,0:T(4,128)S(1)}, f32[2,4,128]{2,1,0:T(4,128)}, u32[]{:S(2)}) copy-start(f32[2,4,128]{2,1,0:T(4,128)} %param.24) | copy-start | bytes 12292
  26.4 49.9 %copy-start.166 = (f32[2,4,256]{2,1,0:T(4,128)S(1)}, f32[2,4,256]{2,1,0:T(4,128)}, u32[]{:S(2)}) copy-start(f32[2,4,256]{2,1,0:T(4,128)} %param.26) | copy-start | bytes 24580
  26.4 237.3 %reduce-scatter.9.cloned.1.call-start = ((), (), s32[]{:S(2)}) async-start(), calls=%async_computation.7 | async-start | bytes 4456448 | tf_op jit(solution)/shard_map/reduce_scatter | solution.py:192
  50.5 69.5 %copy-start.95 = (f32[1,1024,2]{1,2,0:T(2,128)}, f32[1,1024,2]{1,2,0:T(2,128)S(1)}, u32[]{:S(2)}) copy-start(f32[1,1024,2]{1,2,0:T(2,128)S(1)} %compare_select_fusion.5) | copy-start | bytes 24580
  71.8 47.0 %copy-start.159 = (f32[2]{0:T(128)}, f32[2]{0:T(128)S(1)}, u32[]{:S(2)}) copy-start(f32[2]{0:T(128)S(1)} %get-tuple-element.56) | copy-start | bytes 28
  71.8 47.0 %copy-start.184 = (f32[2]{0:T(128)}, f32[2]{0:T(128)S(1)}, u32[]{:S(2)}) copy-start(f32[2]{0:T(128)S(1)} %get-tuple-element.55) | copy-start | bytes 28
  76.2 275.8 %copy-start.99 = (f32[4,256]{1,0:T(4,128)}, f32[4,256]{1,0:T(4,128)S(1)}, u32[]{:S(2)}) copy-start(f32[4,256]{1,0:T(4,128)S(1)} %compare_convert_fusion.6) | copy-start | bytes 12292
  76.3 43.7 %copy-start.122 = (f32[256,2]{0,1:T(2,128)}, f32[256,2]{0,1:T(2,128)S(1)}, u32[]{:S(2)}) copy-start(f32[256,2]{0,1:T(2,128)S(1)} %get-tuple-element.189) | copy-start | bytes 6148
  76.3 43.7 %copy-start.124 = (f32[256,2]{0,1:T(2,128)}, f32[256,2]{0,1:T(2,128)S(1)}, u32[]{:S(2)}) copy-start(f32[256,2]{0,1:T(2,128)S(1)} %get-tuple-element.190) | copy-start | bytes 6148
  76.3 43.7 %copy-start.126 = (f32[256,2]{0,1:T(2,128)}, f32[256,2]{0,1:T(2,128)S(1)}, u32[]{:S(2)}) copy-start(f32[256,2]{0,1:T(2,128)S(1)} %get-tuple-element.191) | copy-start | bytes 6148
  77.0 315.9 %copy-start.83 = (f32[1,1024]{1,0:T(1,128)}, f32[1,1024]{1,0:T(1,128)S(1)}, u32[]{:S(2)}) copy-start(f32[1,1024]{1,0:T(1,128)S(1)} %get-tuple-element.207) | copy-start | bytes 12292
  77.0 315.8 %copy-start.86 = (f32[1,1024]{1,0:T(1,128)}, f32[1,1024]{1,0:T(1,128)S(1)}, u32[]{:S(2)}) copy-start(f32[1,1024]{1,0:T(1,128)S(1)} %get-tuple-element.208) | copy-start | bytes 12292
  77.0 315.8 %copy-start.89 = (f32[1,1024]{1,0:T(1,128)}, f32[1,1024]{1,0:T(1,128)S(1)}, u32[]{:S(2)}) copy-start(f32[1,1024]{1,0:T(1,128)S(1)} %get-tuple-element.209) | copy-start | bytes 12292
  77.1 41.0 %copy-start.105 = (f32[4,256,2]{1,2,0:T(2,128)}, f32[4,256,2]{1,2,0:T(2,128)S(1)}, u32[]{:S(2)}) copy-start(f32[4,256,2]{1,2,0:T(2,128)S(1)} %multiply_bitcast_fusion.7) | copy-start | bytes 24580
  80.4 39.2 %copy-start.13 = (f32[1,1024,128]{2,1,0:T(8,128)}, f32[1,1024,128]{2,1,0:T(8,128)S(1)}, u32[]{:S(2)}) copy-start(f32[1,1024,128]{2,1,0:T(8,128)S(1)} %get-tuple-element.151) | copy-start | bytes 1572868
  120.1 45.6 %copy-start.217 = (f32[2,64]{1,0:T(2,128)S(1)}, f32[2,64]{1,0:T(2,128)}, u32[]{:S(2)}) copy-start(f32[2,64]{1,0:T(2,128)} %mul.2202) | copy-start | bytes 1540
  120.1 47.0 %copy-start.79 = (bf16[2,128,1024]{2,1,0:T(8,128)(2,1)S(1)}, bf16[2,128,1024]{2,1,0:T(8,128)(2,1)}, u32[]{:S(2)}) copy-start(bf16[2,128,1024]{2,1,0:T(8,128)(2,1)} %param.32) | copy-start | bytes 1572868
  169.8 122.1 %copy-start.2 = (bf16[256,1024]{1,0:T(8,128)(2,1)S(1)}, bf16[256,1024]{1,0:T(8,128)(2,1)}, u32[]{:S(2)}) copy-start(bf16[256,1024]{1,0:T(8,128)(2,1)} %param.17) | copy-start | bytes 1572868
  169.9 122.1 %all-gather.11.cloned.1.call-start = ((), (), s32[]{:S(2)}) async-start(), calls=%async_computation.8 | async-start | bytes 1310720 | tf_op jit(solution)/shard_map/all_gather | solution.py:198
  263.7 122.1 %reduce-scatter.11.cloned.1.call-start = ((), (), s32[]{:S(2)}) async-start(), calls=%async_computation.9 | async-start | bytes 5242880 | tf_op jit(solution)/shard_map/reduce_scatter | solution.py:165
  309.2 147.9 %all-gather.15.cloned.1.call-start = ((), (), s32[]{:S(2)}) async-start(), calls=%async_computation.12 | async-start | bytes 2621440 | tf_op jit(solution)/shard_map/all_gather | solution.py:210
  309.8 39.0 %copy-start.149 = (f32[1,1,256]{2,1,0:T(1,128)S(1)}, f32[1,1,256]{2,1,0:T(1,128)}, u32[]{:S(2)}) copy-start(f32[1,1,256]{2,1,0:T(1,128)} %get-tuple-element.185) | copy-start | bytes 3076
  309.9 294.6 %all-gather.17.cloned.1.call-start = ((), (), s32[]{:S(2)}) async-start(), calls=%async_computation.13 | async-start | bytes 2621440 | tf_op jit(solution)/shard_map/all_gather | solution.py:234
  334.3 68.6 %copy-start.161 = (f32[2]{0:T(128)}, f32[2]{0:T(128)S(1)}, u32[]{:S(2)}) copy-start(f32[2]{0:T(128)S(1)} %get-tuple-element.54) | copy-start | bytes 28
  334.3 68.6 %copy-start.186 = (f32[2]{0:T(128)}, f32[2]{0:T(128)S(1)}, u32[]{:S(2)}) copy-start(f32[2]{0:T(128)S(1)} %get-tuple-element.53) | copy-start | bytes 28
  352.2 48.6 %copy-start.107 = (f32[4,256,2]{1,2,0:T(2,128)}, f32[4,256,2]{1,2,0:T(2,128)S(1)}, u32[]{:S(2)}) copy-start(f32[4,256,2]{1,2,0:T(2,128)S(1)} %multiply_bitcast_fusion.6) | copy-start | bytes 24580
  540.8 52.5 %copy-start.78 = (f32[1,1,2,128,64]{3,4,2,1,0:T(8,128)S(1)}, f32[1,1,2,128,64]{3,4,2,1,0:T(8,128)}, u32[]{:S(2)}) copy-start(f32[1,1,2,128,64]{3,4,2,1,0:T(8,128)} %copy-done.77) | copy-start | bytes 196612
  541.6 53.0 %copy-start.76 = (f32[1,1,2,128,64]{3,4,2,1,0:T(8,128)S(1)}, f32[1,1,2,128,64]{3,4,2,1,0:T(8,128)}, u32[]{:S(2)}) copy-start(f32[1,1,2,128,64]{3,4,2,1,0:T(8,128)} %copy-done.75) | copy-start | bytes 196612
  541.6 55.6 %copy-start.8 = (f32[1,1024,128]{2,1,0:T(8,128)S(1)}, f32[1,1024,128]{2,1,0:T(8,128)}, u32[]{:S(2)}) copy-start(f32[1,1024,128]{2,1,0:T(8,128)} %copy-done.6) | copy-start | bytes 1572868
  542.5 92.0 %reduce-scatter.15.cloned.1.call-start = ((), (), s32[]{:S(2)}) async-start(), calls=%async_computation.14 | async-start | bytes 1310720 | tf_op jit(solution)/shard_map/reduce_scatter | solution.py:261
  608.6 141.3 %reduce-scatter.13.cloned.1.call-start = ((), (), s32[]{:S(2)}) async-start(), calls=%async_computation.10 | async-start | bytes 4456448 | tf_op jit(solution)/shard_map/reduce_scatter | solution.py:192
  611.9 138.1 %all-gather.19.cloned.1.call-start = ((), (), s32[]{:S(2)}) async-start(), calls=%async_computation.15 | async-start | bytes 1310720 | tf_op jit(solution)/shard_map/all_gather | solution.py:269
  634.5 141.9 %all-gather.13.cloned.1.call-start = ((), (), s32[]{:S(2)}) async-start(), calls=%async_computation.11 | async-start | bytes 1310720 | tf_op jit(solution)/shard_map/all_gather | solution.py:198
  750.0 64.3 %all-gather.21.cloned.1.call-start = ((), (), s32[]{:S(2)}) async-start(), calls=%async_computation.16 | async-start | bytes 2621440 | tf_op jit(solution)/shard_map/all_gather | solution.py:210
  779.7 176.1 %all-gather.23.cloned.1.call-start = ((), (), s32[]{:S(2)}) async-start(), calls=%async_computation.17 | async-start | bytes 2621440 | tf_op jit(solution)/shard_map/all_gather | solution.py:234
  893.7 51.3 %copy-start.24 = (f32[1,4,256,2,64]{2,4,3,1,0:T(8,128)S(1)}, f32[1,4,256,2,64]{2,4,3,1,0:T(8,128)}, u32[]{:S(2)}) copy-start(f32[1,4,256,2,64]{2,4,3,1,0:T(8,128)} %copy-done.23) | copy-start | bytes 1572868
  894.6 90.6 %reduce-scatter.17.cloned.1.call-start = ((), (), s32[]{:S(2)}) async-start(), calls=%async_computation.18 | async-start | bytes 1310720 | tf_op jit(solution)/shard_map/reduce_scatter | solution.py:261
  959.9 53.4 %all-gather.25.cloned.1.call-start = ((), (), s32[]{:S(2)}) async-start(), calls=%async_computation.19 | async-start | bytes 1310720 | tf_op jit(solution)/shard_map/all_gather | solution.py:269
  985.2 37.4 %all-reduce.84.cloned.1.call-start = ((), (), s32[]{:S(2)}) async-start(), calls=%async_computation.21 | async-start | bytes 3145728 | tf_op jit(solution)/shard_map/psum | solution.py:111
  994.7 161.5 %all-reduce.82.cloned.1.call-start = ((), (), s32[]{:S(2)}) async-start(), calls=%async_computation.20 | async-start | bytes 4194304 | tf_op jit(solution)/shard_map/psum | solution.py:115
  1026.8 42.6 %copy-start.37 = (f32[256,1024]{1,0:T(8,128)S(1)}, f32[256,1024]{1,0:T(8,128)}, u32[]{:S(2)}) copy-start(f32[256,1024]{1,0:T(8,128)} %get-tuple-element.111) | copy-start | bytes 3145732
  1026.8 42.6 %copy-start.192 = (f32[256]{0:T(256)S(1)}, f32[256]{0:T(256)}, u32[]{:S(2)}) copy-start(f32[256]{0:T(256)} %get-tuple-element.214) | copy-start | bytes 3076
  (203 other events, 1555.4 us)
Sparse Core Ops, SparseCore 0:
  26.4 77.8 reduce-scatter.6
  170.0 93.6 reduce-scatter.8
  265.3 26.6 all-gather.10
  309.3 76.5 reduce-scatter.10
  542.6 43.7 all-gather.16
  634.6 45.1 all-gather.18
  750.1 26.2 all-gather.12
  894.7 43.2 all-gather.22
  985.3 27.9 all-gather.24
Sparse Core Ops, SparseCore 1:
  311.5 36.3 all-gather.14
  608.7 25.7 reduce-scatter.14
  636.6 113.3 reduce-scatter.12
  779.8 34.4 all-gather.20
  960.0 25.1 reduce-scatter.16
  994.7 20.1 all-reduce.83
  1022.0 134.1 all-reduce.81
where the time goes:
time: 1180 us; the launch traced here: 1170 us
  waiting for transfers between devices  476 us (40%)
  blocking collectives  320 us (27%)
  other arithmetic  141 us (12%)
  matrix products  104 us (9%)
  local copies, waits for them, and re-layouts  102 us (9%)
  between operations  22.1 us (2%)
    reduce_scatter x2, waiting for transfers between devices, shards(): lax.psum_scatter(project(jnp.int32(0), lax.axis_size(('row', 'col')) * ke...  209 us
    psum x1, waiting for transfers between devices, total_shared(): return lax.psum(terms, ('dp', 'row', 'col'))  85.4 us
    psum x2, blocking collectives, shards(): squares = lax.psum(jnp.sum(gated * gated, axis=1), ('row', 'col'))  83.2 us
    psum x2, blocking collectives, shards(): inner_dot = lax.psum(jnp.sum(gated * weighted, axis=1), ('row', 'col'))  78.6 us
    reduce_scatter x2, waiting for transfers between devices, shards(): lax.psum_scatter(part_mixed, 'col', scatter_dimension=1, tiled=True)  52 us
    all_gather x2, waiting for transfers between devices, shards(): branch = lax.all_gather(shared_rows, 'col', axis=0, tiled=True)  46.2 us
    reduce_scatter x2, waiting for transfers between devices, shards(): lax.psum_scatter(back_rows(jnp.int32(0), lax.axis_size('row') * (mixed_ro...  40.9 us
    psum x1, blocking collectives, total_shared(): return lax.psum(terms, ('dp', 'row', 'col'))  40.8 us
  transfers between devices with their start and end apart: 16, of which 11 were waited for; matrix products, arithmetic and copies ran while one was open for 17% of the time, Pallas kernels for 0%

commit v1 on v0

v1 whole, which is shorter than its diff:
```python
import jax
import jax.numpy as jnp
from jax import lax
from jax.experimental import pallas as pl
from jax.experimental.pallas import tpu as pltpu
from jax.sharding import PartitionSpec as P

EPS = 1e-05
BF = jnp.bfloat16
F32 = jnp.float32
HEAD_DIM = 64
STATE = 128
LANES = 128
NN = (((1,), (0,)), ((), ()))
NT = (((1,), (1,)), ((), ()))
TN = (((0,), (0,)), ((), ()))
VMEM_BYTES = 58 * 1024 * 1024


def dot(left, right, dims=NN):
    return lax.dot_general(left, right, dims, preferred_element_type=F32)


def shape(dims, dtype):
    return jax.ShapeDtypeStruct(dims, dtype)


def local_call(body, outs, scalars, arrays, scratch=(), name=None):
    smem = pl.BlockSpec(memory_space=pltpu.SMEM)
    vmem = pl.BlockSpec(memory_space=pltpu.VMEM)
    return pl.pallas_call(
        body,
        out_shape=tuple(outs),
        in_specs=[smem] * len(scalars) + [vmem] * len(arrays),
        out_specs=tuple(vmem for _ in outs),
        scratch_shapes=list(scratch),
        compiler_params=pltpu.CompilerParams(vmem_limit_bytes=VMEM_BYTES),
        name=name,
    )(*scalars, *arrays)


def row_peer(index, step):
    return index ^ step


def col_dest(index, step):
    return lax.rem(index + step, 4)


def col_source(index, step):
    return lax.rem(index + 4 - step, 4)


def block(index, size):
    return pl.ds(pl.multiple_of(index * size, size), size)


def across_rows(pieces):
    return [pieces[0]] + [
        lax.ppermute(pieces[step], "row", [(i, i ^ step) for i in range(4)]) for step in range(1, 4)
    ]


def across_cols(pieces):
    return [pieces[0]] + [
        lax.ppermute(pieces[step], "col", [(i, (i + step) % 4) for i in range(4)])
        for step in range(1, 4)
    ]


def pair_swap(array):
    count = lax.axis_size("dp")
    return lax.ppermute(array, "dp", [(i, i ^ 1) for i in range(count)])


def copies_sum(array):
    if lax.axis_size("dp") > 2:
        return lax.psum(array, "dp").astype(F32)
    return array.astype(F32) + pair_swap(array).astype(F32)


def split_wide(value, rows):
    high = value.astype(BF).astype(F32)
    lane = lax.broadcasted_iota(jnp.int32, (rows, LANES), 1)
    return jnp.where(lane < 64, high, value - high)


def join_wide(lanes):
    return lanes[:, 0:1] + lanes[:, 64:65]


def start_body(tokens_ref, gain_ref, resid_ref, normed_ref, scale_ref):
    resid = tokens_ref[...].astype(F32)
    width = resid.shape[1]
    scale = lax.rsqrt(jnp.sum(resid * resid, axis=1, keepdims=True) / width + EPS)
    resid_ref[...] = resid
    normed_ref[...] = (resid * scale * gain_ref[...]).astype(BF)
    scale_ref[...] = jnp.broadcast_to(scale, scale_ref.shape)


def collect_branch(own_ref, others, inner):
    total = own_ref[...]
    for other in others:
        total = total + other[...].astype(F32)
    width = total.shape[1] - LANES
    inverse = lax.rsqrt(join_wide(total[:, width:]) / inner + EPS)
    return total[:, :width], inverse


def middle_body(inner, own, one, two, three, resid_ref, gain_ref, next_ref, mixed_ref, inv_ref,
                normed_ref, scale_ref):
    mixed, inverse = collect_branch(own, (one, two, three), inner)
    resid = resid_ref[...] + inverse * mixed
    width = resid.shape[1]
    scale = lax.rsqrt(jnp.sum(resid * resid, axis=1, keepdims=True) / width + EPS)
    next_ref[...] = resid
    mixed_ref[...] = mixed
    inv_ref[...] = jnp.broadcast_to(inverse, inv_ref.shape)
    normed_ref[...] = (resid * scale * gain_ref[...]).astype(BF)
    scale_ref[...] = jnp.broadcast_to(scale, scale_ref.shape)


def send_grad(grad, mixed, inverse, inner, out_ref):
    rows, width = grad.shape
    scaled = (grad * inverse).astype(BF)
    along = jnp.sum(scaled.astype(F32) * mixed, axis=1, keepdims=True)
    factor = inverse * inverse * along / inner
    out_ref[:, :width] = scaled
    out_ref[:, width:] = split_wide(factor, rows).astype(BF)


def turn_body(inner, own, one, two, three, resid_ref, cot_ref, result_ref, sent_ref):
    mixed, inverse = collect_branch(own, (one, two, three), inner)
    result_ref[...] = (resid_ref[...] + inverse * mixed).astype(BF)
    send_grad(cot_ref[...].astype(F32), mixed, inverse, inner, sent_ref)


def norm_back(own, others, grad, resid, scale, gain):
    total = own[...]
    for other in others:
        total = total + other[...].astype(F32)
    weighted = total * gain
    width = resid.shape[1]
    along = jnp.sum(resid * weighted, axis=1, keepdims=True)
    return grad + scale * weighted - resid * (scale * scale * scale * along / width)


def back_middle_body(inner, own, one, two, three, grad_ref, resid_ref, scale_ref, gain_ref,
                     mixed_ref, inv_ref, out_ref, sent_ref):
    grad = norm_back(own, (one, two, three), grad_ref[...].astype(F32), resid_ref[...],
                     scale_ref[:, 0:1], gain_ref[...])
    out_ref[...] = grad
    send_grad(grad, mixed_ref[...], inv_ref[:, 0:1], inner, sent_ref)


def back_end_body(own, one, two, three, grad_ref, resid_ref, scale_ref, gain_ref, out_ref):
    grad = norm_back(own, (one, two, three), grad_ref[...], resid_ref[...], scale_ref[:, 0:1],
                     gain_ref[...])
    out_ref[...] = grad.astype(BF)


def place_body(place_ref, a0, a1, a2, a3, b0, b1, b2, b3, low_ref, wide_ref):
    col = place_ref[1]
    for step, (low, wide) in enumerate(((a0, b0), (a1, b1), (a2, b2), (a3, b3))):
        rows = block(col_source(col, step), low.shape[0])
        low_ref[rows, :] = low[...]
        wide_ref[rows, :] = wide[...].astype(F32)


def project_in_body(place_ref, x0, x1, x2, x3, mine_ref, other_ref, side_ref, normed_ref,
                    m0, m1, m2, m3):
    row, col, half = place_ref[0], place_ref[1], place_ref[2]
    for step, piece in enumerate((x0, x1, x2, x3)):
        normed_ref[block(row_peer(row, step), 64), :] = piece[...]
    mine = jnp.concatenate([normed_ref[:, block(2 * j + half, 128)] for j in range(4)], axis=1)
    other = jnp.concatenate([normed_ref[:, block(2 * j + 1 - half, 128)] for j in range(4)], axis=1)
    side = dot(normed_ref[...], side_ref[...]).astype(BF)
    width = mine_ref.shape[1] - LANES
    steps = dot(mine, mine_ref[:, width:]) + dot(other, other_ref[:, width:])
    steps = steps.astype(BF).astype(F32).T[0:16, :].astype(BF)
    for step, out in enumerate((m0, m1, m2, m3)):
        cols = block(col_dest(col, step), 256)
        value = dot(mine, mine_ref[:, cols]) + dot(other, other_ref[:, cols])
        out[0:256, 0:256] = value.astype(BF)
        out[0:256, 256:512] = side
        out[256:272, 0:256] = steps
        out[256:272, 256:512] = jnp.zeros((16, 256), BF)


def sigmoid(value):
    return 1.0 / (1.0 + jnp.exp(-value))


def lane_scan(value):
    length = value.shape[1]
    lane = lax.broadcasted_iota(jnp.int32, value.shape, 1)
    step = 1
    while step < length:
        value = value + jnp.where(lane >= step, pltpu.roll(value, step, 1), 0.0)
        step *= 2
    return value


def lane_scan_back(value):
    length = value.shape[1]
    lane = lax.broadcasted_iota(jnp.int32, value.shape, 1)
    step = 1
    while step < length:
        value = value + jnp.where(
            lane < length - step, pltpu.roll(value, length - step, 1), 0.0
        )
        step *= 2
    return value


def gather_sequence(col, pieces, zx_s, bc_s, dt_s):
    for step, piece in enumerate(pieces):
        at = col_source(col, step)
        zx_s[block(at, 256), :] = piece[0:256, 0:256]
        bc_s[block(at, 256), :] = piece[0:256, 256:512]
        dt_s[:, block(at, 256)] = piece[256:272, 0:256].astype(F32)


def step_rows(col, dt_s, params):
    raw = dt_s[...]
    at = lax.broadcasted_iota(jnp.int32, raw.shape, 0)
    first = jnp.sum(jnp.where(at == 2 * col, raw, 0.0), axis=0, keepdims=True) + params[0]
    second = jnp.sum(jnp.where(at == 2 * col + 1, raw, 0.0), axis=0, keepdims=True) + params[1]
    at8 = lax.broadcasted_iota(jnp.int32, (8, raw.shape[1]), 0)
    pre = jnp.where(at8 == 0, first, second)
    steps = jnp.maximum(pre, 0.0) + jnp.log1p(jnp.exp(-jnp.abs(pre)))
    rate = jnp.where(at8 == 0, params[2], params[3])
    return pre, steps, rate, lane_scan(steps * rate)


def conv_pre(values, taps, masks_ref):
    total = taps[4:5, :] + taps[0:1, :] * values
    for offset in range(1, 4):
        moved = pltpu.roll(values, offset, 0) * masks_ref[:, offset:offset + 1]
        total = total + taps[offset:offset + 1, :] * moved
    return total


def head_pre(head, zx_s, taps_ref, masks_ref):
    values = zx_s[:, head * 128:head * 128 + 128].astype(F32)
    lane = lax.broadcasted_iota(jnp.int32, values.shape, 1)
    conv = conv_pre(values, taps_ref[head * 8:head * 8 + 8, :], masks_ref)
    return values, jnp.where(lane < 64, values, conv)


def reach(i, j, masks_ref, seg_ref):
    same = masks_ref[i * 256:i * 256 + 256, 0:1] == seg_ref[0:1, j * 256:j * 256 + 256]
    if i == j:
        at = lax.broadcasted_iota(jnp.int32, (256, 256), 0)
        to = lax.broadcasted_iota(jnp.int32, (256, 256), 1)
        same = same & (at >= to)
    return same


def pairs():
    return [(i, j) for i in range(4) for j in range(max(0, i - 2), i + 1)]


def mix_body(place_ref, params, m0, m1, m2, m3, masks_ref, seg_ref, taps_ref, side_taps_ref,
             y_ref, g0, g1, g2, g3, zx_s, bc_s, dt_s, src_s, src_low, b_s, c_s, row_s, col_s, acc_s,
             g_s):
    col = place_ref[1]
    gather_sequence(col, (m0, m1, m2, m3), zx_s, bc_s, dt_s)
    pre, steps, rate, cum = step_rows(col, dt_s, params)
    row_s[0:8, :] = steps
    row_s[8:16, :] = cum
    col_s[...] = jnp.concatenate([cum, jnp.zeros((120, cum.shape[1]), F32)], axis=0).T
    for head in range(2):
        values, active = head_pre(head, zx_s, taps_ref, masks_ref)
        active = active * sigmoid(active)
        src_s[:, head * 128:head * 128 + 128] = active
        src_low[:, head * 128:head * 128 + 128] = active.astype(BF)
    for part, out in enumerate((b_s, c_s)):
        lanes = slice(part * 128, part * 128 + 128)
        conv = conv_pre(bc_s[:, lanes].astype(F32), side_taps_ref[:, lanes], masks_ref)
        out[...] = (conv * sigmoid(conv)).astype(BF)
    acc_s[...] = jnp.zeros_like(acc_s)
    for i, j in pairs():
        ri, rj = slice(i * 256, i * 256 + 256), slice(j * 256, j * 256 + 256)
        affinity = dot(c_s[ri, :], b_s[rj, :], NT)
        allowed = reach(i, j, masks_ref, seg_ref)
        for head in range(2):
            lanes = slice(head * 128, head * 128 + 128)
            span = col_s[ri, head:head + 1] - row_s[8 + head:9 + head, rj]
            weight = jnp.exp(jnp.where(allowed, span, -1e30)) * affinity * row_s[head:head + 1, rj]
            acc_s[ri, lanes] += dot(weight.astype(BF), src_low[rj, lanes])
    lane = lax.broadcasted_iota(jnp.int32, (1024, 128), 1)
    y0 = acc_s[:, 0:128] + params[4] * src_s[:, 0:128]
    y1 = acc_s[:, 128:256] + params[5] * src_s[:, 128:256]
    y = jnp.where(lane < 64, pltpu.roll(y0, 64, 1), y1)
    gate = jnp.where(lane < 64, src_s[:, 0:128], pltpu.roll(src_s[:, 128:256], 64, 1))
    y_ref[...] = y
    g_s[...] = (y * gate).astype(BF)
    for step, out in enumerate((g0, g1, g2, g3)):
        out[...] = g_s[block(col_dest(col, step), 256), :]


def mix_back_body(place_ref, params, d0, d1, d2, d3, m0, m1, m2, m3, y_ref, masks_ref, seg_ref,
                  taps_ref, side_taps_ref, o0, o1, o2, o3, head_ref, side_ref, small_ref,
                  zx_s, bc_s, dt_s, src_s, src_low, slope_s, bc_low, bc_slope, row_s, col_s,
                  dy_s, dy_low, dgy_s, dsrc_s, dbc_s, rows_s, cols_s, dg_s, out_zx, out_bc, out_dt):
    col = place_ref[1]
    gather_sequence(col, (m0, m1, m2, m3), zx_s, bc_s, dt_s)
    for step, piece in enumerate((d0, d1, d2, d3)):
        dg_s[block(col_source(col, step), 256), :] = piece[...].astype(F32)
    pre, steps, rate, cum = step_rows(col, dt_s, params)
    row_s[0:8, :] = steps
    row_s[8:16, :] = cum
    col_s[...] = jnp.concatenate([cum, jnp.zeros((120, cum.shape[1]), F32)], axis=0).T
    lane = lax.broadcasted_iota(jnp.int32, (1024, 128), 1)
    skips = []
    for head in range(2):
        lanes = slice(head * 128, head * 128 + 128)
        values, active = head_pre(head, zx_s, taps_ref, masks_ref)
        sig = sigmoid(active)
        source = active * sig
        slope = sig * (1.0 + active * (1.0 - sig))
        src_low[:, lanes] = source.astype(BF)
        slope_s[:, lanes] = slope
        grad = dg_s[...] if head == 0 else pltpu.roll(dg_s[...], 64, 1)
        y = y_ref[...] if head == 0 else pltpu.roll(y_ref[...], 64, 1)
        dgy_s[:, lanes] = grad * y * slope
        dy = jnp.where(lane < 64, 0.0, pltpu.roll(grad * source, 64, 1))
        dy_low[:, lanes] = dy.astype(BF)
        dsrc_s[:, lanes] = params[4 + head] * dy
        skips.append(jnp.sum(dy * source))
    for part in range(2):
        lanes = slice(part * 128, part * 128 + 128)
        conv = conv_pre(bc_s[:, lanes].astype(F32), side_taps_ref[:, lanes], masks_ref)
        sig = sigmoid(conv)
        bc_low[:, lanes] = (conv * sig).astype(BF)
        bc_slope[:, lanes] = sig * (1.0 + conv * (1.0 - sig))
    dbc_s[...] = jnp.zeros_like(dbc_s)
    rows_s[...] = jnp.zeros_like(rows_s)
    cols_s[...] = jnp.zeros_like(cols_s)
    lane256 = lax.broadcasted_iota(jnp.int32, (256, 128), 1)
    for i, j in pairs():
        ri, rj = slice(i * 256, i * 256 + 256), slice(j * 256, j * 256 + 256)
        affinity = dot(bc_low[ri, 128:256], bc_low[rj, 0:128], NT)
        allowed = reach(i, j, masks_ref, seg_ref)
        shared = None
        for head in range(2):
            lanes = slice(head * 128, head * 128 + 128)
            span = col_s[ri, head:head + 1] - row_s[8 + head:9 + head, rj]
            decay = jnp.exp(jnp.where(allowed, span, -1e30))
            step = row_s[head:head + 1, rj]
            inner = dot(dy_low[ri, lanes], src_low[rj, lanes], NT)
            weight = (decay * affinity * step).astype(BF)
            dsrc_s[rj, lanes] += dot(weight, dy_low[ri, lanes], TN)
            both = decay * inner
            term = both * step
            shared = term if shared is None else shared + term
            product = affinity * both
            cols_s[head:head + 1, rj] += jnp.sum(product, axis=0, keepdims=True)
            total = jnp.sum(affinity * term, axis=1, keepdims=True)
            rows_s[ri, :] += jnp.where(lane256 == head, total, 0.0)
        low = shared.astype(BF)
        dbc_s[ri, 128:256] += dot(low, bc_low[rj, 0:128])
        dbc_s[rj, 0:128] += dot(low, bc_low[ri, 128:256], TN)
    sums = rows_s[...].T[0:8, :]
    col_sum = cols_s[...]
    back = lane_scan_back(sums - col_sum * steps)
    dstep = col_sum + rate * back
    at8 = lax.broadcasted_iota(jnp.int32, steps.shape, 0)
    dlog = rate * jnp.sum(steps * back, axis=1, keepdims=True)
    draw = dstep * sigmoid(pre)
    dbias = jnp.sum(draw, axis=1, keepdims=True)
    lane8 = lax.broadcasted_iota(jnp.int32, (8, 128), 1)
    row8 = lax.broadcasted_iota(jnp.int32, (8, 128), 0)
    dskip = jnp.where(row8 == 0, skips[0], skips[1])
    small_ref[...] = jnp.where(
        lane8 == 0, dbias, jnp.where(lane8 == 1, dlog[:, 0:1], jnp.where(lane8 == 2, dskip, 0.0))
    )
    at16 = lax.broadcasted_iota(jnp.int32, (16, 1024), 0)
    out_dt[...] = jnp.where(
        at16 == 2 * col, draw[0:1, :], jnp.where(at16 == 2 * col + 1, draw[1:2, :], 0.0)
    ).astype(BF)

    def conv_back(values, du, taps, out_ref, rows, lanes):
        dv = taps[0:1, :] * du
        out_ref[rows:rows + 1, lanes] = jnp.sum(du * values, axis=0, keepdims=True)
        for offset in range(1, 4):
            masked = du * masks_ref[:, offset:offset + 1]
            out_ref[rows + offset:rows + offset + 1, lanes] = jnp.sum(
                masked * pltpu.roll(values, offset, 0), axis=0, keepdims=True
            )
            dv = dv + taps[offset:offset + 1, :] * pltpu.roll(masked, 1024 - offset, 0)
        out_ref[rows + 4:rows + 5, lanes] = jnp.sum(du, axis=0, keepdims=True)
        return dv

    head_ref[...] = jnp.zeros_like(head_ref)
    side_ref[...] = jnp.zeros_like(side_ref)
    for head in range(2):
        lanes = slice(head * 128, head * 128 + 128)
        values = zx_s[:, lanes].astype(F32)
        du = jnp.where(lane < 64, 0.0, dsrc_s[:, lanes] * slope_s[:, lanes])
        taps = taps_ref[head * 8:head * 8 + 8, :]
        dv = conv_back(values, du, taps, head_ref, head * 8, slice(0, 128))
        out_zx[:, lanes] = jnp.where(lane < 64, dgy_s[:, lanes], dv).astype(BF)
    for part in range(2):
        lanes = slice(part * 128, part * 128 + 128)
        values = bc_s[:, lanes].astype(F32)
        du = dbc_s[:, lanes] * bc_slope[:, lanes]
        dv = conv_back(values, du, side_taps_ref[:, lanes], side_ref, 0, lanes)
        out_bc[:, lanes] = dv.astype(BF)
    for step, out in enumerate((o0, o1, o2, o3)):
        at = col_dest(col, step)
        out[0:256, 0:256] = out_zx[block(at, 256), :]
        out[0:256, 256:512] = out_bc[block(at, 256), :]
        out[256:272, 0:256] = out_dt[:, block(at, 256)]
        out[256:272, 256:512] = jnp.zeros((16, 256), BF)


def project_out_body(place_ref, g0, g1, g2, g3, mine_ref, other_ref, full_ref, o0, o1, o2, o3,
                     acc_s):
    row, col, half = place_ref[0], place_ref[1], place_ref[2]
    for step, piece in enumerate((g0, g1, g2, g3)):
        full_ref[:, block(col_source(col, step), 128)] = piece[...]
    full = full_ref[...]
    width = 2 * mine_ref.shape[1]
    acc_s[:, block(half, width // 2)] = dot(full, mine_ref[...])
    acc_s[:, block(1 - half, width // 2)] = dot(full, other_ref[...])
    wide = full.astype(F32)
    acc_s[:, width:] = split_wide(jnp.sum(wide * wide, axis=1, keepdims=True), wide.shape[0])
    for step, out in enumerate((o0, o1, o2, o3)):
        out[...] = acc_s[block(row_peer(row, step), 64), :].astype(out.dtype)


def out_back_body(place_ref, q0, q1, q2, q3, mine_ref, other_ref, full_ref, grad_ref, gain_ref,
                  d0, d1, d2, d3, dg_s, fac_s):
    row, col, half = place_ref[0], place_ref[1], place_ref[2]
    width = grad_ref.shape[1]
    for step, piece in enumerate((q0, q1, q2, q3)):
        rows = block(row_peer(row, step), 64)
        grad_ref[rows, :] = piece[:, 0:width]
        fac_s[rows, :] = piece[:, width:].astype(F32)
    value = dot(grad_ref[:, block(half, width // 2)], mine_ref[...], NT)
    value = value + dot(grad_ref[:, block(1 - half, width // 2)], other_ref[...], NT)
    full = full_ref[...].astype(F32)
    gain_ref[...] = (value * full).astype(BF)
    dg_s[...] = (value - full * join_wide(fac_s[...])).astype(BF)
    for step, out in enumerate((d0, d1, d2, d3)):
        out[...] = dg_s[:, block(col_dest(col, step), 128)]


def out_weight_body(full_ref, grad_ref, gain_ref, out_ref):
    width = grad_ref.shape[1]
    out_ref[:, 0:width] = dot(full_ref[...], grad_ref[...], TN).astype(BF)
    ones = jnp.ones((gain_ref.shape[0], LANES), BF)
    out_ref[:, width:] = dot(gain_ref[...], ones, TN).astype(BF)


def in_back_body(place_ref, d0, d1, d2, d3, mine_ref, other_ref, side_ref, normed_ref,
                 full_ref, dside_ref, gain_ref, o0, o1, o2, o3, dx_s):
    row, col, half = place_ref[0], place_ref[1], place_ref[2]
    pieces = (d0, d1, d2, d3)
    side = None
    steps = None
    for step, piece in enumerate(pieces):
        full_ref[:, block(col_source(col, step), 256)] = piece[0:256, 0:256]
        part = piece[0:256, 256:512].astype(F32)
        more = piece[256:272, 0:256].astype(F32)
        side = part if side is None else side + part
        steps = more if steps is None else steps + more
    dside = side.astype(BF)
    dside_ref[...] = dside
    width = full_ref.shape[1] - LANES
    full_ref[:, width:] = jnp.concatenate([steps, jnp.zeros((112, 256), F32)], axis=0).T.astype(BF)
    full = full_ref[...]
    mine = dot(full, mine_ref[...], NT)
    other = dot(full, other_ref[...], NT)
    for j in range(4):
        dx_s[:, block(2 * j + half, 128)] = mine[:, j * 128:j * 128 + 128]
        dx_s[:, block(2 * j + 1 - half, 128)] = other[:, j * 128:j * 128 + 128]
    dx_s[...] += dot(dside, side_ref[...], NT)
    gains = jnp.sum(dx_s[...] * normed_ref[...].astype(F32), axis=0, keepdims=True)
    gain_ref[...] = jnp.broadcast_to(gains, gain_ref.shape)
    for step, out in enumerate((o0, o1, o2, o3)):
        out[...] = dx_s[block(row_peer(row, step), 64), :].astype(out.dtype)


def in_weight_body(normed_ref, full_ref, dside_ref, out_ref, side_ref):
    normed = normed_ref[...]
    out_ref[...] = dot(normed, full_ref[...], TN).astype(BF)
    side_ref[...] = dot(normed, dside_ref[...], TN).astype(BF)


def whole_sum(array, row):
    total = copies_sum(array).astype(BF)
    rows = array.shape[0] // 4
    mine = [
        lax.dynamic_slice_in_dim(total, (row ^ step) * rows, rows, 0) for step in range(4)
    ]
    got = across_rows(mine)
    part = sum(piece.astype(F32) for piece in got).astype(BF)
    got = across_cols([part] * 4)
    part = sum(piece.astype(F32) for piece in got).astype(BF)
    got = across_rows([part] * 4)
    out = jnp.zeros(array.shape, BF)
    for step in range(4):
        out = lax.dynamic_update_slice_in_dim(out, got[step], (row ^ step) * rows, 0)
    return out.astype(F32)


def shards(
    hidden,
    segments,
    cotangent,
    norm_gain,
    zx_weight,
    dt_weight,
    bc_weight,
    conv_x,
    conv_x_bias,
    conv_bc,
    conv_bc_bias,
    dt_bias,
    a_log,
    skip_d,
    gnorm_gain,
    out_weight,
):
    row, col, copy = lax.axis_index("row"), lax.axis_index("col"), lax.axis_index("dp")
    half = copy % 2
    layers, width = norm_gain.shape
    length = segments.shape[1]
    heads_here = dt_weight.shape[2]
    inner = 4 * 4 * conv_x.shape[2]
    place = jnp.stack([row, col, half, row]).astype(jnp.int32)
    swap = [(i * 4 + j, j * 4 + i) for i in range(4) for j in range(4)]

    tokens = lax.ppermute(
        lax.dynamic_slice_in_dim(hidden, col * 64, 64, 0), ("row", "col"), swap
    )
    cot = lax.ppermute(
        lax.dynamic_slice_in_dim(cotangent, col * 64, 64, 0), ("row", "col"), swap
    )

    def fetch(array):
        mine = lax.all_gather(array, "col", axis=0, tiled=True)
        return mine, pair_swap(mine)

    in_weights, out_weights = [], []
    for layer in range(layers):
        joined = jnp.concatenate(
            [zx_weight[layer], jnp.pad(dt_weight[layer], ((0, 0), (0, LANES - heads_here)))], axis=1
        )
        in_weights.append(fetch(lax.dynamic_slice_in_dim(joined, half * 128, 128, 0)))
        scaled = (gnorm_gain[layer][:, None] * out_weight[layer].astype(F32)).astype(BF)
        out_weights.append(
            fetch(lax.dynamic_slice_in_dim(scaled, half * (width // 2), width // 2, 1))
        )

    seg = segments[0].astype(F32)
    columns = [seg]
    for offset in range(1, 4):
        earlier = jnp.concatenate([jnp.full((offset,), -1.0, F32), seg[:-offset]])
        columns.append((earlier == seg).astype(F32))
    masks = jnp.pad(jnp.stack(columns, axis=1), ((0, 0), (0, LANES - 4)))
    seg_rows = jnp.broadcast_to(seg[None], (8, length))
    taps_x = jnp.concatenate([conv_x, conv_x_bias[:, None]], axis=1).reshape(layers, 5, 2, 64)
    taps_x = jnp.pad(taps_x.transpose(0, 2, 1, 3), ((0, 0), (0, 0), (0, 3), (64, 0)))
    taps_x = taps_x.reshape(layers, 16, LANES)
    taps_bc = jnp.pad(
        jnp.concatenate([conv_bc, conv_bc_bias[:, None]], axis=1), ((0, 0), (0, 3), (0, 0))
    )
    params = jnp.concatenate(
        [dt_bias, -jnp.exp(a_log), skip_d, jnp.zeros_like(skip_d)], axis=1
    )
    gains = norm_gain[:, None]

    wide = width + LANES
    kept = []
    resid, normed, scale = local_call(
        start_body,
        [shape((64, width), F32), shape((64, width), BF), shape((64, LANES), F32)],
        [], [tokens, gains[0]], name="start",
    )
    for layer in range(layers):
        pieces = across_rows([normed] * 4)
        full_normed, *sent = local_call(
            project_in_body,
            [shape((256, width), BF)] + [shape((272, 512), BF)] * 4,
            [place], [*pieces, *in_weights[layer], bc_weight[layer]], name="project_in",
        )
        mixed_in = across_cols(sent)
        y, *sent = local_call(
            mix_body,
            [shape((length, 128), F32)] + [shape((256, 128), BF)] * 4,
            [place, params[layer]],
            [*mixed_in, masks, seg_rows, taps_x[layer], taps_bc[layer]],
            [
                pltpu.VMEM((length, 256), BF),
                pltpu.VMEM((length, 256), BF),
                pltpu.VMEM((16, length), F32),
                pltpu.VMEM((length, 256), F32),
                pltpu.VMEM((length, 256), BF),
                pltpu.VMEM((length, 128), BF),
                pltpu.VMEM((length, 128), BF),
                pltpu.VMEM((16, length), F32),
                pltpu.VMEM((length, 128), F32),
                pltpu.VMEM((length, 256), F32),
                pltpu.VMEM((length, 128), BF),
            ],
            name="mix",
        )
        gated = across_cols(sent)
        full_gated, *sent = local_call(
            project_out_body,
            [shape((256, 512), BF), shape((64, wide), F32)] + [shape((64, wide), BF)] * 3,
            [place], [*gated, *out_weights[layer]],
            [pltpu.VMEM((256, wide), F32)], name="project_out",
        )
        parts = across_rows(sent)
        entry = [resid, scale, full_normed, mixed_in, y, full_gated]
        if layer + 1 < layers:
            resid, mixed, inverse, normed, scale = local_call(
                lambda *refs: middle_body(inner, *refs),
                [shape((64, width), F32), shape((64, width), F32), shape((64, LANES), F32),
                 shape((64, width), BF), shape((64, LANES), F32)],
                [], [*parts, resid, gains[layer + 1]], name="middle",
            )
            entry += [mixed, inverse]
        else:
            result, sent_grad = local_call(
                lambda *refs: turn_body(inner, *refs),
                [shape((64, width), BF), shape((64, wide), BF)],
                [], [*parts, resid, cot], name="turn",
            )
        kept.append(entry)

    grad = cot
    head_out, shared_out = [None] * layers, [None] * layers
    for layer in reversed(range(layers)):
        resid, scale, full_normed, mixed_in, y, full_gated = kept[layer][:6]
        pieces = across_rows([sent_grad] * 4)
        full_grad, gain_terms, *sent = local_call(
            out_back_body,
            [shape((256, width), BF), shape((256, 512), BF)] + [shape((256, 128), BF)] * 4,
            [place], [*pieces, *out_weights[layer], full_gated],
            [pltpu.VMEM((256, 512), BF), pltpu.VMEM((256, LANES), F32)], name="out_back",
        )
        dgated = across_cols(sent)
        (out_grad,) = local_call(
            out_weight_body, [shape((512, wide), BF)], [], [full_gated, full_grad, gain_terms],
            name="out_weight",
        )
        o0, o1, o2, o3, head_grads, side_grads, small_grads = local_call(
            mix_back_body,
            [shape((272, 512), BF)] * 4
            + [shape((16, LANES), F32), shape((8, 256), F32), shape((8, LANES), F32)],
            [place, params[layer]],
            [*dgated, *mixed_in, y, masks, seg_rows, taps_x[layer], taps_bc[layer]],
            [
                pltpu.VMEM((length, 256), BF),
                pltpu.VMEM((length, 256), BF),
                pltpu.VMEM((16, length), F32),
                pltpu.VMEM((length, 256), F32),
                pltpu.VMEM((length, 256), BF),
                pltpu.VMEM((length, 256), F32),
                pltpu.VMEM((length, 256), BF),
                pltpu.VMEM((length, 256), F32),
                pltpu.VMEM((16, length), F32),
                pltpu.VMEM((length, 128), F32),
                pltpu.VMEM((8, 128), F32),
                pltpu.VMEM((length, 256), BF),
                pltpu.VMEM((length, 256), F32),
                pltpu.VMEM((length, 256), F32),
                pltpu.VMEM((length, 256), F32),
                pltpu.VMEM((length, 128), F32),
                pltpu.VMEM((8, length), F32),
                pltpu.VMEM((length, 128), F32),
                pltpu.VMEM((length, 256), BF),
                pltpu.VMEM((length, 256), BF),
                pltpu.VMEM((16, length), BF),
            ],
            name="mix_back",
        )
        dmixed = across_cols([o0, o1, o2, o3])
        full_dzx, full_dside, gain_rows, *sent = local_call(
            in_back_body,
            [shape((256, wide), BF), shape((256, 256), BF), shape((8, width), F32),
             shape((64, width), F32)] + [shape((64, width), BF)] * 3,
            [place], [*dmixed, *in_weights[layer], bc_weight[layer], full_normed],
            [pltpu.VMEM((256, width), F32)], name="in_back",
        )
        parts = across_rows(sent)
        if layer > 0:
            mixed, inverse = kept[layer - 1][6:]
            grad, sent_grad = local_call(
                lambda *refs: back_middle_body(inner, *refs),
                [shape((64, width), F32), shape((64, wide), BF)],
                [], [*parts, grad, resid, scale, gains[layer], mixed, inverse],
                name="back_middle",
            )
        else:
            (final,) = local_call(
                back_end_body, [shape((64, width), BF)],
                [], [*parts, grad, resid, scale, gains[layer]], name="back_end",
            )
        in_grad, side_weight = local_call(
            in_weight_body, [shape((width, wide), BF), shape((width, 256), BF)],
            [], [full_normed, full_dzx, full_dside], name="in_weight",
        )
        in_total = lax.psum_scatter(
            copies_sum(in_grad).astype(BF), "col", scatter_dimension=0, tiled=True
        ).astype(F32)
        out_total = lax.psum_scatter(
            copies_sum(out_grad).astype(BF), "col", scatter_dimension=0, tiled=True
        ).astype(F32)
        small = copies_sum(jnp.concatenate([head_grads, small_grads], axis=0))
        gain_part = (gain_rows[0] / norm_gain[layer]).reshape(4, 256)
        shared = jnp.concatenate(
            [side_weight, jnp.pad(
                jnp.concatenate([gain_part, side_grads[:5]], axis=0), ((0, 55), (0, 0))
            ).astype(BF)], axis=0,
        )
        shared = whole_sum(shared, row)
        taps_grad = small[:16].reshape(2, 8, LANES)[:, :5, 64:].transpose(1, 0, 2).reshape(5, 128)
        own_gain = gnorm_gain[layer]
        head_out[layer] = (
            in_total[:, :width],
            in_total[:, width:width + heads_here],
            taps_grad[:4],
            taps_grad[4],
            small[16:18, 0],
            small[16:18, 1],
            small[16:18, 2],
            out_total[:, width] / own_gain,
            out_total[:, :width] * own_gain[:, None],
        )
        shared_out[layer] = (
            shared[width:width + 4].reshape(width),
            shared[:width],
            shared[width + 4:width + 8],
            shared[width + 8],
        )

    def home(array):
        return across_cols([lax.ppermute(array, ("row", "col"), swap)] * 4)

    result_out, grad_out = local_call(
        place_body, [shape((256, width), BF), shape((256, width), F32)],
        [place], [*home(result), *home(final)], name="place",
    )
    heads = [jnp.stack([head_out[i][k] for i in range(layers)]) for k in range(9)]
    shared = [jnp.stack([shared_out[i][k] for i in range(layers)]) for k in range(4)]
    return (
        result_out, grad_out, shared[0], heads[0], heads[1], shared[1], heads[2], heads[3],
        shared[2], shared[3], heads[4], heads[5], heads[6], heads[7], heads[8],
    )


def solution(mesh):
    placed = (
        P(("dp", "row"), None),
        P("dp", None),
        P(("dp", "row"), None),
        P(),
        P(None, "col", "row"),
        P(None, "col", "row"),
        P(),
        P(None, None, ("row", "col")),
        P(None, ("row", "col")),
        P(),
        P(),
        P(None, ("row", "col")),
        P(None, ("row", "col")),
        P(None, ("row", "col")),
        P(None, ("row", "col")),
        P(None, ("row", "col"), None),
    )
    return jax.shard_map(
        shards,
        mesh=mesh,
        in_specs=placed,
        out_specs=(
            P(("dp", "row"), None),
            P(("dp", "row"), None),
            P(),
            P(None, "col", "row"),
            P(None, "col", "row"),
            P(),
            P(None, None, ("row", "col")),
            P(None, ("row", "col")),
            P(),
            P(),
            P(None, ("row", "col")),
            P(None, ("row", "col")),
            P(None, ("row", "col")),
            P(None, ("row", "col")),
            P(None, ("row", "col"), None),
        ),
        check_vma=False,
    )
```

time: 1180 us -> 628 us (0.53)
  the two profiles are of different devices: /device:TPU:0 before, /device:TPU:8 now
where the time goes in v1:
time: 628 us; the launch traced here: 619 us
  waiting for transfers between devices  311 us (50%)
  starting transfers between devices  103 us (16%)
  Pallas kernels  100 us (16%)
  other arithmetic  31.8 us (5%)
  blocking collectives  31.5 us (5%)
  local copies, waits for them, and re-layouts  26.3 us (4%)
  between operations  15.6 us (2%)
    ppermute x36, waiting for transfers between devices, across_cols(): lax.ppermute(pieces[step], 'col', [(i, (i + step) % 4) for i in range(4)])  190 us
    pallas_call x22, Pallas kernels, local_call(): pl.pallas_call(body, out_shape=tuple(outs), in_specs=[smem] * len(scalars...  100 us
    ppermute x36, starting transfers between devices, across_cols(): lax.ppermute(pieces[step], 'col', [(i, (i + step) % 4) for i in range(4)])  46 us
    ppermute x36, starting transfers between devices, across_rows(): lax.ppermute(pieces[step], 'row', [(i, i ^ step) for i in range(4)])  43.6 us
    all_gather x2, waiting for transfers between devices, fetch(): mine = lax.all_gather(array, 'col', axis=0, tiled=True)  41.8 us
    ppermute x36, waiting for transfers between devices, across_rows(): lax.ppermute(pieces[step], 'row', [(i, i ^ step) for i in range(4)])  39.4 us
    all_gather x2, blocking collectives, fetch(): mine = lax.all_gather(array, 'col', axis=0, tiled=True)  31.5 us
    ppermute x2, waiting for transfers between devices, home(): return across_cols([lax.ppermute(array, ('row', 'col'), swap)] * 4)  29.1 us
  transfers between devices with their start and end apart: 94, of which 54 were waited for; matrix products, arithmetic and copies ran while one was open for 6% of the time, Pallas kernels for 14%

profile of v1, /device:TPU:8, one launch (start us, length us, event | category | flops | bytes accessed | tf_op | source)
XLA Modules:
  0.0 619.0 jit_solution(16854052083823157960)
XLA Ops:
  9.6 3.3 collective-permute-start
  15.5 25.8 %all-gather.3.cloned.1.call-done.mine_ref = bf16[512,1152]{1,0:T(8,128)(2,1)} async-done(((bf16[128,1152]{1,0:T(8,128)(2,1)}), bf16[512,1152]{1,0:T(8,128)(2,1)}) %all-gather.3.cloned.1.call-update) | async-done | bytes 1179664 | tf_op jit(solution)/shard_map/all_gather | solution.py:545
  41.4 16.6 %all_gather.13.mine_ref = bf16[512,512]{1,0:T(8,128)(2,1)S(1)} all-gather(bf16[128,512]{1,0:T(8,128)(2,1)S(1)} %fusion.7), channel_id=1, replica_groups=mesh['dp'=2,'row'=4,'col'=4] {'col'}, dimensions={0}, use_global_device_ids=true | all-gather | bytes 655360 | tf_op jit(solution)/shard_map/all_gather | solution.py:545
  59.9 16.0 %all-gather.5.cloned.1.call-done.mine_ref = bf16[512,1152]{1,0:T(8,128)(2,1)} async-done(((bf16[128,1152]{1,0:T(8,128)(2,1)}), bf16[512,1152]{1,0:T(8,128)(2,1)}) %all-gather.5.cloned.1.call-update) | async-done | bytes 1179664 | tf_op jit(solution)/shard_map/all_gather | solution.py:545
  85.5 3.4 collective-permute-done.2.x2
  90.0 3.9 project_in.2
  95.1 3.1 collective-permute-start.6
  99.9 14.5 %collective-permute-done.5.m1 = bf16[272,512]{1,0:T(8,128)(2,1)S(1)} collective-permute-done((bf16[272,512]{1,0:T(8,128)(2,1)}, bf16[272,512]{1,0:T(8,128)(2,1)S(1)}, u32[]{:S(2)}, u32[]{:S(2)}) %collective-permute-start.5) | collective-permute-done | bytes 278560 | tf_op jit(solution)/shard_map/ppermute | solution.py:66
  114.4 3.9 collective-permute-done.6.m2
  121.7 7.1 %mix.2 = (f32[1024,128]{1,0:T(8,128)}, bf16[256,128]{1,0:T(8,128)(2,1)}, bf16[256,128]{1,0:T(8,128)(2,1)}, bf16[256,128]{1,0:T(8,128)(2,1)}, bf16[256,128]{1,0:T(8,128)(2,1)}) custom-call(s32[4]{0:T(128)} %pad_add_fusion.place_ref, f32[8]{0:T(128)} %get-tuple-element.265.params, bf16[272,512]{1,0:T(8,128)(2,1)} %get-tuple-element.104.m0, ...), custom_call_target="tpu_custom_call" | custom-call | tf_op jit(solution)/shard_map/mix/pallas_call | solution.py:31
  143.5 14.9 %all_gather.15.mine_ref = bf16[512,512]{1,0:T(8,128)(2,1)S(1)} all-gather(bf16[128,512]{1,0:T(8,128)(2,1)S(1)} %fusion.6), channel_id=1, replica_groups=mesh['dp'=2,'row'=4,'col'=4] {'col'}, dimensions={0}, use_global_device_ids=true | all-gather | bytes 655360 | tf_op jit(solution)/shard_map/all_gather | solution.py:545
  165.0 3.0 collective-permute-done.15.x1
  168.0 4.1 collective-permute-done.16.x2
  172.8 3.9 project_in.3
  178.7 3.1 collective-permute-start.20
  182.0 16.0 %collective-permute-done.19.m1 = bf16[272,512]{1,0:T(8,128)(2,1)S(1)} collective-permute-done((bf16[272,512]{1,0:T(8,128)(2,1)}, bf16[272,512]{1,0:T(8,128)(2,1)S(1)}, u32[]{:S(2)}, u32[]{:S(2)}) %collective-permute-start.19) | collective-permute-done | bytes 278560 | tf_op jit(solution)/shard_map/ppermute | solution.py:66
  198.0 4.5 collective-permute-done.20.m2
  205.8 7.1 %mix.3 = (f32[1024,128]{1,0:T(8,128)}, bf16[256,128]{1,0:T(8,128)(2,1)}, bf16[256,128]{1,0:T(8,128)(2,1)}, bf16[256,128]{1,0:T(8,128)(2,1)}, bf16[256,128]{1,0:T(8,128)(2,1)}) custom-call(s32[4]{0:T(128)} %pad_add_fusion.place_ref, f32[8]{0:T(128)} %get-tuple-element.266.params, bf16[272,512]{1,0:T(8,128)(2,1)} %get-tuple-element.118.m0, ...), custom_call_target="tpu_custom_call" | custom-call | tf_op jit(solution)/shard_map/mix/pallas_call | solution.py:31
  230.2 6.5 %collective-permute-done.29.refs_5_.refs_4_ = bf16[64,1024]{1,0:T(8,128)(2,1)S(1)} collective-permute-done((bf16[64,1024]{1,0:T(8,128)(2,1)S(1)}, bf16[64,1024]{1,0:T(8,128)(2,1)S(1)}, u32[]{:S(2)}, u32[]{:S(2)}) %collective-permute-start.29) | collective-permute-done | bytes 131104 | tf_op jit(solution)/shard_map/ppermute | solution.py:540
  256.2 4.6 collective-permute-start.38
  267.3 15.9 %mix_back.2 = (bf16[272,512]{1,0:T(8,128)(2,1)}, bf16[272,512]{1,0:T(8,128)(2,1)}, bf16[272,512]{1,0:T(8,128)(2,1)}, bf16[272,512]{1,0:T(8,128)(2,1)}, f32[16,12...) custom-call(s32[4]{0:T(128)} %pad_add_fusion.place_ref, f32[8]{0:T(128)} %get-tuple-element.266.params, ...), custom_call_target="tpu_custom_call" | custom-call | tf_op jit(solution)/shard_map/mix_back/pallas_call | solution.py:31
  283.3 3.0 collective-permute-start.41
  286.5 8.5 %collective-permute-done.40.d1 = bf16[272,512]{1,0:T(8,128)(2,1)S(1)} collective-permute-done((bf16[272,512]{1,0:T(8,128)(2,1)}, bf16[272,512]{1,0:T(8,128)(2,1)S(1)}, u32[]{:S(2)}, u32[]{:S(2)}) %collective-permute-start.40) | collective-permute-done | bytes 278560 | tf_op jit(solution)/shard_map/ppermute | solution.py:66
  295.0 16.8 %collective-permute-done.41.d2 = bf16[272,512]{1,0:T(8,128)(2,1)S(1)} collective-permute-done((bf16[272,512]{1,0:T(8,128)(2,1)}, bf16[272,512]{1,0:T(8,128)(2,1)S(1)}, u32[]{:S(2)}, u32[]{:S(2)}) %collective-permute-start.41) | collective-permute-done | bytes 278560 | tf_op jit(solution)/shard_map/ppermute | solution.py:66
  314.4 4.3 in_back.2
  324.6 3.6 collective-permute-done.44.refs_2_
  334.9 3.3 collective-permute-done.46.q1
  346.8 3.9 in_weight.3
  352.6 3.1 collective-permute-done.83
  355.7 3.7 add_convert_fusion
  362.7 21.5 %collective-permute-done.30.a0 = bf16[64,1024]{1,0:T(8,128)(2,1)} collective-permute-done((bf16[64,1024]{1,0:T(8,128)(2,1)S(1)}, bf16[64,1024]{1,0:T(8,128)(2,1)}, u32[]{:S(2)}, u32[]{:S(2)}) %collective-permute-start.30) | collective-permute-done | bytes 131104 | tf_op jit(solution)/shard_map/ppermute | solution.py:745
  384.3 4.4 collective-permute-start.50
  388.7 5.9 collective-permute-done.49.d1
  397.2 16.0 %mix_back.3 = (bf16[272,512]{1,0:T(8,128)(2,1)}, bf16[272,512]{1,0:T(8,128)(2,1)}, bf16[272,512]{1,0:T(8,128)(2,1)}, bf16[272,512]{1,0:T(8,128)(2,1)}, f32[16,12...) custom-call(s32[4]{0:T(128)} %pad_add_fusion.place_ref, f32[8]{0:T(128)} %get-tuple-element.265.params, ...), custom_call_target="tpu_custom_call" | custom-call | tf_op jit(solution)/shard_map/mix_back/pallas_call | solution.py:31
  421.4 18.9 %collective-permute-done.52.d1 = bf16[272,512]{1,0:T(8,128)(2,1)S(1)} collective-permute-done((bf16[272,512]{1,0:T(8,128)(2,1)}, bf16[272,512]{1,0:T(8,128)(2,1)S(1)}, u32[]{:S(2)}, u32[]{:S(2)}) %collective-permute-start.52) | collective-permute-done | bytes 278560 | tf_op jit(solution)/shard_map/ppermute | solution.py:66
  440.3 24.6 %collective-permute-done.53.d2 = bf16[272,512]{1,0:T(8,128)(2,1)S(1)} collective-permute-done((bf16[272,512]{1,0:T(8,128)(2,1)}, bf16[272,512]{1,0:T(8,128)(2,1)S(1)}, u32[]{:S(2)}, u32[]{:S(2)}) %collective-permute-start.53) | collective-permute-done | bytes 278560 | tf_op jit(solution)/shard_map/ppermute | solution.py:66
  467.4 4.3 in_back.3
  471.7 3.8 in_weight.2
  492.4 4.3 collective-permute-start.58
  497.2 7.6 %collective-permute-done.58.b0 = bf16[64,1024]{1,0:T(8,128)(2,1)} collective-permute-done((bf16[64,1024]{1,0:T(8,128)(2,1)}, bf16[64,1024]{1,0:T(8,128)(2,1)}, u32[]{:S(2)}, u32[]{:S(2)}) %collective-permute-start.58) | collective-permute-done | bytes 131104 | tf_op jit(solution)/shard_map/ppermute | solution.py:745
  507.0 7.4 %collective-permute-done.59.b1 = bf16[64,1024]{1,0:T(8,128)(2,1)S(1)} collective-permute-done((bf16[64,1024]{1,0:T(8,128)(2,1)}, bf16[64,1024]{1,0:T(8,128)(2,1)S(1)}, u32[]{:S(2)}, u32[]{:S(2)}) %collective-permute-start.59) | collective-permute-done | bytes 131104 | tf_op jit(solution)/shard_map/ppermute | solution.py:66
  521.6 5.0 collective-permute-start.63
  536.8 3.0 collective-permute-start.67
  543.7 5.0 collective-permute-done.66
  548.8 13.2 %collective-permute-done.67 = bf16[272,256]{1,0:T(8,128)(2,1)S(1)} collective-permute-done((bf16[272,256]{1,0:T(8,128)(2,1)S(1)}, bf16[272,256]{1,0:T(8,128)(2,1)S(1)}, u32[]{:S(2)}, u32[]{:S(2)}) %collective-permute-start.67) | collective-permute-done | bytes 139296 | tf_op jit(solution)/shard_map/ppermute | solution.py:66
  561.9 8.5 %collective-permute-done.68 = bf16[272,256]{1,0:T(8,128)(2,1)S(1)} collective-permute-done((bf16[272,256]{1,0:T(8,128)(2,1)S(1)}, bf16[272,256]{1,0:T(8,128)(2,1)S(1)}, u32[]{:S(2)}, u32[]{:S(2)}) %collective-permute-start.68) | collective-permute-done | bytes 139296 | tf_op jit(solution)/shard_map/ppermute | solution.py:66
  572.4 7.4 %collective-permute-done.76 = bf16[272,256]{1,0:T(8,128)(2,1)S(1)} collective-permute-done((bf16[272,256]{1,0:T(8,128)(2,1)S(1)}, bf16[272,256]{1,0:T(8,128)(2,1)S(1)}, u32[]{:S(2)}, u32[]{:S(2)}) %collective-permute-start.76) | collective-permute-done | bytes 139296 | tf_op jit(solution)/shard_map/ppermute | solution.py:66
  579.8 9.5 %collective-permute-done.77 = bf16[272,256]{1,0:T(8,128)(2,1)S(1)} collective-permute-done((bf16[272,256]{1,0:T(8,128)(2,1)S(1)}, bf16[272,256]{1,0:T(8,128)(2,1)S(1)}, u32[]{:S(2)}, u32[]{:S(2)}) %collective-permute-start.77) | collective-permute-done | bytes 139296 | tf_op jit(solution)/shard_map/ppermute | solution.py:66
  (473 shorter events, 201.8 us)
Async XLA Ops:
  7.2 34.2 %all-gather.3.cloned.1.call-start = ((), (), s32[]{:S(2)}) async-start(), calls=%async_computation.4 | async-start | bytes 1474560 | tf_op jit(solution)/shard_map/all_gather | solution.py:545
  9.5 66.4 %all-gather.5.cloned.1.call-start = ((), (), s32[]{:S(2)}) async-start(), calls=%async_computation.5 | async-start | bytes 1474560 | tf_op jit(solution)/shard_map/all_gather | solution.py:545
  9.6 67.0 %collective-permute-start = (bf16[64,1024]{1,0:T(8,128)(2,1)S(1)}, bf16[64,1024]{1,0:T(8,128)(2,1)S(1)}, u32[]{:S(2)}, u32[]{:S(2)}) collective-permute-start(bf16[64,1024]{1,0:T(8,128)(2,1)S(1)} %constant_dynamic-slice_fusion.7), channel_id=1, source_target_pairs={{0,0},{1,4},{2,8},{3,12},{4,1},{5,5},{6,9},{7,13},{8,2},{9,6},{10,... | collective-permute-start | bytes 393224 | tf_op jit(solution)/shard_map/ppermute | solution.py:537
  13.8 589.0 %reduce-scatter.11.cloned.1.call-start = ((), (), s32[]{:S(2)}) async-start(), calls=%async_computation.9 | async-start | bytes 1474560 | tf_op jit(solution)/shard_map/reduce_scatter | solution.py:713
  41.4 47.6 %collective-permute-start.4 = (bf16[512,1152]{1,0:T(8,128)(2,1)}, bf16[512,1152]{1,0:T(8,128)(2,1)S(1)}, u32[]{:S(2)}, u32[]{:S(2)}) collective-permute-start(bf16[512,1152]{1,0:T(8,128)(2,1)} %all-gather.3.cloned.1.call-done.mine_ref), channel_id=1, source_target_pairs={{0,16},{16,0},{1,17},{17,1},{2,18},{18,2},{3,19},{19,3},{4,20},{20... | collective-permute-start | bytes 3538952 | tf_op jit(solution)/shard_map/ppermute | solution.py:73
  75.9 89.1 %collective-permute-start.18 = (bf16[512,1152]{1,0:T(8,128)(2,1)}, bf16[512,1152]{1,0:T(8,128)(2,1)S(1)}, u32[]{:S(2)}, u32[]{:S(2)}) collective-permute-start(bf16[512,1152]{1,0:T(8,128)(2,1)} %all-gather.5.cloned.1.call-done.mine_ref), channel_id=1, source_target_pairs={{0,16},{16,0},{1,17},{17,1},{2,18},{18,2},{3,19},{19,3},{4,20},{20... | collective-permute-start | bytes 3538952 | tf_op jit(solution)/shard_map/ppermute | solution.py:73
  85.5 47.9 %collective-permute-start.11 = (bf16[512,512]{1,0:T(8,128)(2,1)S(1)}, bf16[512,512]{1,0:T(8,128)(2,1)S(1)}, u32[]{:S(2)}, u32[]{:S(2)}) collective-permute-start(bf16[512,512]{1,0:T(8,128)(2,1)S(1)} %all_gather.13.mine_ref), channel_id=1, source_target_pairs={{0,16},{16,0},{1,17},{17,1},{2,18},{18,2},{3,19},{19,3},{4,20},{20... | collective-permute-start | bytes 1572872 | tf_op jit(solution)/shard_map/ppermute | solution.py:73
  93.9 20.5 %collective-permute-start.5 = (bf16[272,512]{1,0:T(8,128)(2,1)}, bf16[272,512]{1,0:T(8,128)(2,1)S(1)}, u32[]{:S(2)}, u32[]{:S(2)}) collective-permute-start(bf16[272,512]{1,0:T(8,128)(2,1)} %get-tuple-element.105), channel_id=1, source_target_pairs={{0,1},{1,2},{2,3},{3,0},{4,5},{5,6},{6,7},{7,4},{8,9},{9,10},{10,1... | collective-permute-start | bytes 835592 | tf_op jit(solution)/shard_map/ppermute | solution.py:66
  95.1 23.2 %collective-permute-start.6 = (bf16[272,512]{1,0:T(8,128)(2,1)}, bf16[272,512]{1,0:T(8,128)(2,1)S(1)}, u32[]{:S(2)}, u32[]{:S(2)}) collective-permute-start(bf16[272,512]{1,0:T(8,128)(2,1)} %get-tuple-element.106), channel_id=1, source_target_pairs={{0,2},{1,3},{2,0},{3,1},{4,6},{5,7},{6,4},{7,5},{8,10},{9,11},{10,... | collective-permute-start | bytes 835592 | tf_op jit(solution)/shard_map/ppermute | solution.py:66
  98.2 22.8 %collective-permute-start.7 = (bf16[272,512]{1,0:T(8,128)(2,1)}, bf16[272,512]{1,0:T(8,128)(2,1)}, u32[]{:S(2)}, u32[]{:S(2)}) collective-permute-start(bf16[272,512]{1,0:T(8,128)(2,1)} %get-tuple-element.107), channel_id=1, source_target_pairs={{0,3},{1,0},{2,1},{3,2},{4,7},{5,4},{6,5},{7,6},{8,11},{9,8},{10,9... | collective-permute-start | bytes 835592 | tf_op jit(solution)/shard_map/ppermute | solution.py:66
  139.9 18.5 %collective-permute-start.12 = (bf16[64,1152]{1,0:T(8,128)(2,1)}, bf16[64,1152]{1,0:T(8,128)(2,1)S(1)}, u32[]{:S(2)}, u32[]{:S(2)}) collective-permute-start(bf16[64,1152]{1,0:T(8,128)(2,1)} %get-tuple-element.113), channel_id=1, source_target_pairs={{0,4},{4,0},{8,12},{12,8},{1,5},{5,1},{9,13},{13,9},{2,6},{6,2},{1... | collective-permute-start | bytes 442376 | tf_op jit(solution)/shard_map/ppermute | solution.py:60
  142.0 16.4 %collective-permute-start.13 = (bf16[64,1152]{1,0:T(8,128)(2,1)}, bf16[64,1152]{1,0:T(8,128)(2,1)S(1)}, u32[]{:S(2)}, u32[]{:S(2)}) collective-permute-start(bf16[64,1152]{1,0:T(8,128)(2,1)} %get-tuple-element.114), channel_id=1, source_target_pairs={{0,8},{4,12},{8,0},{12,4},{1,9},{5,13},{9,1},{13,5},{2,10},{6,14},... | collective-permute-start | bytes 442376 | tf_op jit(solution)/shard_map/ppermute | solution.py:60
  142.6 15.8 %collective-permute-start.14 = (bf16[64,1152]{1,0:T(8,128)(2,1)}, bf16[64,1152]{1,0:T(8,128)(2,1)S(1)}, u32[]{:S(2)}, u32[]{:S(2)}) collective-permute-start(bf16[64,1152]{1,0:T(8,128)(2,1)} %get-tuple-element.115), channel_id=1, source_target_pairs={{0,12},{4,8},{8,4},{12,0},{1,13},{5,9},{9,5},{13,1},{2,14},{6,10},... | collective-permute-start | bytes 442376 | tf_op jit(solution)/shard_map/ppermute | solution.py:60
  158.4 57.3 %collective-permute-start.25 = (bf16[512,512]{1,0:T(8,128)(2,1)S(1)}, bf16[512,512]{1,0:T(8,128)(2,1)S(1)}, u32[]{:S(2)}, u32[]{:S(2)}) collective-permute-start(bf16[512,512]{1,0:T(8,128)(2,1)S(1)} %all_gather.15.mine_ref), channel_id=1, source_target_pairs={{0,16},{16,0},{1,17},{17,1},{2,18},{18,2},{3,19},{19,3},{4,20},{20... | collective-permute-start | bytes 1572872 | tf_op jit(solution)/shard_map/ppermute | solution.py:73
  176.7 21.3 %collective-permute-start.19 = (bf16[272,512]{1,0:T(8,128)(2,1)}, bf16[272,512]{1,0:T(8,128)(2,1)S(1)}, u32[]{:S(2)}, u32[]{:S(2)}) collective-permute-start(bf16[272,512]{1,0:T(8,128)(2,1)} %get-tuple-element.119), channel_id=1, source_target_pairs={{0,1},{1,2},{2,3},{3,0},{4,5},{5,6},{6,7},{7,4},{8,9},{9,10},{10,1... | collective-permute-start | bytes 835592 | tf_op jit(solution)/shard_map/ppermute | solution.py:66
  178.7 23.8 %collective-permute-start.20 = (bf16[272,512]{1,0:T(8,128)(2,1)}, bf16[272,512]{1,0:T(8,128)(2,1)S(1)}, u32[]{:S(2)}, u32[]{:S(2)}) collective-permute-start(bf16[272,512]{1,0:T(8,128)(2,1)} %get-tuple-element.120), channel_id=1, source_target_pairs={{0,2},{1,3},{2,0},{3,1},{4,6},{5,7},{6,4},{7,5},{8,10},{9,11},{10,... | collective-permute-start | bytes 835592 | tf_op jit(solution)/shard_map/ppermute | solution.py:66
  181.8 23.3 %collective-permute-start.21 = (bf16[272,512]{1,0:T(8,128)(2,1)}, bf16[272,512]{1,0:T(8,128)(2,1)S(1)}, u32[]{:S(2)}, u32[]{:S(2)}) collective-permute-start(bf16[272,512]{1,0:T(8,128)(2,1)} %get-tuple-element.121), channel_id=1, source_target_pairs={{0,3},{1,0},{2,1},{3,2},{4,7},{5,4},{6,5},{7,6},{8,11},{9,8},{10,9... | collective-permute-start | bytes 835592 | tf_op jit(solution)/shard_map/ppermute | solution.py:66
  223.7 13.1 %collective-permute-start.26 = (bf16[64,1152]{1,0:T(8,128)(2,1)}, bf16[64,1152]{1,0:T(8,128)(2,1)S(1)}, u32[]{:S(2)}, u32[]{:S(2)}) collective-permute-start(bf16[64,1152]{1,0:T(8,128)(2,1)} %get-tuple-element.127), channel_id=1, source_target_pairs={{0,4},{4,0},{8,12},{12,8},{1,5},{5,1},{9,13},{13,9},{2,6},{6,2},{1... | collective-permute-start | bytes 442376 | tf_op jit(solution)/shard_map/ppermute | solution.py:60
  223.7 13.1 %collective-permute-start.27 = (bf16[64,1152]{1,0:T(8,128)(2,1)}, bf16[64,1152]{1,0:T(8,128)(2,1)S(1)}, u32[]{:S(2)}, u32[]{:S(2)}) collective-permute-start(bf16[64,1152]{1,0:T(8,128)(2,1)} %get-tuple-element.128), channel_id=1, source_target_pairs={{0,8},{4,12},{8,0},{12,4},{1,9},{5,13},{9,1},{13,5},{2,10},{6,14},... | collective-permute-start | bytes 442376 | tf_op jit(solution)/shard_map/ppermute | solution.py:60
  263.5 340.6 %reduce-scatter.9.cloned.1.call-start = ((), (), s32[]{:S(2)}) async-start(), calls=%async_computation.8 | async-start | bytes 1474560 | tf_op jit(solution)/shard_map/reduce_scatter | solution.py:713
  283.3 11.8 %collective-permute-start.40 = (bf16[272,512]{1,0:T(8,128)(2,1)}, bf16[272,512]{1,0:T(8,128)(2,1)S(1)}, u32[]{:S(2)}, u32[]{:S(2)}) collective-permute-start(bf16[272,512]{1,0:T(8,128)(2,1)} %get-tuple-element.140), channel_id=1, source_target_pairs={{0,1},{1,2},{2,3},{3,0},{4,5},{5,6},{6,7},{7,4},{8,9},{9,10},{10,1... | collective-permute-start | bytes 835592 | tf_op jit(solution)/shard_map/ppermute | solution.py:66
  283.3 28.5 %collective-permute-start.41 = (bf16[272,512]{1,0:T(8,128)(2,1)}, bf16[272,512]{1,0:T(8,128)(2,1)S(1)}, u32[]{:S(2)}, u32[]{:S(2)}) collective-permute-start(bf16[272,512]{1,0:T(8,128)(2,1)} %get-tuple-element.141), channel_id=1, source_target_pairs={{0,2},{1,3},{2,0},{3,1},{4,6},{5,7},{6,4},{7,5},{8,10},{9,11},{10,... | collective-permute-start | bytes 835592 | tf_op jit(solution)/shard_map/ppermute | solution.py:66
  286.3 27.3 %collective-permute-start.42 = (bf16[272,512]{1,0:T(8,128)(2,1)}, bf16[272,512]{1,0:T(8,128)(2,1)S(1)}, u32[]{:S(2)}, u32[]{:S(2)}) collective-permute-start(bf16[272,512]{1,0:T(8,128)(2,1)} %get-tuple-element.142), channel_id=1, source_target_pairs={{0,3},{1,0},{2,1},{3,2},{4,7},{5,4},{6,5},{7,6},{8,11},{9,8},{10,9... | collective-permute-start | bytes 835592 | tf_op jit(solution)/shard_map/ppermute | solution.py:66
  352.5 254.5 %reduce-scatter.7.cloned.1.call-start = ((), (), s32[]{:S(2)}) async-start(), calls=%async_computation.7 | async-start | bytes 2949120 | tf_op jit(solution)/shard_map/reduce_scatter | solution.py:710
  359.4 248.9 %reduce-scatter.5.cloned.1.call-start = ((), (), s32[]{:S(2)}) async-start(), calls=%async_computation.6 | async-start | bytes 2949120 | tf_op jit(solution)/shard_map/reduce_scatter | solution.py:710
  360.3 23.9 %collective-permute-start.30 = (bf16[64,1024]{1,0:T(8,128)(2,1)S(1)}, bf16[64,1024]{1,0:T(8,128)(2,1)}, u32[]{:S(2)}, u32[]{:S(2)}) collective-permute-start(bf16[64,1024]{1,0:T(8,128)(2,1)S(1)} %copy-done.83), channel_id=1, source_target_pairs={{0,0},{1,4},{2,8},{3,12},{4,1},{5,5},{6,9},{7,13},{8,2},{9,6},{10,... | collective-permute-start | bytes 393224 | tf_op jit(solution)/shard_map/ppermute | solution.py:745
  362.2 22.0 %collective-permute-start.85 = (f32[24,128]{1,0:T(8,128)S(1)}, f32[24,128]{1,0:T(8,128)S(1)}, u32[]{:S(2)}, u32[]{:S(2)}) collective-permute-start(f32[24,128]{1,0:T(8,128)S(1)} %constant_dynamic-update-slice_fusion.2), channel_id=1, source_target_pairs={{0,16},{16,0},{1,17},{17,1},{2,18},{18,2},{3,19},{19,3},{4,20},{20... | collective-permute-start | bytes 36872 | tf_op jit(solution)/shard_map/ppermute | solution.py:73
  384.2 108.2 %collective-permute-start.31 = (bf16[64,1024]{1,0:T(8,128)(2,1)}, bf16[64,1024]{1,0:T(8,128)(2,1)}, u32[]{:S(2)}, u32[]{:S(2)}) collective-permute-start(bf16[64,1024]{1,0:T(8,128)(2,1)} %collective-permute-done.30.a0), channel_id=1, source_target_pairs={{0,1},{1,2},{2,3},{3,0},{4,5},{5,6},{6,7},{7,4},{8,9},{9,10},{10,1... | collective-permute-start | bytes 393224 | tf_op jit(solution)/shard_map/ppermute | solution.py:66
  384.3 12.2 %collective-permute-start.50 = (bf16[256,128]{1,0:T(8,128)(2,1)S(1)}, bf16[256,128]{1,0:T(8,128)(2,1)S(1)}, u32[]{:S(2)}, u32[]{:S(2)}) collective-permute-start(bf16[256,128]{1,0:T(8,128)(2,1)S(1)} %copy-done.85), channel_id=1, source_target_pairs={{0,2},{1,3},{2,0},{3,1},{4,6},{5,7},{6,4},{7,5},{8,10},{9,11},{10,... | collective-permute-start | bytes 196616 | tf_op jit(solution)/shard_map/ppermute | solution.py:66
  415.0 25.3 %collective-permute-start.52 = (bf16[272,512]{1,0:T(8,128)(2,1)}, bf16[272,512]{1,0:T(8,128)(2,1)S(1)}, u32[]{:S(2)}, u32[]{:S(2)}) collective-permute-start(bf16[272,512]{1,0:T(8,128)(2,1)} %get-tuple-element.159), channel_id=1, source_target_pairs={{0,1},{1,2},{2,3},{3,0},{4,5},{5,6},{6,7},{7,4},{8,9},{9,10},{10,1... | collective-permute-start | bytes 835592 | tf_op jit(solution)/shard_map/ppermute | solution.py:66
  415.8 49.1 %collective-permute-start.53 = (bf16[272,512]{1,0:T(8,128)(2,1)}, bf16[272,512]{1,0:T(8,128)(2,1)S(1)}, u32[]{:S(2)}, u32[]{:S(2)}) collective-permute-start(bf16[272,512]{1,0:T(8,128)(2,1)} %get-tuple-element.160), channel_id=1, source_target_pairs={{0,2},{1,3},{2,0},{3,1},{4,6},{5,7},{6,4},{7,5},{8,10},{9,11},{10,... | collective-permute-start | bytes 835592 | tf_op jit(solution)/shard_map/ppermute | solution.py:66
  418.4 48.3 %collective-permute-start.54 = (bf16[272,512]{1,0:T(8,128)(2,1)}, bf16[272,512]{1,0:T(8,128)(2,1)S(1)}, u32[]{:S(2)}, u32[]{:S(2)}) collective-permute-start(bf16[272,512]{1,0:T(8,128)(2,1)} %get-tuple-element.161), channel_id=1, source_target_pairs={{0,3},{1,0},{2,1},{3,2},{4,7},{5,4},{6,5},{7,6},{8,11},{9,8},{10,9... | collective-permute-start | bytes 835592 | tf_op jit(solution)/shard_map/ppermute | solution.py:66
  475.5 52.7 %collective-permute-start.82 = (bf16[1024,1152]{1,0:T(8,128)(2,1)}, bf16[1024,1152]{1,0:T(8,128)(2,1)S(1)}, u32[]{:S(2)}, u32[]{:S(2)}) collective-permute-start(bf16[1024,1152]{1,0:T(8,128)(2,1)} %get-tuple-element.181), channel_id=1, source_target_pairs={{0,16},{16,0},{1,17},{17,1},{2,18},{18,2},{3,19},{19,3},{4,20},{20... | collective-permute-start | bytes 7077896 | tf_op jit(solution)/shard_map/ppermute | solution.py:73
  484.4 35.2 %collective-permute-start.62 = (bf16[1088,256]{1,0:T(8,128)(2,1)}, bf16[1088,256]{1,0:T(8,128)(2,1)}, u32[]{:S(2)}, u32[]{:S(2)}) collective-permute-start(bf16[1088,256]{1,0:T(8,128)(2,1)} %pad_maximum_fusion.3), channel_id=1, source_target_pairs={{0,16},{16,0},{1,17},{17,1},{2,18},{18,2},{3,19},{19,3},{4,20},{20... | collective-permute-start | bytes 1671176 | tf_op jit(solution)/shard_map/ppermute | solution.py:73
  488.0 16.9 %collective-permute-start.32 = (bf16[64,1024]{1,0:T(8,128)(2,1)}, bf16[64,1024]{1,0:T(8,128)(2,1)}, u32[]{:S(2)}, u32[]{:S(2)}) collective-permute-start(bf16[64,1024]{1,0:T(8,128)(2,1)} %collective-permute-done.30.a0), channel_id=1, source_target_pairs={{0,2},{1,3},{2,0},{3,1},{4,6},{5,7},{6,4},{7,5},{8,10},{9,11},{10,... | collective-permute-start | bytes 393224 | tf_op jit(solution)/shard_map/ppermute | solution.py:66
  489.5 15.4 %collective-permute-start.33 = (bf16[64,1024]{1,0:T(8,128)(2,1)}, bf16[64,1024]{1,0:T(8,128)(2,1)}, u32[]{:S(2)}, u32[]{:S(2)}) collective-permute-start(bf16[64,1024]{1,0:T(8,128)(2,1)} %collective-permute-done.30.a0), channel_id=1, source_target_pairs={{0,3},{1,0},{2,1},{3,2},{4,7},{5,4},{6,5},{7,6},{8,11},{9,8},{10,9... | collective-permute-start | bytes 393224 | tf_op jit(solution)/shard_map/ppermute | solution.py:66
  492.4 12.5 %collective-permute-start.58 = (bf16[64,1024]{1,0:T(8,128)(2,1)}, bf16[64,1024]{1,0:T(8,128)(2,1)}, u32[]{:S(2)}, u32[]{:S(2)}) collective-permute-start(bf16[64,1024]{1,0:T(8,128)(2,1)} %back_end.1), channel_id=1, source_target_pairs={{0,0},{1,4},{2,8},{3,12},{4,1},{5,5},{6,9},{7,13},{8,2},{9,6},{10,... | collective-permute-start | bytes 393224 | tf_op jit(solution)/shard_map/ppermute | solution.py:745
  504.9 11.5 %collective-permute-start.61 = (bf16[64,1024]{1,0:T(8,128)(2,1)}, bf16[64,1024]{1,0:T(8,128)(2,1)S(1)}, u32[]{:S(2)}, u32[]{:S(2)}) collective-permute-start(bf16[64,1024]{1,0:T(8,128)(2,1)} %collective-permute-done.58.b0), channel_id=1, source_target_pairs={{0,3},{1,0},{2,1},{3,2},{4,7},{5,4},{6,5},{7,6},{8,11},{9,8},{10,9... | collective-permute-start | bytes 393224 | tf_op jit(solution)/shard_map/ppermute | solution.py:66
  514.4 13.6 %collective-permute-start.72 = (bf16[1088,256]{1,0:T(8,128)(2,1)S(1)}, bf16[1088,256]{1,0:T(8,128)(2,1)S(1)}, u32[]{:S(2)}, u32[]{:S(2)}) collective-permute-start(bf16[1088,256]{1,0:T(8,128)(2,1)S(1)} %pad_maximum_fusion.4), channel_id=1, source_target_pairs={{0,16},{16,0},{1,17},{17,1},{2,18},{18,2},{3,19},{19,3},{4,20},{20... | collective-permute-start | bytes 1671176 | tf_op jit(solution)/shard_map/ppermute | solution.py:73
  536.7 12.0 %collective-permute-start.66 = (bf16[272,256]{1,0:T(8,128)(2,1)S(1)}, bf16[272,256]{1,0:T(8,128)(2,1)S(1)}, u32[]{:S(2)}, u32[]{:S(2)}) collective-permute-start(bf16[272,256]{1,0:T(8,128)(2,1)S(1)} %add_convert_fusion.9), channel_id=1, source_target_pairs={{0,1},{1,2},{2,3},{3,0},{4,5},{5,6},{6,7},{7,4},{8,9},{9,10},{10,1... | collective-permute-start | bytes 417800 | tf_op jit(solution)/shard_map/ppermute | solution.py:66
  536.8 25.2 %collective-permute-start.67 = (bf16[272,256]{1,0:T(8,128)(2,1)S(1)}, bf16[272,256]{1,0:T(8,128)(2,1)S(1)}, u32[]{:S(2)}, u32[]{:S(2)}) collective-permute-start(bf16[272,256]{1,0:T(8,128)(2,1)S(1)} %add_convert_fusion.9), channel_id=1, source_target_pairs={{0,2},{1,3},{2,0},{3,1},{4,6},{5,7},{6,4},{7,5},{8,10},{9,11},{10,... | collective-permute-start | bytes 417800 | tf_op jit(solution)/shard_map/ppermute | solution.py:66
  539.7 30.7 %collective-permute-start.68 = (bf16[272,256]{1,0:T(8,128)(2,1)S(1)}, bf16[272,256]{1,0:T(8,128)(2,1)S(1)}, u32[]{:S(2)}, u32[]{:S(2)}) collective-permute-start(bf16[272,256]{1,0:T(8,128)(2,1)S(1)} %add_convert_fusion.9), channel_id=1, source_target_pairs={{0,3},{1,0},{2,1},{3,2},{4,7},{5,4},{6,5},{7,6},{8,11},{9,8},{10,9... | collective-permute-start | bytes 417800 | tf_op jit(solution)/shard_map/ppermute | solution.py:66
  540.7 39.1 %collective-permute-start.76 = (bf16[272,256]{1,0:T(8,128)(2,1)S(1)}, bf16[272,256]{1,0:T(8,128)(2,1)S(1)}, u32[]{:S(2)}, u32[]{:S(2)}) collective-permute-start(bf16[272,256]{1,0:T(8,128)(2,1)S(1)} %add_convert_fusion.7), channel_id=1, source_target_pairs={{0,1},{1,2},{2,3},{3,0},{4,5},{5,6},{6,7},{7,4},{8,9},{9,10},{10,1... | collective-permute-start | bytes 417800 | tf_op jit(solution)/shard_map/ppermute | solution.py:66
  541.9 47.4 %collective-permute-start.77 = (bf16[272,256]{1,0:T(8,128)(2,1)S(1)}, bf16[272,256]{1,0:T(8,128)(2,1)S(1)}, u32[]{:S(2)}, u32[]{:S(2)}) collective-permute-start(bf16[272,256]{1,0:T(8,128)(2,1)S(1)} %add_convert_fusion.7), channel_id=1, source_target_pairs={{0,2},{1,3},{2,0},{3,1},{4,6},{5,7},{6,4},{7,5},{8,10},{9,11},{10,... | collective-permute-start | bytes 417800 | tf_op jit(solution)/shard_map/ppermute | solution.py:66
  548.7 42.9 %collective-permute-start.78 = (bf16[272,256]{1,0:T(8,128)(2,1)S(1)}, bf16[272,256]{1,0:T(8,128)(2,1)S(1)}, u32[]{:S(2)}, u32[]{:S(2)}) collective-permute-start(bf16[272,256]{1,0:T(8,128)(2,1)S(1)} %add_convert_fusion.7), channel_id=1, source_target_pairs={{0,3},{1,0},{2,1},{3,2},{4,7},{5,4},{6,5},{7,6},{8,11},{9,8},{10,9... | collective-permute-start | bytes 417800 | tf_op jit(solution)/shard_map/ppermute | solution.py:66
  570.6 22.7 %collective-permute-start.69 = (bf16[272,256]{1,0:T(8,128)(2,1)S(1)}, bf16[272,256]{1,0:T(8,128)(2,1)S(1)}, u32[]{:S(2)}, u32[]{:S(2)}) collective-permute-start(bf16[272,256]{1,0:T(8,128)(2,1)S(1)} %get-tuple-element.230), channel_id=1, source_target_pairs={{0,4},{4,0},{8,12},{12,8},{1,5},{5,1},{9,13},{13,9},{2,6},{6,2},{1... | collective-permute-start | bytes 417800 | tf_op jit(solution)/shard_map/ppermute | solution.py:60
  571.2 24.2 %collective-permute-start.70 = (bf16[272,256]{1,0:T(8,128)(2,1)S(1)}, bf16[272,256]{1,0:T(8,128)(2,1)S(1)}, u32[]{:S(2)}, u32[]{:S(2)}) collective-permute-start(bf16[272,256]{1,0:T(8,128)(2,1)S(1)} %get-tuple-element.230), channel_id=1, source_target_pairs={{0,8},{4,12},{8,0},{12,4},{1,9},{5,13},{9,1},{13,5},{2,10},{6,14},... | collective-permute-start | bytes 417800 | tf_op jit(solution)/shard_map/ppermute | solution.py:60
  579.8 15.6 %collective-permute-start.71 = (bf16[272,256]{1,0:T(8,128)(2,1)S(1)}, bf16[272,256]{1,0:T(8,128)(2,1)S(1)}, u32[]{:S(2)}, u32[]{:S(2)}) collective-permute-start(bf16[272,256]{1,0:T(8,128)(2,1)S(1)} %get-tuple-element.230), channel_id=1, source_target_pairs={{0,12},{4,8},{8,4},{12,0},{1,13},{5,9},{9,5},{13,1},{2,14},{6,10},... | collective-permute-start | bytes 417800 | tf_op jit(solution)/shard_map/ppermute | solution.py:60
  (136 other events, 1036.9 us)
Sparse Core Ops, SparseCore 0:
  10.2 31.1 all-gather.2
  43.5 32.3 all-gather.4
  263.6 40.3 reduce-scatter.10
  352.6 41.0 reduce-scatter.8
  395.9 71.7 reduce-scatter.6
  530.4 68.8 reduce-scatter.4

commit v2 on v1

--- a/solution.py
+++ b/solution.py
@@ -39,33 +39,55 @@
     )(*scalars, *arrays)
 
 
-def row_peer(index, step):
+def ring_dest(index, step):
+    return lax.rem(index + step, 4)
+
+
+def ring_source(index, step):
+    return lax.rem(index + 4 - step, 4)
+
+
+def peer(index, step):
     return index ^ step
-
-
-def col_dest(index, step):
-    return lax.rem(index + step, 4)
-
-
-def col_source(index, step):
-    return lax.rem(index + 4 - step, 4)
 
 
 def block(index, size):
     return pl.ds(pl.multiple_of(index * size, size), size)
 
 
-def across_rows(pieces):
-    return [pieces[0]] + [
-        lax.ppermute(pieces[step], "row", [(i, i ^ step) for i in range(4)]) for step in range(1, 4)
-    ]
-
-
-def across_cols(pieces):
+def across_heads(pieces):
     return [pieces[0]] + [
         lax.ppermute(pieces[step], "col", [(i, (i + step) % 4) for i in range(4)])
         for step in range(1, 4)
     ]
+
+
+def across_tokens(pieces):
+    return [pieces[0]] + [
+        lax.ppermute(pieces[step], "row", [(i, i ^ step) for i in range(4)]) for step in range(1, 4)
+    ]
+
+
+def transposed(array):
+    return lax.ppermute(
+        array, ("row", "col"), [(i * 4 + j, j * 4 + i) for i in range(4) for j in range(4)]
+    )
+
+
+def added(pieces):
+    total = pieces[0].astype(F32)
+    for piece in pieces[1:]:
+        total = total + piece.astype(F32)
+    return total.astype(BF)
+
+
+def parity_sum(array):
+    count = lax.axis_size("dp")
+    moved = [
+        lax.ppermute(array, "dp", [(i, (i + step) % count) for i in range(count)])
+        for step in range(2, count, 2)
+    ]
+    return added([array, *moved]) if moved else array
 
 
 def pair_swap(array):
@@ -160,18 +182,34 @@
 
 
 def place_body(place_ref, a0, a1, a2, a3, b0, b1, b2, b3, low_ref, wide_ref):
-    col = place_ref[1]
+    row = place_ref[0]
     for step, (low, wide) in enumerate(((a0, b0), (a1, b1), (a2, b2), (a3, b3))):
-        rows = block(col_source(col, step), low.shape[0])
+        rows = block(ring_source(row, step), low.shape[0])
         low_ref[rows, :] = low[...]
         wide_ref[rows, :] = wide[...].astype(F32)
 
 
-def project_in_body(place_ref, x0, x1, x2, x3, mine_ref, other_ref, side_ref, normed_ref,
-                    m0, m1, m2, m3):
+def tied(first, second):
+    both = lax.optimization_barrier((tuple(first), tuple(second)))
+    return list(both[0]), list(both[1])
+
+
+def joined_weights(place_ref, weights, mine_s, other_s):
+    if len(weights) == 2:
+        return weights
+    for step in range(4):
+        rows = block(peer(place_ref[1], step), 128)
+        mine_s[rows, :] = weights[step][...]
+        other_s[rows, :] = weights[4 + step][...]
+    return mine_s, other_s
+
+
+def project_in_body(place_ref, x0, x1, x2, x3, *refs):
+    *weights, side_ref, normed_ref, m0, m1, m2, m3, mine_s, other_s = refs
     row, col, half = place_ref[0], place_ref[1], place_ref[2]
+    mine_ref, other_ref = joined_weights(place_ref, weights, mine_s, other_s)
     for step, piece in enumerate((x0, x1, x2, x3)):
-        normed_ref[block(row_peer(row, step), 64), :] = piece[...]
+        normed_ref[block(ring_source(row, step), 64), :] = piece[...]
     mine = jnp.concatenate([normed_ref[:, block(2 * j + half, 128)] for j in range(4)], axis=1)
     other = jnp.concatenate([normed_ref[:, block(2 * j + 1 - half, 128)] for j in range(4)], axis=1)
     side = dot(normed_ref[...], side_ref[...]).astype(BF)
@@ -179,7 +217,7 @@
     steps = dot(mine, mine_ref[:, width:]) + dot(other, other_ref[:, width:])
     steps = steps.astype(BF).astype(F32).T[0:16, :].astype(BF)
     for step, out in enumerate((m0, m1, m2, m3)):
-        cols = block(col_dest(col, step), 256)
+        cols = block(peer(col, step), 256)
         value = dot(mine, mine_ref[:, cols]) + dot(other, other_ref[:, cols])
         out[0:256, 0:256] = value.astype(BF)
         out[0:256, 256:512] = side
@@ -215,7 +253,7 @@
 
 def gather_sequence(col, pieces, zx_s, bc_s, dt_s):
     for step, piece in enumerate(pieces):
-        at = col_source(col, step)
+        at = peer(col, step)
         zx_s[block(at, 256), :] = piece[0:256, 0:256]
         bc_s[block(at, 256), :] = piece[0:256, 256:512]
         dt_s[:, block(at, 256)] = piece[256:272, 0:256].astype(F32)
@@ -297,7 +335,7 @@
     y_ref[...] = y
     g_s[...] = (y * gate).astype(BF)
     for step, out in enumerate((g0, g1, g2, g3)):
-        out[...] = g_s[block(col_dest(col, step), 256), :]
+        out[...] = g_s[block(peer(col, step), 256), :]
 
 
 def mix_back_body(place_ref, params, d0, d1, d2, d3, m0, m1, m2, m3, y_ref, masks_ref, seg_ref,
@@ -307,7 +345,7 @@
     col = place_ref[1]
     gather_sequence(col, (m0, m1, m2, m3), zx_s, bc_s, dt_s)
     for step, piece in enumerate((d0, d1, d2, d3)):
-        dg_s[block(col_source(col, step), 256), :] = piece[...].astype(F32)
+        dg_s[block(peer(col, step), 256), :] = piece[...].astype(F32)
     pre, steps, rate, cum = step_rows(col, dt_s, params)
     row_s[0:8, :] = steps
     row_s[8:16, :] = cum
@@ -409,18 +447,19 @@
         dv = conv_back(values, du, side_taps_ref[:, lanes], side_ref, 0, lanes)
         out_bc[:, lanes] = dv.astype(BF)
     for step, out in enumerate((o0, o1, o2, o3)):
-        at = col_dest(col, step)
+        at = peer(col, step)
         out[0:256, 0:256] = out_zx[block(at, 256), :]
         out[0:256, 256:512] = out_bc[block(at, 256), :]
         out[256:272, 0:256] = out_dt[:, block(at, 256)]
         out[256:272, 256:512] = jnp.zeros((16, 256), BF)
 
 
-def project_out_body(place_ref, g0, g1, g2, g3, mine_ref, other_ref, full_ref, o0, o1, o2, o3,
-                     acc_s):
+def project_out_body(place_ref, g0, g1, g2, g3, *refs):
+    *weights, full_ref, o0, o1, o2, o3, acc_s, mine_s, other_s = refs
     row, col, half = place_ref[0], place_ref[1], place_ref[2]
+    mine_ref, other_ref = joined_weights(place_ref, weights, mine_s, other_s)
     for step, piece in enumerate((g0, g1, g2, g3)):
-        full_ref[:, block(col_source(col, step), 128)] = piece[...]
+        full_ref[:, block(peer(col, step), 128)] = piece[...]
     full = full_ref[...]
     width = 2 * mine_ref.shape[1]
     acc_s[:, block(half, width // 2)] = dot(full, mine_ref[...])
@@ -428,15 +467,16 @@
     wide = full.astype(F32)
     acc_s[:, width:] = split_wide(jnp.sum(wide * wide, axis=1, keepdims=True), wide.shape[0])
     for step, out in enumerate((o0, o1, o2, o3)):
-        out[...] = acc_s[block(row_peer(row, step), 64), :].astype(out.dtype)
-
-
-def out_back_body(place_ref, q0, q1, q2, q3, mine_ref, other_ref, full_ref, grad_ref, gain_ref,
-                  d0, d1, d2, d3, dg_s, fac_s):
+        out[...] = acc_s[block(ring_dest(row, step), 64), :].astype(out.dtype)
+
+
+def out_back_body(place_ref, q0, q1, q2, q3, *refs):
+    *weights, full_ref, grad_ref, gain_ref, d0, d1, d2, d3, dg_s, fac_s, mine_s, other_s = refs
     row, col, half = place_ref[0], place_ref[1], place_ref[2]
+    mine_ref, other_ref = joined_weights(place_ref, weights, mine_s, other_s)
     width = grad_ref.shape[1]
     for step, piece in enumerate((q0, q1, q2, q3)):
-        rows = block(row_peer(row, step), 64)
+        rows = block(ring_source(row, step), 64)
         grad_ref[rows, :] = piece[:, 0:width]
         fac_s[rows, :] = piece[:, width:].astype(F32)
     value = dot(grad_ref[:, block(half, width // 2)], mine_ref[...], NT)
@@ -445,24 +485,31 @@
     gain_ref[...] = (value * full).astype(BF)
     dg_s[...] = (value - full * join_wide(fac_s[...])).astype(BF)
     for step, out in enumerate((d0, d1, d2, d3)):
-        out[...] = dg_s[:, block(col_dest(col, step), 128)]
-
-
-def out_weight_body(full_ref, grad_ref, gain_ref, out_ref):
+        out[...] = dg_s[:, block(peer(col, step), 128)]
+
+
+def out_weight_body(place_ref, full_ref, grad_ref, gain_ref, keep_ref, give_ref, acc_s):
+    col, half = place_ref[1], place_ref[2]
     width = grad_ref.shape[1]
-    out_ref[:, 0:width] = dot(full_ref[...], grad_ref[...], TN).astype(BF)
+    acc_s[:, 0:width] = dot(full_ref[...], grad_ref[...], TN).astype(BF)
     ones = jnp.ones((gain_ref.shape[0], LANES), BF)
-    out_ref[:, width:] = dot(gain_ref[...], ones, TN).astype(BF)
-
-
-def in_back_body(place_ref, d0, d1, d2, d3, mine_ref, other_ref, side_ref, normed_ref,
-                 full_ref, dside_ref, gain_ref, o0, o1, o2, o3, dx_s):
+    acc_s[:, width:] = dot(gain_ref[...], ones, TN).astype(BF)
+    for step in range(4):
+        at = 2 * peer(col, step)
+        keep_ref[step * 64:step * 64 + 64, :] = acc_s[block(at + half, 64), :]
+        give_ref[step * 64:step * 64 + 64, :] = acc_s[block(at + 1 - half, 64), :]
+
+
+def in_back_body(place_ref, d0, d1, d2, d3, *refs):
+    *weights, side_ref, normed_ref, full_ref, dside_ref, gain_ref, o0, o1, o2, o3 = refs[:-3]
+    dx_s, mine_s, other_s = refs[-3:]
     row, col, half = place_ref[0], place_ref[1], place_ref[2]
+    mine_ref, other_ref = joined_weights(place_ref, weights, mine_s, other_s)
     pieces = (d0, d1, d2, d3)
     side = None
     steps = None
     for step, piece in enumerate(pieces):
-        full_ref[:, block(col_source(col, step), 256)] = piece[0:256, 0:256]
+        full_ref[:, block(peer(col, step), 256)] = piece[0:256, 0:256]
         part = piece[0:256, 256:512].astype(F32)
         more = piece[256:272, 0:256].astype(F32)
         side = part if side is None else side + part
@@ -481,30 +528,78 @@
     gains = jnp.sum(dx_s[...] * normed_ref[...].astype(F32), axis=0, keepdims=True)
     gain_ref[...] = jnp.broadcast_to(gains, gain_ref.shape)
     for step, out in enumerate((o0, o1, o2, o3)):
-        out[...] = dx_s[block(row_peer(row, step), 64), :].astype(out.dtype)
-
-
-def in_weight_body(normed_ref, full_ref, dside_ref, out_ref, side_ref):
+        out[...] = dx_s[block(ring_dest(row, step), 64), :].astype(out.dtype)
+
+
+def in_weight_body(place_ref, normed_ref, full_ref, dside_ref, gains_ref, gain_ref, taps_ref,
+                   keep_ref, give_ref, keep_side, give_side, acc_s, side_s):
+    col, half = place_ref[1], place_ref[2]
     normed = normed_ref[...]
-    out_ref[...] = dot(normed, full_ref[...], TN).astype(BF)
-    side_ref[...] = dot(normed, dside_ref[...], TN).astype(BF)
-
-
-def whole_sum(array, row):
-    total = copies_sum(array).astype(BF)
-    rows = array.shape[0] // 4
-    mine = [
-        lax.dynamic_slice_in_dim(total, (row ^ step) * rows, rows, 0) for step in range(4)
-    ]
-    got = across_rows(mine)
-    part = sum(piece.astype(F32) for piece in got).astype(BF)
-    got = across_cols([part] * 4)
-    part = sum(piece.astype(F32) for piece in got).astype(BF)
-    got = across_rows([part] * 4)
-    out = jnp.zeros(array.shape, BF)
+    width = normed.shape[1]
+    acc_s[...] = dot(normed, full_ref[...], TN).astype(BF)
+    side_s[0:width, :] = dot(normed, dside_ref[...], TN).astype(BF)
+    gains = gains_ref[0:1, :] / gain_ref[...]
+    rows = [gains[:, at * 256:at * 256 + 256] for at in range(width // 256)]
+    rows.append(taps_ref[0:5, :])
+    rows.append(jnp.zeros((123 - width // 256, 256), F32))
+    side_s[width:, :] = jnp.concatenate(rows, axis=0).astype(BF)
     for step in range(4):
-        out = lax.dynamic_update_slice_in_dim(out, got[step], (row ^ step) * rows, 0)
-    return out.astype(F32)
+        at = 2 * peer(col, step)
+        keep_ref[step * 128:step * 128 + 128, :] = acc_s[block(at + half, 128), :]
+        give_ref[step * 128:step * 128 + 128, :] = acc_s[block(at + 1 - half, 128), :]
+    size = keep_side.shape[0]
+    keep_side[...] = side_s[block(half, size), :]
+    give_side[...] = side_s[block(1 - half, size), :]
+
+
+def combine_body(count, *refs):
+    pairs_in, outs = refs[:2 * count], refs[2 * count:]
+    for step, out in enumerate(outs):
+        base = 0
+        for index in range(count):
+            keep, got = pairs_in[2 * index], pairs_in[2 * index + 1]
+            size = keep.shape[0] // 4
+            rows = slice(step * size, step * size + size)
+            total = keep[rows, :].astype(F32) + got[rows, :].astype(F32)
+            out[base:base + size, :] = total.astype(out.dtype)
+            base += size
+
+
+def combine_side_body(place_ref, keep, got, o0, o1, o2, o3, acc_s):
+    acc_s[...] = (keep[...].astype(F32) + got[...].astype(F32)).astype(BF)
+    for step, out in enumerate((o0, o1, o2, o3)):
+        out[...] = acc_s[block(peer(place_ref[1], step), out.shape[0]), :]
+
+
+def quarters_body(place_ref, a0, a1, a2, a3, out_ref):
+    for step, piece in enumerate((a0, a1, a2, a3)):
+        out_ref[block(peer(place_ref[1], step), piece.shape[0]), :] = piece[...]
+
+
+def finish_body(layers, place_ref, *refs):
+    sides, grads, gain_ref = refs[:2 * layers], refs[2 * layers:4 * layers], refs[4 * layers]
+    zx_ref, dt_ref, out_ref, gain_out, side_ref, rest_ref, side_s = refs[4 * layers + 1:]
+    half = place_ref[2]
+    for layer in range(layers):
+        mine, other = sides[2 * layer], sides[2 * layer + 1]
+        size = mine.shape[0]
+        side_s[block(half, size), :] = mine[...].astype(F32)
+        side_s[block(1 - half, size), :] = other[...].astype(F32)
+        rows = side_ref.shape[1]
+        side_ref[layer] = side_s[0:rows, :]
+        rest_ref[layer] = side_s[rows:, :]
+    width = zx_ref.shape[2]
+    for layer in range(layers):
+        at = 2 * (layers - 1 - layer)
+        group = grads[at:at + 2]
+        for part, which in zip(group, (half, 1 - half)):
+            rows = block(which, 128)
+            zx_ref[layer, rows, :] = part[0:128, 0:width].astype(F32)
+            dt_ref[layer, rows, :] = part[0:128, width:].astype(F32)
+            rows = block(which, 64)
+            gain = gain_ref[layer, rows, :]
+            out_ref[layer, rows, :] = part[128:192, 0:width].astype(F32) * gain[:, 0:1]
+            gain_out[layer, rows, :] = part[128:192, width:].astype(F32) / gain
 
 
 def shards(
@@ -531,30 +626,53 @@
     length = segments.shape[1]
     heads_here = dt_weight.shape[2]
     inner = 4 * 4 * conv_x.shape[2]
-    place = jnp.stack([row, col, half, row]).astype(jnp.int32)
-    swap = [(i * 4 + j, j * 4 + i) for i in range(4) for j in range(4)]
-
-    tokens = lax.ppermute(
-        lax.dynamic_slice_in_dim(hidden, col * 64, 64, 0), ("row", "col"), swap
+    place = jnp.stack([col, row, half, row]).astype(jnp.int32)
+
+    tokens = lax.dynamic_slice_in_dim(hidden, col * 64, 64, 0)
+    cot = lax.dynamic_slice_in_dim(cotangent, col * 64, 64, 0)
+
+    def half_in(layer):
+        mine = lax.dynamic_slice_in_dim(zx_weight[layer], half * 128, 128, 0)
+        steps = lax.dynamic_slice_in_dim(dt_weight[layer], half * 128, 128, 0)
+        return jnp.concatenate(
+            [mine, jnp.pad(steps, ((0, 0), (0, LANES - heads_here)))], axis=1
+        )
+
+    def half_out(layer):
+        mine = lax.dynamic_slice_in_dim(out_weight[layer], half * (width // 2), width // 2, 1)
+        return (gnorm_gain[layer][:, None] * mine.astype(F32)).astype(BF)
+
+    def spread(array):
+        pieces = across_tokens([transposed(array)] * 4)
+        return pieces, [pair_swap(piece) for piece in pieces]
+
+    in_mine, in_other = spread(half_in(0))
+    in_mine, (out_half,) = tied(in_mine, [half_out(0)])
+    out_mine, out_other = spread(out_half)
+    rest = []
+    for layer in range(1, layers):
+        rest += [half_in(layer), half_out(layer)]
+    sizes = [piece.shape[1] for piece in rest]
+    out_mine, (rest,) = tied(out_mine, [jnp.concatenate(rest, axis=1)])
+    rest = lax.all_gather(transposed(rest), "row", axis=0, tiled=True)
+    in_weights = [[*in_mine, *in_other]]
+    out_weights = [[*out_mine, *out_other]]
+    cuts = [sum(sizes[:at]) for at in range(len(sizes) + 1)]
+    out_scratch = [pltpu.VMEM((512, width // 2), BF)] * 2
+
+    packed = jnp.concatenate(
+        [
+            conv_x,
+            conv_x_bias[:, None],
+            jnp.pad(
+                jnp.concatenate([dt_bias, -jnp.exp(a_log), skip_d], axis=1),
+                ((0, 0), (0, LANES - 6)),
+            )[:, None],
+            jnp.zeros((layers, 2, LANES), F32),
+        ],
+        axis=1,
     )
-    cot = lax.ppermute(
-        lax.dynamic_slice_in_dim(cotangent, col * 64, 64, 0), ("row", "col"), swap
-    )
-
-    def fetch(array):
-        mine = lax.all_gather(array, "col", axis=0, tiled=True)
-        return mine, pair_swap(mine)
-
-    in_weights, out_weights = [], []
-    for layer in range(layers):
-        joined = jnp.concatenate(
-            [zx_weight[layer], jnp.pad(dt_weight[layer], ((0, 0), (0, LANES - heads_here)))], axis=1
-        )
-        in_weights.append(fetch(lax.dynamic_slice_in_dim(joined, half * 128, 128, 0)))
-        scaled = (gnorm_gain[layer][:, None] * out_weight[layer].astype(F32)).astype(BF)
-        out_weights.append(
-            fetch(lax.dynamic_slice_in_dim(scaled, half * (width // 2), width // 2, 1))
-        )
+    packed = transposed(packed)
 
     seg = segments[0].astype(F32)
     columns = [seg]
@@ -563,15 +681,13 @@
         columns.append((earlier == seg).astype(F32))
     masks = jnp.pad(jnp.stack(columns, axis=1), ((0, 0), (0, LANES - 4)))
     seg_rows = jnp.broadcast_to(seg[None], (8, length))
-    taps_x = jnp.concatenate([conv_x, conv_x_bias[:, None]], axis=1).reshape(layers, 5, 2, 64)
+    taps_x = packed[:, :5].reshape(layers, 5, 2, 64)
     taps_x = jnp.pad(taps_x.transpose(0, 2, 1, 3), ((0, 0), (0, 0), (0, 3), (64, 0)))
     taps_x = taps_x.reshape(layers, 16, LANES)
     taps_bc = jnp.pad(
         jnp.concatenate([conv_bc, conv_bc_bias[:, None]], axis=1), ((0, 0), (0, 3), (0, 0))
     )
-    params = jnp.concatenate(
-        [dt_bias, -jnp.exp(a_log), skip_d, jnp.zeros_like(skip_d)], axis=1
-    )
+    params = packed[:, 5, :8]
     gains = norm_gain[:, None]
 
     wide = width + LANES
@@ -582,13 +698,14 @@
         [], [tokens, gains[0]], name="start",
     )
     for layer in range(layers):
-        pieces = across_rows([normed] * 4)
+        pieces = across_heads([normed] * 4)
         full_normed, *sent = local_call(
             project_in_body,
             [shape((256, width), BF)] + [shape((272, 512), BF)] * 4,
-            [place], [*pieces, *in_weights[layer], bc_weight[layer]], name="project_in",
-        )
-        mixed_in = across_cols(sent)
+            [place], [*pieces, *in_weights[layer], bc_weight[layer]],
+            [pltpu.VMEM((512, wide), BF)] * 2, name="project_in",
+        )
+        mixed_in = across_tokens(sent)
         y, *sent = local_call(
             mix_body,
             [shape((length, 128), F32)] + [shape((256, 128), BF)] * 4,
@@ -609,14 +726,23 @@
             ],
             name="mix",
         )
-        gated = across_cols(sent)
+        gated = across_tokens(sent)
         full_gated, *sent = local_call(
             project_out_body,
             [shape((256, 512), BF), shape((64, wide), F32)] + [shape((64, wide), BF)] * 3,
             [place], [*gated, *out_weights[layer]],
-            [pltpu.VMEM((256, wide), F32)], name="project_out",
-        )
-        parts = across_rows(sent)
+            [pltpu.VMEM((256, wide), F32)] + out_scratch, name="project_out",
+        )
+        parts = across_heads(sent)
+        if layer == 0:
+            parts, (rest,) = tied(parts, [rest])
+            other = pair_swap(rest)
+            both = [
+                [whole[:, cuts[at]:cuts[at + 1]] for whole in (rest, other)]
+                for at in range(len(sizes))
+            ]
+            in_weights += both[0::2]
+            out_weights += both[1::2]
         entry = [resid, scale, full_normed, mixed_in, y, full_gated]
         if layer + 1 < layers:
             resid, mixed, inverse, normed, scale = local_call(
@@ -635,21 +761,46 @@
         kept.append(entry)
 
     grad = cot
-    head_out, shared_out = [None] * layers, [None] * layers
+    smalls, sides, grads = [None] * layers, [None] * layers, [None] * layers
+    arrived = [None] * layers
+
+    def side_messages(terms):
+        side = local_call(
+            combine_side_body, [shape((144, 256), BF)] * 4, [place], terms[:2],
+            [pltpu.VMEM((576, 256), BF)], name="combine_side",
+        )
+        sent = local_call(
+            lambda *refs: combine_body(2, *refs),
+            [shape((192, wide), F32)] + [shape((192, wide), BF)] * 3, [], terms[2:],
+            name="combine",
+        )
+        return [*side, *sent]
+
+    home, waiting = None, []
     for layer in reversed(range(layers)):
         resid, scale, full_normed, mixed_in, y, full_gated = kept[layer][:6]
-        pieces = across_rows([sent_grad] * 4)
+        pieces = across_heads([sent_grad] * 4)
+        if waiting:
+            pieces, waiting = tied(pieces, side_messages(waiting))
         full_grad, gain_terms, *sent = local_call(
             out_back_body,
             [shape((256, width), BF), shape((256, 512), BF)] + [shape((256, 128), BF)] * 4,
             [place], [*pieces, *out_weights[layer], full_gated],
-            [pltpu.VMEM((256, 512), BF), pltpu.VMEM((256, LANES), F32)], name="out_back",
-        )
-        dgated = across_cols(sent)
-        (out_grad,) = local_call(
-            out_weight_body, [shape((512, wide), BF)], [], [full_gated, full_grad, gain_terms],
-            name="out_weight",
-        )
+            [pltpu.VMEM((256, 512), BF), pltpu.VMEM((256, LANES), F32)] + out_scratch,
+            name="out_back",
+        )
+        dgated = across_tokens(sent)
+        keep, give = local_call(
+            out_weight_body, [shape((256, wide), BF)] * 2, [place],
+            [full_gated, full_grad, gain_terms], [pltpu.VMEM((512, wide), BF)], name="out_weight",
+        )
+        dgated, (keep_out, give_out) = tied(dgated, [keep, give])
+        if home is None:
+            dgated, (result,) = tied(dgated, [result])
+            home = across_heads([result] * 4)
+        if waiting:
+            dgated, waiting = tied(dgated, waiting)
+            waiting = [*across_tokens(waiting[:4]), *across_tokens(waiting[4:])]
         o0, o1, o2, o3, head_grads, side_grads, small_grads = local_call(
             mix_back_body,
             [shape((272, 512), BF)] * 4
@@ -681,15 +832,39 @@
             ],
             name="mix_back",
         )
-        dmixed = across_cols([o0, o1, o2, o3])
+        if waiting:
+            (o0, o1, o2, o3), waiting = tied([o0, o1, o2, o3], waiting)
+            waiting = [parity_sum(added(waiting[:4])), parity_sum(added(waiting[4:]))]
+            waiting = [*across_heads([waiting[0]] * 4), transposed(waiting[1])]
+        dmixed = across_tokens([o0, o1, o2, o3])
+        if layer == layers - 1:
+            dmixed, home = tied(dmixed, home)
         full_dzx, full_dside, gain_rows, *sent = local_call(
             in_back_body,
             [shape((256, wide), BF), shape((256, 256), BF), shape((8, width), F32),
              shape((64, width), F32)] + [shape((64, width), BF)] * 3,
             [place], [*dmixed, *in_weights[layer], bc_weight[layer], full_normed],
-            [pltpu.VMEM((256, width), F32)], name="in_back",
-        )
-        parts = across_rows(sent)
+            [pltpu.VMEM((256, width), F32)] + [pltpu.VMEM((512, wide), BF)] * 2, name="in_back",
+        )
+        parts = across_heads(sent)
+        smalls[layer] = transposed(
+            copies_sum(jnp.concatenate([head_grads, small_grads], axis=0))
+        )
+        keep, give, keep_side, give_side = local_call(
+            in_weight_body,
+            [shape((512, wide), BF)] * 2 + [shape((576, 256), BF)] * 2,
+            [place], [full_normed, full_dzx, full_dside, gain_rows, gains[layer], side_grads],
+            [pltpu.VMEM((1024, wide), BF), pltpu.VMEM((1152, 256), BF)], name="in_weight",
+        )
+        if waiting:
+            parts, waiting = tied(parts, waiting)
+            arrived[layer + 1] = waiting
+        parts, (keep, give, keep_side, give_side) = tied(
+            parts, [keep, give, keep_side, give_side]
+        )
+        waiting = [
+            keep_side, pair_swap(give_side), keep, pair_swap(give), keep_out, pair_swap(give_out)
+        ]
         if layer > 0:
             mixed, inverse = kept[layer - 1][6:]
             grad, sent_grad = local_call(
@@ -703,56 +878,45 @@
                 back_end_body, [shape((64, width), BF)],
                 [], [*parts, grad, resid, scale, gains[layer]], name="back_end",
             )
-        in_grad, side_weight = local_call(
-            in_weight_body, [shape((width, wide), BF), shape((width, 256), BF)],
-            [], [full_normed, full_dzx, full_dside], name="in_weight",
-        )
-        in_total = lax.psum_scatter(
-            copies_sum(in_grad).astype(BF), "col", scatter_dimension=0, tiled=True
-        ).astype(F32)
-        out_total = lax.psum_scatter(
-            copies_sum(out_grad).astype(BF), "col", scatter_dimension=0, tiled=True
-        ).astype(F32)
-        small = copies_sum(jnp.concatenate([head_grads, small_grads], axis=0))
-        gain_part = (gain_rows[0] / norm_gain[layer]).reshape(4, 256)
-        shared = jnp.concatenate(
-            [side_weight, jnp.pad(
-                jnp.concatenate([gain_part, side_grads[:5]], axis=0), ((0, 55), (0, 0))
-            ).astype(BF)], axis=0,
-        )
-        shared = whole_sum(shared, row)
-        taps_grad = small[:16].reshape(2, 8, LANES)[:, :5, 64:].transpose(1, 0, 2).reshape(5, 128)
-        own_gain = gnorm_gain[layer]
-        head_out[layer] = (
-            in_total[:, :width],
-            in_total[:, width:width + heads_here],
-            taps_grad[:4],
-            taps_grad[4],
-            small[16:18, 0],
-            small[16:18, 1],
-            small[16:18, 2],
-            out_total[:, width] / own_gain,
-            out_total[:, :width] * own_gain[:, None],
-        )
-        shared_out[layer] = (
-            shared[width:width + 4].reshape(width),
-            shared[:width],
-            shared[width + 4:width + 8],
-            shared[width + 8],
-        )
-
-    def home(array):
-        return across_cols([lax.ppermute(array, ("row", "col"), swap)] * 4)
+    waiting = side_messages(waiting)
+    waiting = [*across_tokens(waiting[:4]), *across_tokens(waiting[4:])]
+    waiting = [parity_sum(added(waiting[:4])), parity_sum(added(waiting[4:]))]
+    arrived[0] = [*across_heads([waiting[0]] * 4), transposed(waiting[1])]
+    for layer in reversed(range(layers)):
+        *side, part = arrived[layer]
+        (side,) = local_call(
+            quarters_body, [shape((576, 256), BF)], [place], across_tokens([added(side)] * 4),
+            name="quarters",
+        )
+        sides[layer] = (side, pair_swap(side))
+        grads[layer] = (part, pair_swap(part))
 
     result_out, grad_out = local_call(
         place_body, [shape((256, width), BF), shape((256, width), F32)],
-        [place], [*home(result), *home(final)], name="place",
+        [place], [*home, *across_heads([final] * 4)], name="place",
     )
-    heads = [jnp.stack([head_out[i][k] for i in range(layers)]) for k in range(9)]
-    shared = [jnp.stack([shared_out[i][k] for i in range(layers)]) for k in range(4)]
+    own_gain = jnp.broadcast_to(gnorm_gain[:, :, None], gnorm_gain.shape + (LANES,))
+    order = list(range(layers))
+    d_zx, d_dt, d_out, d_own, d_side, d_rest = local_call(
+        lambda *refs: finish_body(layers, *refs),
+        [
+            shape((layers, 256, width), F32), shape((layers, 256, LANES), F32),
+            shape((layers, 128, width), F32), shape((layers, 128, LANES), F32),
+            shape((layers, width, 256), F32), shape((layers, 128, 256), F32),
+        ],
+        [place],
+        [part for at in order for part in sides[at]]
+        + [part for at in reversed(order) for part in grads[at]] + [own_gain],
+        [pltpu.VMEM((1152, 256), F32)], name="finish",
+    )
+    small = jnp.stack(smalls)
+    taps = small[:, :16].reshape(layers, 2, 8, LANES)[:, :, :5, 64:].transpose(0, 2, 1, 3)
+    taps = taps.reshape(layers, 5, LANES)
     return (
-        result_out, grad_out, shared[0], heads[0], heads[1], shared[1], heads[2], heads[3],
-        shared[2], shared[3], heads[4], heads[5], heads[6], heads[7], heads[8],
+        result_out, grad_out, d_rest[:, 0:4].reshape(layers, width), d_zx,
+        d_dt[:, :, :heads_here], d_side, taps[:, :4], taps[:, 4],
+        d_rest[:, 4:8], d_rest[:, 8], small[:, 16:18, 0], small[:, 16:18, 1], small[:, 16:18, 2],
+        d_own[:, :, 0], d_out,
     )
 
 

time: 628 us -> 573 us (0.912)
  the two profiles are of different devices: /device:TPU:8 before, /device:TPU:0 now
where the time goes in v2:
time: 573 us; the launch traced here: 564 us
  waiting for transfers between devices  201 us (35%)
  starting transfers between devices  178 us (31%)
  Pallas kernels  120 us (21%)
  local copies, waits for them, and re-layouts  41.6 us (7%)
  between operations  15.6 us (3%)
  other arithmetic  8.45 us (1%)
    pallas_call x29, Pallas kernels, local_call(): pl.pallas_call(body, out_shape=tuple(outs), in_specs=[smem] * len(scalars...  120 us
    ppermute x48, starting transfers between devices, across_tokens(): lax.ppermute(pieces[step], 'row', [(i, i ^ step) for i in range(4)])  101 us
    ppermute x48, waiting for transfers between devices, across_tokens(): lax.ppermute(pieces[step], 'row', [(i, i ^ step) for i in range(4)])  98.8 us
    ppermute x36, waiting for transfers between devices, across_heads(): lax.ppermute(pieces[step], 'col', [(i, (i + step) % 4) for i in range(4)])  97.8 us
    ppermute x36, starting transfers between devices, across_heads(): lax.ppermute(pieces[step], 'col', [(i, (i + step) % 4) for i in range(4)])  65.4 us
    unnamed x248, local copies, waits for them, and re-layouts  18.9 us
  transfers between devices with their start and end apart: 114, of which 40 were waited for; matrix products, arithmetic and copies ran while one was open for 4% of the time, Pallas kernels for 13%

profile of v2, /device:TPU:0, one launch (start us, length us, event | category | flops | bytes accessed | tf_op | source)
XLA Modules:
  0.0 563.7 jit_solution(6772653829493115118)
XLA Ops:
  10.4 17.5 %collective-permute-start.7 = (bf16[128,1152]{1,0:T(8,128)(2,1)S(1)}, bf16[128,1152]{1,0:T(8,128)(2,1)S(1)}, u32[]{:S(2)}, u32[]{:S(2)}) collective-permute-start(bf16[128,1152]{1,0:T(8,128)(2,1)S(1)} %collective-permute-done.4.refs_0_), channel_id=1, source_target_pairs={{0,12},{4,8},{8,4},{12,0},{1,13},{5,9},{9,5},{13,1},{2,14},{6,10},... | collective-permute-start | bytes 884744 | tf_op jit(solution)/shard_map/ppermute | solution.py:67
  27.9 10.4 %collective-permute-start.6 = (bf16[128,1152]{1,0:T(8,128)(2,1)S(1)}, bf16[128,1152]{1,0:T(8,128)(2,1)S(1)}, u32[]{:S(2)}, u32[]{:S(2)}) collective-permute-start(bf16[128,1152]{1,0:T(8,128)(2,1)S(1)} %collective-permute-done.4.refs_0_), channel_id=1, source_target_pairs={{0,8},{4,12},{8,0},{12,4},{1,9},{5,13},{9,1},{13,5},{2,10},{6,14},... | collective-permute-start | bytes 884744 | tf_op jit(solution)/shard_map/ppermute | solution.py:67
  40.0 8.3 %collective-permute-done.6.refs_2_ = bf16[128,1152]{1,0:T(8,128)(2,1)S(1)} collective-permute-done((bf16[128,1152]{1,0:T(8,128)(2,1)S(1)}, bf16[128,1152]{1,0:T(8,128)(2,1)S(1)}, u32[]{:S(2)}, u32[]{:S(2)}) %collective-permute-start.6) | collective-permute-done | bytes 294944 | tf_op jit(solution)/shard_map/ppermute | solution.py:67
  50.8 11.8 %collective-permute-start.21 = (bf16[128,512]{1,0:T(8,128)(2,1)S(1)}, bf16[128,512]{1,0:T(8,128)(2,1)S(1)}, u32[]{:S(2)}, u32[]{:S(2)}) collective-permute-start(bf16[128,512]{1,0:T(8,128)(2,1)S(1)} %collective-permute-done.18.refs_0_), channel_id=1, source_target_pairs={{0,12},{4,8},{8,4},{12,0},{1,13},{5,9},{9,5},{13,1},{2,14},{6,10},... | collective-permute-start | bytes 393224 | tf_op jit(solution)/shard_map/ppermute | solution.py:67
  74.6 4.5 collective-permute-start.3
  86.6 22.7 %collective-permute-done.3.x3 = bf16[64,1024]{1,0:T(8,128)(2,1)S(1)} collective-permute-done((bf16[64,1024]{1,0:T(8,128)(2,1)}, bf16[64,1024]{1,0:T(8,128)(2,1)S(1)}, u32[]{:S(2)}, u32[]{:S(2)}) %collective-permute-start.3) | collective-permute-done | bytes 131104 | tf_op jit(solution)/shard_map/ppermute | solution.py:60
  112.2 4.0 project_in.2
  116.2 6.7 %collective-permute-start.12 = (bf16[272,512]{1,0:T(8,128)(2,1)}, bf16[272,512]{1,0:T(8,128)(2,1)S(1)}, u32[]{:S(2)}, u32[]{:S(2)}) collective-permute-start(bf16[272,512]{1,0:T(8,128)(2,1)} %get-tuple-element.240), channel_id=1, source_target_pairs={{0,4},{4,0},{8,12},{12,8},{1,5},{5,1},{9,13},{13,9},{2,6},{6,2},{1... | collective-permute-start | bytes 835592 | tf_op jit(solution)/shard_map/ppermute | solution.py:67
  126.6 4.0 collective-permute-done.12.m1
  130.6 11.2 %collective-permute-done.13.m2 = bf16[272,512]{1,0:T(8,128)(2,1)S(1)} collective-permute-done((bf16[272,512]{1,0:T(8,128)(2,1)}, bf16[272,512]{1,0:T(8,128)(2,1)S(1)}, u32[]{:S(2)}, u32[]{:S(2)}) %collective-permute-start.13) | collective-permute-done | bytes 278560 | tf_op jit(solution)/shard_map/ppermute | solution.py:67
  143.3 7.1 %mix.2 = (f32[1024,128]{1,0:T(8,128)}, bf16[256,128]{1,0:T(8,128)(2,1)}, bf16[256,128]{1,0:T(8,128)(2,1)}, bf16[256,128]{1,0:T(8,128)(2,1)}, bf16[256,128]{1,0:T(8,128)(2,1)}) custom-call(s32[4]{0:T(128)} %pad_add_fusion.place_ref.refs_0_, f32[8]{0:T(128)} %get-tuple-element.517.params, bf16[272,512]{1,0:T(8,128)(2,1)} %get-tuple-element.239.m0, ...), custom_call_target="tpu_custom_call" | custom-call | tf_op jit(solution)/shard_map/mix/pallas_call | solution.py:31
  168.9 5.5 collective-permute-done.27.refs_2_
  177.4 5.8 %collective-permute-start.32 = (bf16[64,1024]{1,0:T(8,128)(2,1)}, bf16[64,1024]{1,0:T(8,128)(2,1)S(1)}, u32[]{:S(2)}, u32[]{:S(2)}) collective-permute-start(bf16[64,1024]{1,0:T(8,128)(2,1)} %get-tuple-element.262.x0), channel_id=1, source_target_pairs={{0,3},{1,0},{2,1},{3,2},{4,7},{5,4},{6,5},{7,6},{8,11},{9,8},{10,9... | collective-permute-start | bytes 393224 | tf_op jit(solution)/shard_map/ppermute | solution.py:60
  187.4 7.3 %collective-permute-done.31.x2 = bf16[64,1024]{1,0:T(8,128)(2,1)S(1)} collective-permute-done((bf16[64,1024]{1,0:T(8,128)(2,1)}, bf16[64,1024]{1,0:T(8,128)(2,1)S(1)}, u32[]{:S(2)}, u32[]{:S(2)}) %collective-permute-start.31) | collective-permute-done | bytes 131104 | tf_op jit(solution)/shard_map/ppermute | solution.py:60
  195.4 3.8 project_in.3
  202.8 6.2 %collective-permute-done.34.m1 = bf16[272,512]{1,0:T(8,128)(2,1)S(1)} collective-permute-done((bf16[272,512]{1,0:T(8,128)(2,1)}, bf16[272,512]{1,0:T(8,128)(2,1)S(1)}, u32[]{:S(2)}, u32[]{:S(2)}) %collective-permute-start.34) | collective-permute-done | bytes 278560 | tf_op jit(solution)/shard_map/ppermute | solution.py:67
  209.0 5.6 collective-permute-done.35.m2
  215.4 7.1 %mix.3 = (f32[1024,128]{1,0:T(8,128)}, bf16[256,128]{1,0:T(8,128)(2,1)}, bf16[256,128]{1,0:T(8,128)(2,1)}, bf16[256,128]{1,0:T(8,128)(2,1)}, bf16[256,128]{1,0:T(8,128)(2,1)}) custom-call(s32[4]{0:T(128)} %pad_add_fusion.place_ref.refs_0_, f32[8]{0:T(128)} %get-tuple-element.518.params, bf16[272,512]{1,0:T(8,128)(2,1)} %get-tuple-element.264.m0, ...), custom_call_target="tpu_custom_call" | custom-call | tf_op jit(solution)/shard_map/mix/pallas_call | solution.py:31
  247.3 3.7 collective-permute-start.45
  252.0 3.5 collective-permute-done.45.q3
  255.5 8.5 %collective-permute-done.44.q2 = bf16[64,1152]{1,0:T(8,128)(2,1)S(1)} collective-permute-done((bf16[64,1152]{1,0:T(8,128)(2,1)}, bf16[64,1152]{1,0:T(8,128)(2,1)S(1)}, u32[]{:S(2)}, u32[]{:S(2)}) %collective-permute-start.44) | collective-permute-done | bytes 147488 | tf_op jit(solution)/shard_map/ppermute | solution.py:60
  274.5 15.9 %mix_back.2 = (bf16[272,512]{1,0:T(8,128)(2,1)}, bf16[272,512]{1,0:T(8,128)(2,1)}, bf16[272,512]{1,0:T(8,128)(2,1)}, bf16[272,512]{1,0:T(8,128)(2,1)}, f32[16,12...) custom-call(s32[4]{0:T(128)} %pad_add_fusion.place_ref.refs_0_, f32[8]{0:T(128)} %get-tuple-element.518.params, ...), custom_call_target="tpu_custom_call" | custom-call | tf_op jit(solution)/shard_map/mix_back/pallas_call | solution.py:31
  294.7 4.3 collective-permute-done.54.a3
  299.9 3.6 collective-permute-done.53.a2
  306.8 4.4 in_back.2
  315.0 4.0 in_weight.2
  324.7 4.3 collective-permute-start.60
  333.5 3.5 combine.2
  337.0 5.5 collective-permute-done.59.q2
  359.2 16.0 %collective-permute-done.67 = bf16[144,256]{1,0:T(8,128)(2,1)S(1)} collective-permute-done((bf16[144,256]{1,0:T(8,128)(2,1)S(1)}, bf16[144,256]{1,0:T(8,128)(2,1)S(1)}, u32[]{:S(2)}, u32[]{:S(2)}) %collective-permute-start.67) | collective-permute-done | bytes 73760 | tf_op jit(solution)/shard_map/ppermute | solution.py:67
  376.5 15.9 %mix_back.3 = (bf16[272,512]{1,0:T(8,128)(2,1)}, bf16[272,512]{1,0:T(8,128)(2,1)}, bf16[272,512]{1,0:T(8,128)(2,1)}, bf16[272,512]{1,0:T(8,128)(2,1)}, f32[16,12...) custom-call(s32[4]{0:T(128)} %pad_add_fusion.place_ref.refs_0_, f32[8]{0:T(128)} %get-tuple-element.517.params, ...), custom_call_target="tpu_custom_call" | custom-call | tf_op jit(solution)/shard_map/mix_back/pallas_call | solution.py:31
  403.3 8.2 %collective-permute-done.73.d1 = bf16[272,512]{1,0:T(8,128)(2,1)S(1)} collective-permute-done((bf16[272,512]{1,0:T(8,128)(2,1)S(1)}, bf16[272,512]{1,0:T(8,128)(2,1)S(1)}, u32[]{:S(2)}, u32[]{:S(2)}) %collective-permute-start.73) | collective-permute-done | bytes 278560 | tf_op jit(solution)/shard_map/ppermute | solution.py:67
  411.5 5.1 collective-permute-done.74.d2
  418.2 4.4 in_back.3
  425.9 8.0 %collective-permute-start.77 = (bf16[64,1024]{1,0:T(8,128)(2,1)}, bf16[64,1024]{1,0:T(8,128)(2,1)S(1)}, u32[]{:S(2)}, u32[]{:S(2)}) collective-permute-start(bf16[64,1024]{1,0:T(8,128)(2,1)} %get-tuple-element.394), channel_id=1, source_target_pairs={{0,2},{1,3},{2,0},{3,1},{4,6},{5,7},{6,4},{7,5},{8,10},{9,11},{10,... | collective-permute-start | bytes 393224 | tf_op jit(solution)/shard_map/ppermute | solution.py:60
  435.9 4.0 in_weight.3
  439.9 4.7 collective-permute-done.79
  450.4 3.4 combine.3
  453.9 3.4 collective-permute-start.106
  461.8 15.6 %collective-permute-done.87 = bf16[144,256]{1,0:T(8,128)(2,1)S(1)} collective-permute-done((bf16[144,256]{1,0:T(8,128)(2,1)}, bf16[144,256]{1,0:T(8,128)(2,1)S(1)}, u32[]{:S(2)}, u32[]{:S(2)}) %collective-permute-start.87) | collective-permute-done | bytes 73760 | tf_op jit(solution)/shard_map/ppermute | solution.py:67
  478.1 4.8 collective-permute-done.89
  484.4 7.3 %collective-permute-start.92 = (bf16[144,256]{1,0:T(8,128)(2,1)S(1)}, bf16[144,256]{1,0:T(8,128)(2,1)S(1)}, u32[]{:S(2)}, u32[]{:S(2)}) collective-permute-start(bf16[144,256]{1,0:T(8,128)(2,1)S(1)} %add_convert_fusion.4), channel_id=1, source_target_pairs={{0,3},{1,0},{2,1},{3,2},{4,7},{5,4},{6,5},{7,6},{8,11},{9,8},{10,9... | collective-permute-start | bytes 221192 | tf_op jit(solution)/shard_map/ppermute | solution.py:60
  495.7 6.9 %collective-permute-start.99 = (bf16[144,256]{1,0:T(8,128)(2,1)S(1)}, bf16[144,256]{1,0:T(8,128)(2,1)S(1)}, u32[]{:S(2)}, u32[]{:S(2)}) collective-permute-start(bf16[144,256]{1,0:T(8,128)(2,1)S(1)} %add_convert_fusion.2.a0), channel_id=1, source_target_pairs={{0,12},{4,8},{8,4},{12,0},{1,13},{5,9},{9,5},{13,1},{2,14},{6,10},... | collective-permute-start | bytes 221192 | tf_op jit(solution)/shard_map/ppermute | solution.py:67
  502.7 3.7 collective-permute-done.91
  508.3 3.4 collective-permute-start.95
  520.5 11.2 %collective-permute-done.85.b3 = bf16[64,1024]{1,0:T(8,128)(2,1)S(1)} collective-permute-done((bf16[64,1024]{1,0:T(8,128)(2,1)}, bf16[64,1024]{1,0:T(8,128)(2,1)S(1)}, u32[]{:S(2)}, u32[]{:S(2)}) %collective-permute-start.85) | collective-permute-done | bytes 131104 | tf_op jit(solution)/shard_map/ppermute | solution.py:60
  534.3 6.7 %collective-permute-done.83.b1 = bf16[64,1024]{1,0:T(8,128)(2,1)S(1)} collective-permute-done((bf16[64,1024]{1,0:T(8,128)(2,1)S(1)}, bf16[64,1024]{1,0:T(8,128)(2,1)S(1)}, u32[]{:S(2)}, u32[]{:S(2)}) %collective-permute-start.83) | collective-permute-done | bytes 131104 | tf_op jit(solution)/shard_map/ppermute | solution.py:60
  545.3 4.6 finish.1
  (522 shorter events, 200.1 us)
Async XLA Ops:
  7.2 167.2 %all-gather.2.cloned.1.call-start = ((), (), s32[]{:S(2)}) async-start(), calls=%async_computation | async-start | bytes 2129920 | tf_op jit(solution)/shard_map/all_gather | solution.py:657
  10.4 29.6 %collective-permute-start.7 = (bf16[128,1152]{1,0:T(8,128)(2,1)S(1)}, bf16[128,1152]{1,0:T(8,128)(2,1)S(1)}, u32[]{:S(2)}, u32[]{:S(2)}) collective-permute-start(bf16[128,1152]{1,0:T(8,128)(2,1)S(1)} %collective-permute-done.4.refs_0_), channel_id=1, source_target_pairs={{0,12},{4,8},{8,4},{12,0},{1,13},{5,9},{9,5},{13,1},{2,14},{6,10},... | collective-permute-start | bytes 884744 | tf_op jit(solution)/shard_map/ppermute | solution.py:67
  27.9 20.4 %collective-permute-start.6 = (bf16[128,1152]{1,0:T(8,128)(2,1)S(1)}, bf16[128,1152]{1,0:T(8,128)(2,1)S(1)}, u32[]{:S(2)}, u32[]{:S(2)}) collective-permute-start(bf16[128,1152]{1,0:T(8,128)(2,1)S(1)} %collective-permute-done.4.refs_0_), channel_id=1, source_target_pairs={{0,8},{4,12},{8,0},{12,4},{1,9},{5,13},{9,1},{13,5},{2,10},{6,14},... | collective-permute-start | bytes 884744 | tf_op jit(solution)/shard_map/ppermute | solution.py:67
  50.8 17.2 %collective-permute-start.21 = (bf16[128,512]{1,0:T(8,128)(2,1)S(1)}, bf16[128,512]{1,0:T(8,128)(2,1)S(1)}, u32[]{:S(2)}, u32[]{:S(2)}) collective-permute-start(bf16[128,512]{1,0:T(8,128)(2,1)S(1)} %collective-permute-done.18.refs_0_), channel_id=1, source_target_pairs={{0,12},{4,8},{8,4},{12,0},{1,13},{5,9},{9,5},{13,1},{2,14},{6,10},... | collective-permute-start | bytes 393224 | tf_op jit(solution)/shard_map/ppermute | solution.py:67
  74.6 34.6 %collective-permute-start.3 = (bf16[64,1024]{1,0:T(8,128)(2,1)}, bf16[64,1024]{1,0:T(8,128)(2,1)S(1)}, u32[]{:S(2)}, u32[]{:S(2)}) collective-permute-start(bf16[64,1024]{1,0:T(8,128)(2,1)} %get-tuple-element.234.x0), channel_id=1, source_target_pairs={{0,3},{1,0},{2,1},{3,2},{4,7},{5,4},{6,5},{7,6},{8,11},{9,8},{10,9... | collective-permute-start | bytes 393224 | tf_op jit(solution)/shard_map/ppermute | solution.py:60
  79.2 30.1 %collective-permute-start.2 = (bf16[64,1024]{1,0:T(8,128)(2,1)}, bf16[64,1024]{1,0:T(8,128)(2,1)S(1)}, u32[]{:S(2)}, u32[]{:S(2)}) collective-permute-start(bf16[64,1024]{1,0:T(8,128)(2,1)} %get-tuple-element.234.x0), channel_id=1, source_target_pairs={{0,2},{1,3},{2,0},{3,1},{4,6},{5,7},{6,4},{7,5},{8,10},{9,11},{10,... | collective-permute-start | bytes 393224 | tf_op jit(solution)/shard_map/ppermute | solution.py:60
  79.2 31.3 %collective-permute-start.1 = (bf16[64,1024]{1,0:T(8,128)(2,1)}, bf16[64,1024]{1,0:T(8,128)(2,1)}, u32[]{:S(2)}, u32[]{:S(2)}) collective-permute-start(bf16[64,1024]{1,0:T(8,128)(2,1)} %get-tuple-element.234.x0), channel_id=1, source_target_pairs={{0,1},{1,2},{2,3},{3,0},{4,5},{5,6},{6,7},{7,4},{8,9},{9,10},{10,1... | collective-permute-start | bytes 393224 | tf_op jit(solution)/shard_map/ppermute | solution.py:60
  86.0 25.1 %collective-permute-start.8 = (bf16[128,1152]{1,0:T(8,128)(2,1)S(1)}, bf16[128,1152]{1,0:T(8,128)(2,1)S(1)}, u32[]{:S(2)}, u32[]{:S(2)}) collective-permute-start(bf16[128,1152]{1,0:T(8,128)(2,1)S(1)} %collective-permute-done.4.refs_0_), channel_id=1, source_target_pairs={{0,16},{16,0},{1,17},{17,1},{2,18},{18,2},{3,19},{19,3},{4,20},{20... | collective-permute-start | bytes 884744 | tf_op jit(solution)/shard_map/ppermute | solution.py:95
  86.1 25.1 %collective-permute-start.11 = (bf16[128,1152]{1,0:T(8,128)(2,1)S(1)}, bf16[128,1152]{1,0:T(8,128)(2,1)S(1)}, u32[]{:S(2)}, u32[]{:S(2)}) collective-permute-start(bf16[128,1152]{1,0:T(8,128)(2,1)S(1)} %collective-permute-done.7.refs_3_), channel_id=1, source_target_pairs={{0,16},{16,0},{1,17},{17,1},{2,18},{18,2},{3,19},{19,3},{4,20},{20... | collective-permute-start | bytes 884744 | tf_op jit(solution)/shard_map/ppermute | solution.py:95
  110.5 14.0 %collective-permute-start = (f32[2,8,128]{2,1,0:T(8,128)S(1)}, f32[2,8,128]{2,1,0:T(8,128)S(1)}, u32[]{:S(2)}, u32[]{:S(2)}) collective-permute-start(f32[2,8,128]{2,1,0:T(8,128)S(1)} %maximum_maximum_fusion), channel_id=1, source_target_pairs={{0,0},{1,4},{2,8},{3,12},{4,1},{5,5},{6,9},{7,13},{8,2},{9,6},{10,... | collective-permute-start | bytes 24584 | tf_op jit(solution)/shard_map/ppermute | solution.py:72
  116.2 14.4 %collective-permute-start.12 = (bf16[272,512]{1,0:T(8,128)(2,1)}, bf16[272,512]{1,0:T(8,128)(2,1)S(1)}, u32[]{:S(2)}, u32[]{:S(2)}) collective-permute-start(bf16[272,512]{1,0:T(8,128)(2,1)} %get-tuple-element.240), channel_id=1, source_target_pairs={{0,4},{4,0},{8,12},{12,8},{1,5},{5,1},{9,13},{13,9},{2,6},{6,2},{1... | collective-permute-start | bytes 835592 | tf_op jit(solution)/shard_map/ppermute | solution.py:67
  122.9 19.0 %collective-permute-start.13 = (bf16[272,512]{1,0:T(8,128)(2,1)}, bf16[272,512]{1,0:T(8,128)(2,1)S(1)}, u32[]{:S(2)}, u32[]{:S(2)}) collective-permute-start(bf16[272,512]{1,0:T(8,128)(2,1)} %get-tuple-element.241), channel_id=1, source_target_pairs={{0,8},{4,12},{8,0},{12,4},{1,9},{5,13},{9,1},{13,5},{2,10},{6,14},... | collective-permute-start | bytes 835592 | tf_op jit(solution)/shard_map/ppermute | solution.py:67
  124.0 26.4 %collective-permute-start.22 = (bf16[128,512]{1,0:T(8,128)(2,1)S(1)}, bf16[128,512]{1,0:T(8,128)(2,1)S(1)}, u32[]{:S(2)}, u32[]{:S(2)}) collective-permute-start(bf16[128,512]{1,0:T(8,128)(2,1)S(1)} %collective-permute-done.18.refs_0_), channel_id=1, source_target_pairs={{0,16},{16,0},{1,17},{17,1},{2,18},{18,2},{3,19},{19,3},{4,20},{20... | collective-permute-start | bytes 393224 | tf_op jit(solution)/shard_map/ppermute | solution.py:95
  124.0 27.2 %collective-permute-start.25 = (bf16[128,512]{1,0:T(8,128)(2,1)S(1)}, bf16[128,512]{1,0:T(8,128)(2,1)S(1)}, u32[]{:S(2)}, u32[]{:S(2)}) collective-permute-start(bf16[128,512]{1,0:T(8,128)(2,1)S(1)} %collective-permute-done.21.refs_3_), channel_id=1, source_target_pairs={{0,16},{16,0},{1,17},{17,1},{2,18},{18,2},{3,19},{19,3},{4,20},{20... | collective-permute-start | bytes 393224 | tf_op jit(solution)/shard_map/ppermute | solution.py:95
  124.5 18.1 %collective-permute-start.14 = (bf16[272,512]{1,0:T(8,128)(2,1)S(1)}, bf16[272,512]{1,0:T(8,128)(2,1)S(1)}, u32[]{:S(2)}, u32[]{:S(2)}) collective-permute-start(bf16[272,512]{1,0:T(8,128)(2,1)S(1)} %copy-done.117), channel_id=1, source_target_pairs={{0,12},{4,8},{8,4},{12,0},{1,13},{5,9},{9,5},{13,1},{2,14},{6,10},... | collective-permute-start | bytes 835592 | tf_op jit(solution)/shard_map/ppermute | solution.py:67
  130.6 23.3 %collective-permute-start.24 = (bf16[128,512]{1,0:T(8,128)(2,1)S(1)}, bf16[128,512]{1,0:T(8,128)(2,1)S(1)}, u32[]{:S(2)}, u32[]{:S(2)}) collective-permute-start(bf16[128,512]{1,0:T(8,128)(2,1)S(1)} %copy-done.26), channel_id=1, source_target_pairs={{0,16},{16,0},{1,17},{17,1},{2,18},{18,2},{3,19},{19,3},{4,20},{20... | collective-permute-start | bytes 393224 | tf_op jit(solution)/shard_map/ppermute | solution.py:95
  200.7 13.9 %collective-permute-start.35 = (bf16[272,512]{1,0:T(8,128)(2,1)}, bf16[272,512]{1,0:T(8,128)(2,1)S(1)}, u32[]{:S(2)}, u32[]{:S(2)}) collective-permute-start(bf16[272,512]{1,0:T(8,128)(2,1)} %get-tuple-element.266), channel_id=1, source_target_pairs={{0,8},{4,12},{8,0},{12,4},{1,9},{5,13},{9,1},{13,5},{2,10},{6,14},... | collective-permute-start | bytes 835592 | tf_op jit(solution)/shard_map/ppermute | solution.py:67
  290.3 15.5 %collective-permute-start.49 = (bf16[272,512]{1,0:T(8,128)(2,1)}, bf16[272,512]{1,0:T(8,128)(2,1)S(1)}, u32[]{:S(2)}, u32[]{:S(2)}) collective-permute-start(bf16[272,512]{1,0:T(8,128)(2,1)} %get-tuple-element.298), channel_id=1, source_target_pairs={{0,4},{4,0},{8,12},{12,8},{1,5},{5,1},{9,13},{13,9},{2,6},{6,2},{1... | collective-permute-start | bytes 835592 | tf_op jit(solution)/shard_map/ppermute | solution.py:67
  291.5 14.4 %collective-permute-start.50 = (bf16[272,512]{1,0:T(8,128)(2,1)}, bf16[272,512]{1,0:T(8,128)(2,1)S(1)}, u32[]{:S(2)}, u32[]{:S(2)}) collective-permute-start(bf16[272,512]{1,0:T(8,128)(2,1)} %get-tuple-element.299), channel_id=1, source_target_pairs={{0,8},{4,12},{8,0},{12,4},{1,9},{5,13},{9,1},{13,5},{2,10},{6,14},... | collective-permute-start | bytes 835592 | tf_op jit(solution)/shard_map/ppermute | solution.py:67
  354.1 38.3 %collective-permute-start.70 = (bf16[192,1152]{1,0:T(8,128)(2,1)S(1)}, bf16[192,1152]{1,0:T(8,128)(2,1)S(1)}, u32[]{:S(2)}, u32[]{:S(2)}) collective-permute-start(bf16[192,1152]{1,0:T(8,128)(2,1)S(1)} %copy-done.113), channel_id=1, source_target_pairs={{0,4},{4,0},{8,12},{12,8},{1,5},{5,1},{9,13},{13,9},{2,6},{6,2},{1... | collective-permute-start | bytes 1327112 | tf_op jit(solution)/shard_map/ppermute | solution.py:67
  354.2 38.2 %collective-permute-start.71 = (bf16[192,1152]{1,0:T(8,128)(2,1)S(1)}, bf16[192,1152]{1,0:T(8,128)(2,1)S(1)}, u32[]{:S(2)}, u32[]{:S(2)}) collective-permute-start(bf16[192,1152]{1,0:T(8,128)(2,1)S(1)} %copy-done.112), channel_id=1, source_target_pairs={{0,8},{4,12},{8,0},{12,4},{1,9},{5,13},{9,1},{13,5},{2,10},{6,14},... | collective-permute-start | bytes 1327112 | tf_op jit(solution)/shard_map/ppermute | solution.py:67
  355.7 36.7 %collective-permute-start.72 = (bf16[192,1152]{1,0:T(8,128)(2,1)S(1)}, bf16[192,1152]{1,0:T(8,128)(2,1)S(1)}, u32[]{:S(2)}, u32[]{:S(2)}) collective-permute-start(bf16[192,1152]{1,0:T(8,128)(2,1)S(1)} %copy-done.111), channel_id=1, source_target_pairs={{0,12},{4,8},{8,4},{12,0},{1,13},{5,9},{9,5},{13,1},{2,14},{6,10},... | collective-permute-start | bytes 1327112 | tf_op jit(solution)/shard_map/ppermute | solution.py:67
  357.6 17.5 %collective-permute-start.67 = (bf16[144,256]{1,0:T(8,128)(2,1)S(1)}, bf16[144,256]{1,0:T(8,128)(2,1)S(1)}, u32[]{:S(2)}, u32[]{:S(2)}) collective-permute-start(bf16[144,256]{1,0:T(8,128)(2,1)S(1)} %copy-done.120), channel_id=1, source_target_pairs={{0,4},{4,0},{8,12},{12,8},{1,5},{5,1},{9,13},{13,9},{2,6},{6,2},{1... | collective-permute-start | bytes 221192 | tf_op jit(solution)/shard_map/ppermute | solution.py:67
  357.7 34.7 %collective-permute-start.68 = (bf16[144,256]{1,0:T(8,128)(2,1)S(1)}, bf16[144,256]{1,0:T(8,128)(2,1)S(1)}, u32[]{:S(2)}, u32[]{:S(2)}) collective-permute-start(bf16[144,256]{1,0:T(8,128)(2,1)S(1)} %copy-done.119), channel_id=1, source_target_pairs={{0,8},{4,12},{8,0},{12,4},{1,9},{5,13},{9,1},{13,5},{2,10},{6,14},... | collective-permute-start | bytes 221192 | tf_op jit(solution)/shard_map/ppermute | solution.py:67
  375.1 17.3 %collective-permute-start.69 = (bf16[144,256]{1,0:T(8,128)(2,1)S(1)}, bf16[144,256]{1,0:T(8,128)(2,1)S(1)}, u32[]{:S(2)}, u32[]{:S(2)}) collective-permute-start(bf16[144,256]{1,0:T(8,128)(2,1)S(1)} %copy-done.118), channel_id=1, source_target_pairs={{0,12},{4,8},{8,4},{12,0},{1,13},{5,9},{9,5},{13,1},{2,14},{6,10},... | collective-permute-start | bytes 221192 | tf_op jit(solution)/shard_map/ppermute | solution.py:67
  392.7 51.9 %collective-permute-start.82 = (bf16[192,1152]{1,0:T(8,128)(2,1)S(1)}, bf16[192,1152]{1,0:T(8,128)(2,1)S(1)}, u32[]{:S(2)}, u32[]{:S(2)}) collective-permute-start(bf16[192,1152]{1,0:T(8,128)(2,1)S(1)} %add_convert_fusion.1), channel_id=1, source_target_pairs={{0,0},{1,4},{2,8},{3,12},{4,1},{5,5},{6,9},{7,13},{8,2},{9,6},{10,... | collective-permute-start | bytes 1327112 | tf_op jit(solution)/shard_map/ppermute | solution.py:72
  393.5 18.0 %collective-permute-start.73 = (bf16[272,512]{1,0:T(8,128)(2,1)S(1)}, bf16[272,512]{1,0:T(8,128)(2,1)S(1)}, u32[]{:S(2)}, u32[]{:S(2)}) collective-permute-start(bf16[272,512]{1,0:T(8,128)(2,1)S(1)} %copy-done.116), channel_id=1, source_target_pairs={{0,4},{4,0},{8,12},{12,8},{1,5},{5,1},{9,13},{13,9},{2,6},{6,2},{1... | collective-permute-start | bytes 835592 | tf_op jit(solution)/shard_map/ppermute | solution.py:67
  396.6 19.9 %collective-permute-start.74 = (bf16[272,512]{1,0:T(8,128)(2,1)S(1)}, bf16[272,512]{1,0:T(8,128)(2,1)S(1)}, u32[]{:S(2)}, u32[]{:S(2)}) collective-permute-start(bf16[272,512]{1,0:T(8,128)(2,1)S(1)} %copy-done.115), channel_id=1, source_target_pairs={{0,8},{4,12},{8,0},{12,4},{1,9},{5,13},{9,1},{13,5},{2,10},{6,14},... | collective-permute-start | bytes 835592 | tf_op jit(solution)/shard_map/ppermute | solution.py:67
  398.5 19.0 %collective-permute-start.75 = (bf16[272,512]{1,0:T(8,128)(2,1)S(1)}, bf16[272,512]{1,0:T(8,128)(2,1)S(1)}, u32[]{:S(2)}, u32[]{:S(2)}) collective-permute-start(bf16[272,512]{1,0:T(8,128)(2,1)S(1)} %copy-done.114), channel_id=1, source_target_pairs={{0,12},{4,8},{8,4},{12,0},{1,13},{5,9},{9,5},{13,1},{2,14},{6,10},... | collective-permute-start | bytes 835592 | tf_op jit(solution)/shard_map/ppermute | solution.py:67
  400.0 33.9 %collective-permute-start.81 = (bf16[144,256]{1,0:T(8,128)(2,1)S(1)}, bf16[144,256]{1,0:T(8,128)(2,1)S(1)}, u32[]{:S(2)}, u32[]{:S(2)}) collective-permute-start(bf16[144,256]{1,0:T(8,128)(2,1)S(1)} %add_convert_fusion.5), channel_id=1, source_target_pairs={{0,3},{1,0},{2,1},{3,2},{4,7},{5,4},{6,5},{7,6},{8,11},{9,8},{10,9... | collective-permute-start | bytes 221192 | tf_op jit(solution)/shard_map/ppermute | solution.py:60
  411.5 22.4 %collective-permute-start.80 = (bf16[144,256]{1,0:T(8,128)(2,1)S(1)}, bf16[144,256]{1,0:T(8,128)(2,1)S(1)}, u32[]{:S(2)}, u32[]{:S(2)}) collective-permute-start(bf16[144,256]{1,0:T(8,128)(2,1)S(1)} %add_convert_fusion.5), channel_id=1, source_target_pairs={{0,2},{1,3},{2,0},{3,1},{4,6},{5,7},{6,4},{7,5},{8,10},{9,11},{10,... | collective-permute-start | bytes 221192 | tf_op jit(solution)/shard_map/ppermute | solution.py:60
  422.7 21.9 %collective-permute-start.76 = (bf16[64,1024]{1,0:T(8,128)(2,1)}, bf16[64,1024]{1,0:T(8,128)(2,1)S(1)}, u32[]{:S(2)}, u32[]{:S(2)}) collective-permute-start(bf16[64,1024]{1,0:T(8,128)(2,1)} %get-tuple-element.393), channel_id=1, source_target_pairs={{0,1},{1,2},{2,3},{3,0},{4,5},{5,6},{6,7},{7,4},{8,9},{9,10},{10,1... | collective-permute-start | bytes 393224 | tf_op jit(solution)/shard_map/ppermute | solution.py:60
  425.9 18.7 %collective-permute-start.77 = (bf16[64,1024]{1,0:T(8,128)(2,1)}, bf16[64,1024]{1,0:T(8,128)(2,1)S(1)}, u32[]{:S(2)}, u32[]{:S(2)}) collective-permute-start(bf16[64,1024]{1,0:T(8,128)(2,1)} %get-tuple-element.394), channel_id=1, source_target_pairs={{0,2},{1,3},{2,0},{3,1},{4,6},{5,7},{6,4},{7,5},{8,10},{9,11},{10,... | collective-permute-start | bytes 393224 | tf_op jit(solution)/shard_map/ppermute | solution.py:60
  445.3 14.7 %collective-permute-start.111 = (f32[24,128]{1,0:T(8,128)S(1)}, f32[24,128]{1,0:T(8,128)S(1)}, u32[]{:S(2)}, u32[]{:S(2)}) collective-permute-start(f32[24,128]{1,0:T(8,128)S(1)} %constant_dynamic-update-slice_fusion.2), channel_id=1, source_target_pairs={{0,16},{16,0},{1,17},{17,1},{2,18},{18,2},{3,19},{19,3},{4,20},{20... | collective-permute-start | bytes 36872 | tf_op jit(solution)/shard_map/ppermute | solution.py:95
  453.9 30.6 %collective-permute-start.104 = (bf16[192,1152]{1,0:T(8,128)(2,1)}, bf16[192,1152]{1,0:T(8,128)(2,1)S(1)}, u32[]{:S(2)}, u32[]{:S(2)}) collective-permute-start(bf16[192,1152]{1,0:T(8,128)(2,1)} %get-tuple-element.440), channel_id=1, source_target_pairs={{0,4},{4,0},{8,12},{12,8},{1,5},{5,1},{9,13},{13,9},{2,6},{6,2},{1... | collective-permute-start | bytes 1327112 | tf_op jit(solution)/shard_map/ppermute | solution.py:67
  453.9 37.9 %collective-permute-start.105 = (bf16[192,1152]{1,0:T(8,128)(2,1)}, bf16[192,1152]{1,0:T(8,128)(2,1)S(1)}, u32[]{:S(2)}, u32[]{:S(2)}) collective-permute-start(bf16[192,1152]{1,0:T(8,128)(2,1)} %get-tuple-element.441), channel_id=1, source_target_pairs={{0,8},{4,12},{8,0},{12,4},{1,9},{5,13},{9,1},{13,5},{2,10},{6,14},... | collective-permute-start | bytes 1327112 | tf_op jit(solution)/shard_map/ppermute | solution.py:67
  453.9 37.9 %collective-permute-start.106 = (bf16[192,1152]{1,0:T(8,128)(2,1)}, bf16[192,1152]{1,0:T(8,128)(2,1)S(1)}, u32[]{:S(2)}, u32[]{:S(2)}) collective-permute-start(bf16[192,1152]{1,0:T(8,128)(2,1)} %get-tuple-element.442), channel_id=1, source_target_pairs={{0,12},{4,8},{8,4},{12,0},{1,13},{5,9},{9,5},{13,1},{2,14},{6,10},... | collective-permute-start | bytes 1327112 | tf_op jit(solution)/shard_map/ppermute | solution.py:67
  460.0 17.4 %collective-permute-start.87 = (bf16[144,256]{1,0:T(8,128)(2,1)}, bf16[144,256]{1,0:T(8,128)(2,1)S(1)}, u32[]{:S(2)}, u32[]{:S(2)}) collective-permute-start(bf16[144,256]{1,0:T(8,128)(2,1)} %get-tuple-element.427), channel_id=1, source_target_pairs={{0,4},{4,0},{8,12},{12,8},{1,5},{5,1},{9,13},{13,9},{2,6},{6,2},{1... | collective-permute-start | bytes 221192 | tf_op jit(solution)/shard_map/ppermute | solution.py:67
  461.3 16.1 %collective-permute-start.88 = (bf16[144,256]{1,0:T(8,128)(2,1)}, bf16[144,256]{1,0:T(8,128)(2,1)S(1)}, u32[]{:S(2)}, u32[]{:S(2)}) collective-permute-start(bf16[144,256]{1,0:T(8,128)(2,1)} %get-tuple-element.428), channel_id=1, source_target_pairs={{0,8},{4,12},{8,0},{12,4},{1,9},{5,13},{9,1},{13,5},{2,10},{6,14},... | collective-permute-start | bytes 221192 | tf_op jit(solution)/shard_map/ppermute | solution.py:67
  477.4 15.3 %collective-permute-start.112 = (f32[24,128]{1,0:T(8,128)S(1)}, f32[24,128]{1,0:T(8,128)S(1)}, u32[]{:S(2)}, u32[]{:S(2)}) collective-permute-start(f32[24,128]{1,0:T(8,128)S(1)} %add.117), channel_id=1, source_target_pairs={{0,0},{1,4},{2,8},{3,12},{4,1},{5,5},{6,9},{7,13},{8,2},{9,6},{10,... | collective-permute-start | bytes 36872 | tf_op jit(solution)/shard_map/ppermute | solution.py:72
  484.4 18.1 %collective-permute-start.92 = (bf16[144,256]{1,0:T(8,128)(2,1)S(1)}, bf16[144,256]{1,0:T(8,128)(2,1)S(1)}, u32[]{:S(2)}, u32[]{:S(2)}) collective-permute-start(bf16[144,256]{1,0:T(8,128)(2,1)S(1)} %add_convert_fusion.4), channel_id=1, source_target_pairs={{0,3},{1,0},{2,1},{3,2},{4,7},{5,4},{6,5},{7,6},{8,11},{9,8},{10,9... | collective-permute-start | bytes 221192 | tf_op jit(solution)/shard_map/ppermute | solution.py:60
  491.8 14.6 %collective-permute-start.91 = (bf16[144,256]{1,0:T(8,128)(2,1)S(1)}, bf16[144,256]{1,0:T(8,128)(2,1)S(1)}, u32[]{:S(2)}, u32[]{:S(2)}) collective-permute-start(bf16[144,256]{1,0:T(8,128)(2,1)S(1)} %add_convert_fusion.4), channel_id=1, source_target_pairs={{0,2},{1,3},{2,0},{3,1},{4,6},{5,7},{6,4},{7,5},{8,10},{9,11},{10,... | collective-permute-start | bytes 221192 | tf_op jit(solution)/shard_map/ppermute | solution.py:60
  491.8 14.6 %collective-permute-start.90 = (bf16[144,256]{1,0:T(8,128)(2,1)S(1)}, bf16[144,256]{1,0:T(8,128)(2,1)S(1)}, u32[]{:S(2)}, u32[]{:S(2)}) collective-permute-start(bf16[144,256]{1,0:T(8,128)(2,1)S(1)} %add_convert_fusion.4), channel_id=1, source_target_pairs={{0,1},{1,2},{2,3},{3,0},{4,5},{5,6},{6,7},{7,4},{8,9},{9,10},{10,1... | collective-permute-start | bytes 221192 | tf_op jit(solution)/shard_map/ppermute | solution.py:60
  492.7 39.0 %collective-permute-start.107 = (bf16[192,1152]{1,0:T(8,128)(2,1)S(1)}, bf16[192,1152]{1,0:T(8,128)(2,1)S(1)}, u32[]{:S(2)}, u32[]{:S(2)}) collective-permute-start(bf16[192,1152]{1,0:T(8,128)(2,1)S(1)} %add_convert_fusion), channel_id=1, source_target_pairs={{0,0},{1,4},{2,8},{3,12},{4,1},{5,5},{6,9},{7,13},{8,2},{9,6},{10,... | collective-permute-start | bytes 1327112 | tf_op jit(solution)/shard_map/ppermute | solution.py:72
  506.4 25.3 %collective-permute-start.85 = (bf16[64,1024]{1,0:T(8,128)(2,1)}, bf16[64,1024]{1,0:T(8,128)(2,1)S(1)}, u32[]{:S(2)}, u32[]{:S(2)}) collective-permute-start(bf16[64,1024]{1,0:T(8,128)(2,1)} %back_end.1.b0), channel_id=1, source_target_pairs={{0,3},{1,0},{2,1},{3,2},{4,7},{5,4},{6,5},{7,6},{8,11},{9,8},{10,9... | collective-permute-start | bytes 393224 | tf_op jit(solution)/shard_map/ppermute | solution.py:60
  515.6 18.1 %collective-permute-start.84 = (bf16[64,1024]{1,0:T(8,128)(2,1)}, bf16[64,1024]{1,0:T(8,128)(2,1)S(1)}, u32[]{:S(2)}, u32[]{:S(2)}) collective-permute-start(bf16[64,1024]{1,0:T(8,128)(2,1)} %back_end.1.b0), channel_id=1, source_target_pairs={{0,2},{1,3},{2,0},{3,1},{4,6},{5,7},{6,4},{7,5},{8,10},{9,11},{10,... | collective-permute-start | bytes 393224 | tf_op jit(solution)/shard_map/ppermute | solution.py:60
  518.1 26.1 %collective-permute-start.101 = (bf16[192,1152]{1,0:T(8,128)(2,1)S(1)}, bf16[192,1152]{1,0:T(8,128)(2,1)S(1)}, u32[]{:S(2)}, u32[]{:S(2)}) collective-permute-start(bf16[192,1152]{1,0:T(8,128)(2,1)S(1)} %collective-permute-done.82.refs_5_), channel_id=1, source_target_pairs={{0,16},{16,0},{1,17},{17,1},{2,18},{18,2},{3,19},{19,3},{4,20},{20... | collective-permute-start | bytes 1327112 | tf_op jit(solution)/shard_map/ppermute | solution.py:95
  518.1 26.1 %collective-permute-start.100 = (bf16[576,256]{1,0:T(8,128)(2,1)}, bf16[576,256]{1,0:T(8,128)(2,1)S(1)}, u32[]{:S(2)}, u32[]{:S(2)}) collective-permute-start(bf16[576,256]{1,0:T(8,128)(2,1)} %quarters.3.refs_3_), channel_id=1, source_target_pairs={{0,16},{16,0},{1,17},{17,1},{2,18},{18,2},{3,19},{19,3},{4,20},{20... | collective-permute-start | bytes 884744 | tf_op jit(solution)/shard_map/ppermute | solution.py:95
  (187 other events, 2124.6 us)
Sparse Core Ops, SparseCore 0:
  81.3 65.4 all-gather.1
